TPU v7x, 512 devices: a whole 4x8x8 slice. The times are simulated.
512 devices in a mesh: row: 32 (over y, z_lo, core), col: 16 (over x, z_hi).
Axes of the slice: x: 4, y: 8, z: 8 (z_hi: 4, z_lo: 2; z = z_hi * 2 + z_lo), core: 2. Of those that a mesh axis runs over, the one named last changes fastest.
Arguments:
- queries: bfloat16 [65536, 512], P(('row', 'col')), may hold values from -6 to 6
- grad_out: bfloat16 [65536, 512], P(('row', 'col')), may hold values from -6 to 6
- attn_out: bfloat16 [65536, 512], P(('row', 'col')), may hold values from -2 to 2
- key_states: bfloat16 [65536, 128], P(('row', 'col')), may hold values from -6 to 6
- value_states: bfloat16 [65536, 128], P(('row', 'col')), may hold values from -2 to 2
- log_norm: float32 [65536, 4], P(('row', 'col')), as said below
- position: int32 [65536], replicated, may hold values from 0 to 8191, as said below
- modality: int32 [65536], replicated, may hold values from 0 to 2, as said below
- bidirectional: int32 [3, 3], replicated, may hold values from 0 to 1
Outputs:
- grad_query: bfloat16 [65536, 512], P(('row', 'col'))
- grad_key: bfloat16 [65536, 128], P(('row', 'col'))
- grad_value: bfloat16 [65536, 128], P(('row', 'col'))
Inputs may be any that keep to these rules, and one draw needn't show every extreme that they name: `position`: within each sequence a permutation of 0 to 8191, token t belonging to sequence (t // 128) % 16 // 2; the tokens of one device hold two runs of 64 consecutive positions. `modality`: the same for all tokens of one sequence within one span of 32 consecutive positions. `log_norm`: the log of the number of keys that the token may see, plus 0.25 to 0.75.
All inputs are finite; a program needn't handle non-finite values.
Results may differ from a plain program's by a relative error of at most 0.0052.
Values may be sent and summed in bfloat16 or wider, within the bound.
No kernel may reach another device: no remote copies, remote signals or barrier semaphores. Data moves between devices by JAX's collectives and lax.ppermute only.
A program may use at most 64 MiB of HBM per device.

v0:
```python
import jax
import jax.numpy as jnp
from jax import lax
from jax.sharding import PartitionSpec as P

UNIT = 64


def partner(value, axis, distance):
    mask = 2**distance
    pairs = [(source, source ^ mask) for source in range(lax.axis_size(axis))]
    return lax.ppermute(value, axis, pairs)


def shifted(block, axis, distance):
    devices = range(lax.axis_size(axis))
    route = [((i - distance) % len(devices), i) for i in devices]
    return lax.ppermute(block, axis, route)


def contract_first(left, right):
    return lax.dot_general(
        left, right, (((0,), (0,)), ((), ())), preferred_element_type=jnp.float32
    )


def contract_last(left, right):
    return lax.dot_general(
        left, right, (((1,), (1,)), ((), ())), preferred_element_type=jnp.float32
    )


def modal_hot(values):
    return (values[:, None] == jnp.arange(3, dtype=jnp.int32)[None, :]).astype(jnp.float32)


def local_tile(
    q_rows,
    d_rows,
    lse_rows,
    delta_rows,
    q_pos,
    q_mod,
    key_rows,
    value_rows,
    key_pos,
    key_mod,
    table_float,
):
    row_count = q_rows.shape[0]
    head_count = lse_rows.shape[1]
    head_width = key_rows.shape[1]
    key_count = key_rows.shape[0]
    score_scale = head_width ** (-0.5)
    flat_q = q_rows.reshape(row_count * head_count, head_width)
    flat_d = d_rows.reshape(row_count * head_count, head_width)
    scores = contract_last(flat_q, key_rows) * score_scale
    causal = key_pos[None, :] <= q_pos[:, None]
    same_unit = key_pos[None, :] // UNIT == q_pos[:, None] // UNIT
    pair_bid = contract_last(jnp.dot(modal_hot(q_mod), table_float), modal_hot(key_mod)) > 0.5
    allowed = causal | same_unit & pair_bid
    allowed = jnp.broadcast_to(allowed[:, None, :], (row_count, head_count, key_count)).reshape(
        row_count * head_count, key_count
    )
    attn_probs = jnp.where(allowed, jnp.exp(scores - lse_rows.reshape(-1, 1)), 0.0)
    probs_low = attn_probs.astype(jnp.bfloat16)
    grad_probs = contract_last(flat_d, value_rows)
    grad_scores = attn_probs * (grad_probs - delta_rows.reshape(-1, 1))
    scores_low = grad_scores.astype(jnp.bfloat16)
    grad_q = jnp.dot(scores_low, key_rows, preferred_element_type=jnp.float32) * score_scale
    grad_k = contract_first(scores_low, flat_q) * score_scale
    grad_v = contract_first(probs_low, flat_d)
    return (grad_q.reshape(row_count, head_count * head_width), grad_k, grad_v)


def shards(
    queries,
    grad_out,
    attn_out,
    key_states,
    value_states,
    log_norm,
    position,
    modality,
    bidirectional,
):
    tok_count = queries.shape[0]
    head_count = log_norm.shape[1]
    head_width = key_states.shape[1]
    row_size = lax.axis_size("row")
    col_size = lax.axis_size("col")
    row_index = lax.axis_index("row")
    col_index = lax.axis_index("col")
    parity = col_index % 2
    pair_col = col_index - parity
    row_delta = jnp.einsum(
        "thd,thd->th",
        grad_out.reshape(tok_count, head_count, head_width),
        attn_out.reshape(tok_count, head_count, head_width),
        preferred_element_type=jnp.float32,
    )
    table_float = bidirectional.astype(jnp.float32)

    def slice_meta(block_col, source, length):
        start = (source * col_size + block_col) * tok_count
        return (
            lax.dynamic_slice_in_dim(position, start, length),
            lax.dynamic_slice_in_dim(modality, start, length),
        )

    def ordered(own, other):
        first = jnp.where(parity == 0, own, other)
        second = jnp.where(parity == 0, other, own)
        return jnp.concatenate([first, second], axis=0)

    def own_half(paired):
        return lax.dynamic_slice_in_dim(paired, parity * tok_count, tok_count)

    def other_half(paired):
        return lax.dynamic_slice_in_dim(paired, (1 - parity) * tok_count, tok_count)

    other_k, other_v = partner((key_states, value_states), "col", 0)
    bundle_k = ordered(key_states, other_k)
    bundle_v = ordered(value_states, other_v)
    own_pos, own_mod = slice_meta(col_index, row_index, tok_count)
    zero_key = jnp.zeros((2 * tok_count, head_width), jnp.float32)
    zero_grad = jnp.zeros((tok_count, head_count * head_width), jnp.float32)

    def turn_keys(step, state):
        cycle_k, cycle_v, acc_k, acc_v, acc_q = state
        source = (row_index - step) % row_size
        key_pos, key_mod = slice_meta(pair_col, source, 2 * tok_count)
        grad_q, grad_k, grad_v = local_tile(
            queries,
            grad_out,
            log_norm,
            row_delta,
            own_pos,
            own_mod,
            cycle_k,
            cycle_v,
            key_pos,
            key_mod,
            table_float,
        )
        cycle_k, cycle_v = shifted((cycle_k, cycle_v), "row", 1)
        acc_k, acc_v = shifted((acc_k + grad_k, acc_v + grad_v), "row", 1)
        return (cycle_k, cycle_v, acc_k, acc_v, acc_q + grad_q)

    final = lax.fori_loop(
        0, row_size, turn_keys, (bundle_k, bundle_v, zero_key, zero_key, zero_grad)
    )
    got_k, got_v = partner((other_half(final[2]), other_half(final[3])), "col", 0)
    key_sum = own_half(final[2]) + got_k
    value_sum = own_half(final[3]) + got_v
    query_sum = final[4]
    return (
        query_sum.astype(jnp.bfloat16),
        key_sum.astype(jnp.bfloat16),
        value_sum.astype(jnp.bfloat16),
    )


def solution(mesh):
    return jax.shard_map(
        shards,
        mesh=mesh,
        in_specs=(
            P(("row", "col"), None),
            P(("row", "col"), None),
            P(("row", "col"), None),
            P(("row", "col"), None),
            P(("row", "col"), None),
            P(("row", "col"), None),
            P(),
            P(),
            P(),
        ),
        out_specs=(P(("row", "col"), None), P(("row", "col"), None), P(("row", "col"), None)),
        check_vma=False,
    )
```

profile of v0, /device:TPU:6, one launch (start us, length us, event | category | flops | bytes accessed | tf_op | source)
XLA Modules:
  0.0 590.1 jit_solution(5965559622644603437)
XLA Ops:
  0.6 6.1 %collective-permute-start.4 = (bf16[128,128]{1,0:T(8,128)(2,1)}, bf16[128,128]{1,0:T(8,128)(2,1)S(1)}, u32[]{:S(2)}, u32[]{:S(2)}) collective-permute-start(bf16[128,128]{1,0:T(8,128)(2,1)} %param.14), channel_id=1, source_target_pairs={{0,1},{1,0},{2,3},{3,2},{4,5},{5,4},{6,7},{7,6},{8,9},{9,8},{10,11... | collective-permute-start | bytes 98312 | tf_op jit(solution)/shard_map/ppermute | solution.py:12
  13.7 563.6 %while.26 = (s32[]{:T(128)}, bf16[256,128]{1,0:T(8,128)(2,1)S(1)}, bf16[256,128]{1,0:T(8,128)(2,1)S(1)}, f32[256,128]{1,0:T(8,128)S(1)}, f32[256,128]{1,0:T(8,12...) while((s32[]{:T(128)}, bf16[256,128]{1,0:T(8,128)(2,1)S(1)}, ...), condition=%wide.wide.region_1.2_spmd.clone, body=%wide.wide.region_0.1_spmd.clone.sunk | while | flops 169354000 | bytes 7618696 | solution.py:150
  15.7 4.4 collective-permute-start
  25.3 2.7 collective-permute-start.3
  28.4 3.1 collective-permute-done.2
  42.8 4.0 collective-permute-start.3
  60.2 2.7 collective-permute-start.3
  63.4 3.0 collective-permute-done.2
  77.7 3.8 collective-permute-start.3
  95.2 2.6 collective-permute-start.3
  98.2 3.1 collective-permute-done.2
  112.7 3.7 collective-permute-start.3
  130.1 4.8 collective-permute-start.3
  140.5 2.7 collective-permute-start
  148.4 5.2 collective-permute-start.3
  154.6 2.2 collective-permute-done.3
  158.7 3.1 collective-permute-start
  167.1 4.0 collective-permute-start.3
  184.6 4.0 collective-permute-start.3
  190.7 2.2 collective-permute-done.3
  202.0 4.0 collective-permute-start.3
  219.5 4.0 collective-permute-start.3
  237.0 4.0 collective-permute-start.3
  254.4 4.0 collective-permute-start.3
  271.9 4.0 collective-permute-start.3
  289.4 4.0 collective-permute-start.3
  306.9 4.0 collective-permute-start.3
  324.3 4.0 collective-permute-start.3
  341.8 4.0 collective-permute-start.3
  359.3 4.0 collective-permute-start.3
  376.7 4.0 collective-permute-start.3
  382.9 2.2 collective-permute-done.3
  394.2 4.0 collective-permute-start.3
  400.4 2.2 collective-permute-done.3
  411.7 4.0 collective-permute-start.3
  417.9 2.2 collective-permute-done.3
  429.2 4.0 collective-permute-start.3
  446.6 4.0 collective-permute-start.3
  464.1 4.0 collective-permute-start.3
  481.6 4.0 collective-permute-start.3
  499.0 4.0 collective-permute-start.3
  516.5 4.0 collective-permute-start.3
  534.0 4.0 collective-permute-start.3
  551.5 4.0 collective-permute-start.3
  568.9 4.0 collective-permute-start.3
  578.0 4.3 collective-permute-start.7
  582.4 2.4 collective-permute-start.6
  585.7 3.7 collective-permute-done.6
  (736 shorter events, 410.5 us)
Async XLA Ops:
  0.6 11.9 %collective-permute-start.4 = (bf16[128,128]{1,0:T(8,128)(2,1)}, bf16[128,128]{1,0:T(8,128)(2,1)S(1)}, u32[]{:S(2)}, u32[]{:S(2)}) collective-permute-start(bf16[128,128]{1,0:T(8,128)(2,1)} %param.14), channel_id=1, source_target_pairs={{0,1},{1,0},{2,3},{3,2},{4,5},{5,4},{6,7},{7,6},{8,9},{9,8},{10,11... | collective-permute-start | bytes 98312 | tf_op jit(solution)/shard_map/ppermute | solution.py:12
  13.8 14.6 %collective-permute-start.1 = (bf16[256,128]{1,0:T(8,128)(2,1)S(1)}, bf16[256,128]{1,0:T(8,128)(2,1)S(1)}, u32[]{:S(2)}, u32[]{:S(2)}) collective-permute-start(bf16[256,128]{1,0:T(8,128)(2,1)S(1)} %copy.26), channel_id=1, source_target_pairs={{496,0},{0,16},{16,32},{32,48},{48,64},{64,80},{80,96},{96,112},{1... | collective-permute-start | bytes 196616 | tf_op jit(solution)/shard_map/while/body/eval_jaxpr/ppermute | solution.py:18
  15.7 12.7 %collective-permute-start = (bf16[256,128]{1,0:T(8,128)(2,1)S(1)}, bf16[256,128]{1,0:T(8,128)(2,1)S(1)}, u32[]{:S(2)}, u32[]{:S(2)}) collective-permute-start(bf16[256,128]{1,0:T(8,128)(2,1)S(1)} %copy.25), channel_id=1, source_target_pairs={{496,0},{0,16},{16,32},{32,48},{48,64},{64,80},{80,96},{96,112},{1... | collective-permute-start | bytes 196616 | tf_op jit(solution)/shard_map/while/body/eval_jaxpr/ppermute | solution.py:18
  33.7 13.4 %collective-permute-start.1 = (bf16[256,128]{1,0:T(8,128)(2,1)S(1)}, bf16[256,128]{1,0:T(8,128)(2,1)S(1)}, u32[]{:S(2)}, u32[]{:S(2)}) collective-permute-start(bf16[256,128]{1,0:T(8,128)(2,1)S(1)} %copy.26), channel_id=1, source_target_pairs={{496,0},{0,16},{16,32},{32,48},{48,64},{64,80},{80,96},{96,112},{1... | collective-permute-start | bytes 196616 | tf_op jit(solution)/shard_map/while/body/eval_jaxpr/ppermute | solution.py:18
  51.2 12.2 %collective-permute-start.1 = (bf16[256,128]{1,0:T(8,128)(2,1)S(1)}, bf16[256,128]{1,0:T(8,128)(2,1)S(1)}, u32[]{:S(2)}, u32[]{:S(2)}) collective-permute-start(bf16[256,128]{1,0:T(8,128)(2,1)S(1)} %copy.26), channel_id=1, source_target_pairs={{496,0},{0,16},{16,32},{32,48},{48,64},{64,80},{80,96},{96,112},{1... | collective-permute-start | bytes 196616 | tf_op jit(solution)/shard_map/while/body/eval_jaxpr/ppermute | solution.py:18
  68.6 13.3 %collective-permute-start.1 = (bf16[256,128]{1,0:T(8,128)(2,1)S(1)}, bf16[256,128]{1,0:T(8,128)(2,1)S(1)}, u32[]{:S(2)}, u32[]{:S(2)}) collective-permute-start(bf16[256,128]{1,0:T(8,128)(2,1)S(1)} %copy.26), channel_id=1, source_target_pairs={{496,0},{0,16},{16,32},{32,48},{48,64},{64,80},{80,96},{96,112},{1... | collective-permute-start | bytes 196616 | tf_op jit(solution)/shard_map/while/body/eval_jaxpr/ppermute | solution.py:18
  86.1 12.1 %collective-permute-start.1 = (bf16[256,128]{1,0:T(8,128)(2,1)S(1)}, bf16[256,128]{1,0:T(8,128)(2,1)S(1)}, u32[]{:S(2)}, u32[]{:S(2)}) collective-permute-start(bf16[256,128]{1,0:T(8,128)(2,1)S(1)} %copy.26), channel_id=1, source_target_pairs={{496,0},{0,16},{16,32},{32,48},{48,64},{64,80},{80,96},{96,112},{1... | collective-permute-start | bytes 196616 | tf_op jit(solution)/shard_map/while/body/eval_jaxpr/ppermute | solution.py:18
  103.6 13.2 %collective-permute-start.1 = (bf16[256,128]{1,0:T(8,128)(2,1)S(1)}, bf16[256,128]{1,0:T(8,128)(2,1)S(1)}, u32[]{:S(2)}, u32[]{:S(2)}) collective-permute-start(bf16[256,128]{1,0:T(8,128)(2,1)S(1)} %copy.26), channel_id=1, source_target_pairs={{496,0},{0,16},{16,32},{32,48},{48,64},{64,80},{80,96},{96,112},{1... | collective-permute-start | bytes 196616 | tf_op jit(solution)/shard_map/while/body/eval_jaxpr/ppermute | solution.py:18
  121.1 14.3 %collective-permute-start.1 = (bf16[256,128]{1,0:T(8,128)(2,1)S(1)}, bf16[256,128]{1,0:T(8,128)(2,1)S(1)}, u32[]{:S(2)}, u32[]{:S(2)}) collective-permute-start(bf16[256,128]{1,0:T(8,128)(2,1)S(1)} %copy.26), channel_id=1, source_target_pairs={{496,0},{0,16},{16,32},{32,48},{48,64},{64,80},{80,96},{96,112},{1... | collective-permute-start | bytes 196616 | tf_op jit(solution)/shard_map/while/body/eval_jaxpr/ppermute | solution.py:18
  123.0 12.4 %collective-permute-start = (bf16[256,128]{1,0:T(8,128)(2,1)S(1)}, bf16[256,128]{1,0:T(8,128)(2,1)S(1)}, u32[]{:S(2)}, u32[]{:S(2)}) collective-permute-start(bf16[256,128]{1,0:T(8,128)(2,1)S(1)} %copy.25), channel_id=1, source_target_pairs={{496,0},{0,16},{16,32},{32,48},{48,64},{64,80},{80,96},{96,112},{1... | collective-permute-start | bytes 196616 | tf_op jit(solution)/shard_map/while/body/eval_jaxpr/ppermute | solution.py:18
  138.5 15.5 %collective-permute-start.1 = (bf16[256,128]{1,0:T(8,128)(2,1)S(1)}, bf16[256,128]{1,0:T(8,128)(2,1)S(1)}, u32[]{:S(2)}, u32[]{:S(2)}) collective-permute-start(bf16[256,128]{1,0:T(8,128)(2,1)S(1)} %copy.26), channel_id=1, source_target_pairs={{496,0},{0,16},{16,32},{32,48},{48,64},{64,80},{80,96},{96,112},{1... | collective-permute-start | bytes 196616 | tf_op jit(solution)/shard_map/while/body/eval_jaxpr/ppermute | solution.py:18
  140.5 13.6 %collective-permute-start = (bf16[256,128]{1,0:T(8,128)(2,1)S(1)}, bf16[256,128]{1,0:T(8,128)(2,1)S(1)}, u32[]{:S(2)}, u32[]{:S(2)}) collective-permute-start(bf16[256,128]{1,0:T(8,128)(2,1)S(1)} %copy.25), channel_id=1, source_target_pairs={{496,0},{0,16},{16,32},{32,48},{48,64},{64,80},{80,96},{96,112},{1... | collective-permute-start | bytes 196616 | tf_op jit(solution)/shard_map/while/body/eval_jaxpr/ppermute | solution.py:18
  156.8 14.7 %collective-permute-start.1 = (bf16[256,128]{1,0:T(8,128)(2,1)S(1)}, bf16[256,128]{1,0:T(8,128)(2,1)S(1)}, u32[]{:S(2)}, u32[]{:S(2)}) collective-permute-start(bf16[256,128]{1,0:T(8,128)(2,1)S(1)} %copy.26), channel_id=1, source_target_pairs={{496,0},{0,16},{16,32},{32,48},{48,64},{64,80},{80,96},{96,112},{1... | collective-permute-start | bytes 196616 | tf_op jit(solution)/shard_map/while/body/eval_jaxpr/ppermute | solution.py:18
  158.7 12.8 %collective-permute-start = (bf16[256,128]{1,0:T(8,128)(2,1)S(1)}, bf16[256,128]{1,0:T(8,128)(2,1)S(1)}, u32[]{:S(2)}, u32[]{:S(2)}) collective-permute-start(bf16[256,128]{1,0:T(8,128)(2,1)S(1)} %copy.25), channel_id=1, source_target_pairs={{496,0},{0,16},{16,32},{32,48},{48,64},{64,80},{80,96},{96,112},{1... | collective-permute-start | bytes 196616 | tf_op jit(solution)/shard_map/while/body/eval_jaxpr/ppermute | solution.py:18
  175.5 13.5 %collective-permute-start.1 = (bf16[256,128]{1,0:T(8,128)(2,1)S(1)}, bf16[256,128]{1,0:T(8,128)(2,1)S(1)}, u32[]{:S(2)}, u32[]{:S(2)}) collective-permute-start(bf16[256,128]{1,0:T(8,128)(2,1)S(1)} %copy.26), channel_id=1, source_target_pairs={{496,0},{0,16},{16,32},{32,48},{48,64},{64,80},{80,96},{96,112},{1... | collective-permute-start | bytes 196616 | tf_op jit(solution)/shard_map/while/body/eval_jaxpr/ppermute | solution.py:18
  177.4 11.6 %collective-permute-start = (bf16[256,128]{1,0:T(8,128)(2,1)S(1)}, bf16[256,128]{1,0:T(8,128)(2,1)S(1)}, u32[]{:S(2)}, u32[]{:S(2)}) collective-permute-start(bf16[256,128]{1,0:T(8,128)(2,1)S(1)} %copy.25), channel_id=1, source_target_pairs={{496,0},{0,16},{16,32},{32,48},{48,64},{64,80},{80,96},{96,112},{1... | collective-permute-start | bytes 196616 | tf_op jit(solution)/shard_map/while/body/eval_jaxpr/ppermute | solution.py:18
  193.0 13.5 %collective-permute-start.1 = (bf16[256,128]{1,0:T(8,128)(2,1)S(1)}, bf16[256,128]{1,0:T(8,128)(2,1)S(1)}, u32[]{:S(2)}, u32[]{:S(2)}) collective-permute-start(bf16[256,128]{1,0:T(8,128)(2,1)S(1)} %copy.26), channel_id=1, source_target_pairs={{496,0},{0,16},{16,32},{32,48},{48,64},{64,80},{80,96},{96,112},{1... | collective-permute-start | bytes 196616 | tf_op jit(solution)/shard_map/while/body/eval_jaxpr/ppermute | solution.py:18
  210.4 13.5 %collective-permute-start.1 = (bf16[256,128]{1,0:T(8,128)(2,1)S(1)}, bf16[256,128]{1,0:T(8,128)(2,1)S(1)}, u32[]{:S(2)}, u32[]{:S(2)}) collective-permute-start(bf16[256,128]{1,0:T(8,128)(2,1)S(1)} %copy.26), channel_id=1, source_target_pairs={{496,0},{0,16},{16,32},{32,48},{48,64},{64,80},{80,96},{96,112},{1... | collective-permute-start | bytes 196616 | tf_op jit(solution)/shard_map/while/body/eval_jaxpr/ppermute | solution.py:18
  227.9 13.5 %collective-permute-start.1 = (bf16[256,128]{1,0:T(8,128)(2,1)S(1)}, bf16[256,128]{1,0:T(8,128)(2,1)S(1)}, u32[]{:S(2)}, u32[]{:S(2)}) collective-permute-start(bf16[256,128]{1,0:T(8,128)(2,1)S(1)} %copy.26), channel_id=1, source_target_pairs={{496,0},{0,16},{16,32},{32,48},{48,64},{64,80},{80,96},{96,112},{1... | collective-permute-start | bytes 196616 | tf_op jit(solution)/shard_map/while/body/eval_jaxpr/ppermute | solution.py:18
  229.8 11.6 %collective-permute-start = (bf16[256,128]{1,0:T(8,128)(2,1)S(1)}, bf16[256,128]{1,0:T(8,128)(2,1)S(1)}, u32[]{:S(2)}, u32[]{:S(2)}) collective-permute-start(bf16[256,128]{1,0:T(8,128)(2,1)S(1)} %copy.25), channel_id=1, source_target_pairs={{496,0},{0,16},{16,32},{32,48},{48,64},{64,80},{80,96},{96,112},{1... | collective-permute-start | bytes 196616 | tf_op jit(solution)/shard_map/while/body/eval_jaxpr/ppermute | solution.py:18
  245.4 13.5 %collective-permute-start.1 = (bf16[256,128]{1,0:T(8,128)(2,1)S(1)}, bf16[256,128]{1,0:T(8,128)(2,1)S(1)}, u32[]{:S(2)}, u32[]{:S(2)}) collective-permute-start(bf16[256,128]{1,0:T(8,128)(2,1)S(1)} %copy.26), channel_id=1, source_target_pairs={{496,0},{0,16},{16,32},{32,48},{48,64},{64,80},{80,96},{96,112},{1... | collective-permute-start | bytes 196616 | tf_op jit(solution)/shard_map/while/body/eval_jaxpr/ppermute | solution.py:18
  262.8 13.5 %collective-permute-start.1 = (bf16[256,128]{1,0:T(8,128)(2,1)S(1)}, bf16[256,128]{1,0:T(8,128)(2,1)S(1)}, u32[]{:S(2)}, u32[]{:S(2)}) collective-permute-start(bf16[256,128]{1,0:T(8,128)(2,1)S(1)} %copy.26), channel_id=1, source_target_pairs={{496,0},{0,16},{16,32},{32,48},{48,64},{64,80},{80,96},{96,112},{1... | collective-permute-start | bytes 196616 | tf_op jit(solution)/shard_map/while/body/eval_jaxpr/ppermute | solution.py:18
  264.8 11.6 %collective-permute-start = (bf16[256,128]{1,0:T(8,128)(2,1)S(1)}, bf16[256,128]{1,0:T(8,128)(2,1)S(1)}, u32[]{:S(2)}, u32[]{:S(2)}) collective-permute-start(bf16[256,128]{1,0:T(8,128)(2,1)S(1)} %copy.25), channel_id=1, source_target_pairs={{496,0},{0,16},{16,32},{32,48},{48,64},{64,80},{80,96},{96,112},{1... | collective-permute-start | bytes 196616 | tf_op jit(solution)/shard_map/while/body/eval_jaxpr/ppermute | solution.py:18
  280.3 13.5 %collective-permute-start.1 = (bf16[256,128]{1,0:T(8,128)(2,1)S(1)}, bf16[256,128]{1,0:T(8,128)(2,1)S(1)}, u32[]{:S(2)}, u32[]{:S(2)}) collective-permute-start(bf16[256,128]{1,0:T(8,128)(2,1)S(1)} %copy.26), channel_id=1, source_target_pairs={{496,0},{0,16},{16,32},{32,48},{48,64},{64,80},{80,96},{96,112},{1... | collective-permute-start | bytes 196616 | tf_op jit(solution)/shard_map/while/body/eval_jaxpr/ppermute | solution.py:18
  297.8 13.5 %collective-permute-start.1 = (bf16[256,128]{1,0:T(8,128)(2,1)S(1)}, bf16[256,128]{1,0:T(8,128)(2,1)S(1)}, u32[]{:S(2)}, u32[]{:S(2)}) collective-permute-start(bf16[256,128]{1,0:T(8,128)(2,1)S(1)} %copy.26), channel_id=1, source_target_pairs={{496,0},{0,16},{16,32},{32,48},{48,64},{64,80},{80,96},{96,112},{1... | collective-permute-start | bytes 196616 | tf_op jit(solution)/shard_map/while/body/eval_jaxpr/ppermute | solution.py:18
  315.3 13.5 %collective-permute-start.1 = (bf16[256,128]{1,0:T(8,128)(2,1)S(1)}, bf16[256,128]{1,0:T(8,128)(2,1)S(1)}, u32[]{:S(2)}, u32[]{:S(2)}) collective-permute-start(bf16[256,128]{1,0:T(8,128)(2,1)S(1)} %copy.26), channel_id=1, source_target_pairs={{496,0},{0,16},{16,32},{32,48},{48,64},{64,80},{80,96},{96,112},{1... | collective-permute-start | bytes 196616 | tf_op jit(solution)/shard_map/while/body/eval_jaxpr/ppermute | solution.py:18
  332.7 13.5 %collective-permute-start.1 = (bf16[256,128]{1,0:T(8,128)(2,1)S(1)}, bf16[256,128]{1,0:T(8,128)(2,1)S(1)}, u32[]{:S(2)}, u32[]{:S(2)}) collective-permute-start(bf16[256,128]{1,0:T(8,128)(2,1)S(1)} %copy.26), channel_id=1, source_target_pairs={{496,0},{0,16},{16,32},{32,48},{48,64},{64,80},{80,96},{96,112},{1... | collective-permute-start | bytes 196616 | tf_op jit(solution)/shard_map/while/body/eval_jaxpr/ppermute | solution.py:18
  334.7 11.6 %collective-permute-start = (bf16[256,128]{1,0:T(8,128)(2,1)S(1)}, bf16[256,128]{1,0:T(8,128)(2,1)S(1)}, u32[]{:S(2)}, u32[]{:S(2)}) collective-permute-start(bf16[256,128]{1,0:T(8,128)(2,1)S(1)} %copy.25), channel_id=1, source_target_pairs={{496,0},{0,16},{16,32},{32,48},{48,64},{64,80},{80,96},{96,112},{1... | collective-permute-start | bytes 196616 | tf_op jit(solution)/shard_map/while/body/eval_jaxpr/ppermute | solution.py:18
  350.2 13.5 %collective-permute-start.1 = (bf16[256,128]{1,0:T(8,128)(2,1)S(1)}, bf16[256,128]{1,0:T(8,128)(2,1)S(1)}, u32[]{:S(2)}, u32[]{:S(2)}) collective-permute-start(bf16[256,128]{1,0:T(8,128)(2,1)S(1)} %copy.26), channel_id=1, source_target_pairs={{496,0},{0,16},{16,32},{32,48},{48,64},{64,80},{80,96},{96,112},{1... | collective-permute-start | bytes 196616 | tf_op jit(solution)/shard_map/while/body/eval_jaxpr/ppermute | solution.py:18
  352.1 11.6 %collective-permute-start = (bf16[256,128]{1,0:T(8,128)(2,1)S(1)}, bf16[256,128]{1,0:T(8,128)(2,1)S(1)}, u32[]{:S(2)}, u32[]{:S(2)}) collective-permute-start(bf16[256,128]{1,0:T(8,128)(2,1)S(1)} %copy.25), channel_id=1, source_target_pairs={{496,0},{0,16},{16,32},{32,48},{48,64},{64,80},{80,96},{96,112},{1... | collective-permute-start | bytes 196616 | tf_op jit(solution)/shard_map/while/body/eval_jaxpr/ppermute | solution.py:18
  367.7 13.5 %collective-permute-start.1 = (bf16[256,128]{1,0:T(8,128)(2,1)S(1)}, bf16[256,128]{1,0:T(8,128)(2,1)S(1)}, u32[]{:S(2)}, u32[]{:S(2)}) collective-permute-start(bf16[256,128]{1,0:T(8,128)(2,1)S(1)} %copy.26), channel_id=1, source_target_pairs={{496,0},{0,16},{16,32},{32,48},{48,64},{64,80},{80,96},{96,112},{1... | collective-permute-start | bytes 196616 | tf_op jit(solution)/shard_map/while/body/eval_jaxpr/ppermute | solution.py:18
  369.6 11.6 %collective-permute-start = (bf16[256,128]{1,0:T(8,128)(2,1)S(1)}, bf16[256,128]{1,0:T(8,128)(2,1)S(1)}, u32[]{:S(2)}, u32[]{:S(2)}) collective-permute-start(bf16[256,128]{1,0:T(8,128)(2,1)S(1)} %copy.25), channel_id=1, source_target_pairs={{496,0},{0,16},{16,32},{32,48},{48,64},{64,80},{80,96},{96,112},{1... | collective-permute-start | bytes 196616 | tf_op jit(solution)/shard_map/while/body/eval_jaxpr/ppermute | solution.py:18
  385.1 13.5 %collective-permute-start.1 = (bf16[256,128]{1,0:T(8,128)(2,1)S(1)}, bf16[256,128]{1,0:T(8,128)(2,1)S(1)}, u32[]{:S(2)}, u32[]{:S(2)}) collective-permute-start(bf16[256,128]{1,0:T(8,128)(2,1)S(1)} %copy.26), channel_id=1, source_target_pairs={{496,0},{0,16},{16,32},{32,48},{48,64},{64,80},{80,96},{96,112},{1... | collective-permute-start | bytes 196616 | tf_op jit(solution)/shard_map/while/body/eval_jaxpr/ppermute | solution.py:18
  387.1 11.6 %collective-permute-start = (bf16[256,128]{1,0:T(8,128)(2,1)S(1)}, bf16[256,128]{1,0:T(8,128)(2,1)S(1)}, u32[]{:S(2)}, u32[]{:S(2)}) collective-permute-start(bf16[256,128]{1,0:T(8,128)(2,1)S(1)} %copy.25), channel_id=1, source_target_pairs={{496,0},{0,16},{16,32},{32,48},{48,64},{64,80},{80,96},{96,112},{1... | collective-permute-start | bytes 196616 | tf_op jit(solution)/shard_map/while/body/eval_jaxpr/ppermute | solution.py:18
  402.6 13.5 %collective-permute-start.1 = (bf16[256,128]{1,0:T(8,128)(2,1)S(1)}, bf16[256,128]{1,0:T(8,128)(2,1)S(1)}, u32[]{:S(2)}, u32[]{:S(2)}) collective-permute-start(bf16[256,128]{1,0:T(8,128)(2,1)S(1)} %copy.26), channel_id=1, source_target_pairs={{496,0},{0,16},{16,32},{32,48},{48,64},{64,80},{80,96},{96,112},{1... | collective-permute-start | bytes 196616 | tf_op jit(solution)/shard_map/while/body/eval_jaxpr/ppermute | solution.py:18
  404.5 11.6 %collective-permute-start = (bf16[256,128]{1,0:T(8,128)(2,1)S(1)}, bf16[256,128]{1,0:T(8,128)(2,1)S(1)}, u32[]{:S(2)}, u32[]{:S(2)}) collective-permute-start(bf16[256,128]{1,0:T(8,128)(2,1)S(1)} %copy.25), channel_id=1, source_target_pairs={{496,0},{0,16},{16,32},{32,48},{48,64},{64,80},{80,96},{96,112},{1... | collective-permute-start | bytes 196616 | tf_op jit(solution)/shard_map/while/body/eval_jaxpr/ppermute | solution.py:18
  420.1 13.5 %collective-permute-start.1 = (bf16[256,128]{1,0:T(8,128)(2,1)S(1)}, bf16[256,128]{1,0:T(8,128)(2,1)S(1)}, u32[]{:S(2)}, u32[]{:S(2)}) collective-permute-start(bf16[256,128]{1,0:T(8,128)(2,1)S(1)} %copy.26), channel_id=1, source_target_pairs={{496,0},{0,16},{16,32},{32,48},{48,64},{64,80},{80,96},{96,112},{1... | collective-permute-start | bytes 196616 | tf_op jit(solution)/shard_map/while/body/eval_jaxpr/ppermute | solution.py:18
  422.0 11.6 %collective-permute-start = (bf16[256,128]{1,0:T(8,128)(2,1)S(1)}, bf16[256,128]{1,0:T(8,128)(2,1)S(1)}, u32[]{:S(2)}, u32[]{:S(2)}) collective-permute-start(bf16[256,128]{1,0:T(8,128)(2,1)S(1)} %copy.25), channel_id=1, source_target_pairs={{496,0},{0,16},{16,32},{32,48},{48,64},{64,80},{80,96},{96,112},{1... | collective-permute-start | bytes 196616 | tf_op jit(solution)/shard_map/while/body/eval_jaxpr/ppermute | solution.py:18
  437.6 13.5 %collective-permute-start.1 = (bf16[256,128]{1,0:T(8,128)(2,1)S(1)}, bf16[256,128]{1,0:T(8,128)(2,1)S(1)}, u32[]{:S(2)}, u32[]{:S(2)}) collective-permute-start(bf16[256,128]{1,0:T(8,128)(2,1)S(1)} %copy.26), channel_id=1, source_target_pairs={{496,0},{0,16},{16,32},{32,48},{48,64},{64,80},{80,96},{96,112},{1... | collective-permute-start | bytes 196616 | tf_op jit(solution)/shard_map/while/body/eval_jaxpr/ppermute | solution.py:18
  439.5 11.6 %collective-permute-start = (bf16[256,128]{1,0:T(8,128)(2,1)S(1)}, bf16[256,128]{1,0:T(8,128)(2,1)S(1)}, u32[]{:S(2)}, u32[]{:S(2)}) collective-permute-start(bf16[256,128]{1,0:T(8,128)(2,1)S(1)} %copy.25), channel_id=1, source_target_pairs={{496,0},{0,16},{16,32},{32,48},{48,64},{64,80},{80,96},{96,112},{1... | collective-permute-start | bytes 196616 | tf_op jit(solution)/shard_map/while/body/eval_jaxpr/ppermute | solution.py:18
  455.0 13.5 %collective-permute-start.1 = (bf16[256,128]{1,0:T(8,128)(2,1)S(1)}, bf16[256,128]{1,0:T(8,128)(2,1)S(1)}, u32[]{:S(2)}, u32[]{:S(2)}) collective-permute-start(bf16[256,128]{1,0:T(8,128)(2,1)S(1)} %copy.26), channel_id=1, source_target_pairs={{496,0},{0,16},{16,32},{32,48},{48,64},{64,80},{80,96},{96,112},{1... | collective-permute-start | bytes 196616 | tf_op jit(solution)/shard_map/while/body/eval_jaxpr/ppermute | solution.py:18
  472.5 13.5 %collective-permute-start.1 = (bf16[256,128]{1,0:T(8,128)(2,1)S(1)}, bf16[256,128]{1,0:T(8,128)(2,1)S(1)}, u32[]{:S(2)}, u32[]{:S(2)}) collective-permute-start(bf16[256,128]{1,0:T(8,128)(2,1)S(1)} %copy.26), channel_id=1, source_target_pairs={{496,0},{0,16},{16,32},{32,48},{48,64},{64,80},{80,96},{96,112},{1... | collective-permute-start | bytes 196616 | tf_op jit(solution)/shard_map/while/body/eval_jaxpr/ppermute | solution.py:18
  490.0 13.5 %collective-permute-start.1 = (bf16[256,128]{1,0:T(8,128)(2,1)S(1)}, bf16[256,128]{1,0:T(8,128)(2,1)S(1)}, u32[]{:S(2)}, u32[]{:S(2)}) collective-permute-start(bf16[256,128]{1,0:T(8,128)(2,1)S(1)} %copy.26), channel_id=1, source_target_pairs={{496,0},{0,16},{16,32},{32,48},{48,64},{64,80},{80,96},{96,112},{1... | collective-permute-start | bytes 196616 | tf_op jit(solution)/shard_map/while/body/eval_jaxpr/ppermute | solution.py:18
  507.4 13.5 %collective-permute-start.1 = (bf16[256,128]{1,0:T(8,128)(2,1)S(1)}, bf16[256,128]{1,0:T(8,128)(2,1)S(1)}, u32[]{:S(2)}, u32[]{:S(2)}) collective-permute-start(bf16[256,128]{1,0:T(8,128)(2,1)S(1)} %copy.26), channel_id=1, source_target_pairs={{496,0},{0,16},{16,32},{32,48},{48,64},{64,80},{80,96},{96,112},{1... | collective-permute-start | bytes 196616 | tf_op jit(solution)/shard_map/while/body/eval_jaxpr/ppermute | solution.py:18
  509.4 11.6 %collective-permute-start = (bf16[256,128]{1,0:T(8,128)(2,1)S(1)}, bf16[256,128]{1,0:T(8,128)(2,1)S(1)}, u32[]{:S(2)}, u32[]{:S(2)}) collective-permute-start(bf16[256,128]{1,0:T(8,128)(2,1)S(1)} %copy.25), channel_id=1, source_target_pairs={{496,0},{0,16},{16,32},{32,48},{48,64},{64,80},{80,96},{96,112},{1... | collective-permute-start | bytes 196616 | tf_op jit(solution)/shard_map/while/body/eval_jaxpr/ppermute | solution.py:18
  524.9 13.5 %collective-permute-start.1 = (bf16[256,128]{1,0:T(8,128)(2,1)S(1)}, bf16[256,128]{1,0:T(8,128)(2,1)S(1)}, u32[]{:S(2)}, u32[]{:S(2)}) collective-permute-start(bf16[256,128]{1,0:T(8,128)(2,1)S(1)} %copy.26), channel_id=1, source_target_pairs={{496,0},{0,16},{16,32},{32,48},{48,64},{64,80},{80,96},{96,112},{1... | collective-permute-start | bytes 196616 | tf_op jit(solution)/shard_map/while/body/eval_jaxpr/ppermute | solution.py:18
  542.4 13.5 %collective-permute-start.1 = (bf16[256,128]{1,0:T(8,128)(2,1)S(1)}, bf16[256,128]{1,0:T(8,128)(2,1)S(1)}, u32[]{:S(2)}, u32[]{:S(2)}) collective-permute-start(bf16[256,128]{1,0:T(8,128)(2,1)S(1)} %copy.26), channel_id=1, source_target_pairs={{496,0},{0,16},{16,32},{32,48},{48,64},{64,80},{80,96},{96,112},{1... | collective-permute-start | bytes 196616 | tf_op jit(solution)/shard_map/while/body/eval_jaxpr/ppermute | solution.py:18
  559.9 13.5 %collective-permute-start.1 = (bf16[256,128]{1,0:T(8,128)(2,1)S(1)}, bf16[256,128]{1,0:T(8,128)(2,1)S(1)}, u32[]{:S(2)}, u32[]{:S(2)}) collective-permute-start(bf16[256,128]{1,0:T(8,128)(2,1)S(1)} %copy.26), channel_id=1, source_target_pairs={{496,0},{0,16},{16,32},{32,48},{48,64},{64,80},{80,96},{96,112},{1... | collective-permute-start | bytes 196616 | tf_op jit(solution)/shard_map/while/body/eval_jaxpr/ppermute | solution.py:18
  (92 other events, 760.2 us)
where the time goes:
time: 597 us; the launch traced here: 590 us
  starting transfers between devices  330 us (55%)
  waiting for transfers between devices  135 us (23%)
  matrix products  51.8 us (9%)
  local copies, waits for them, and re-layouts  37 us (6%)
  other arithmetic  30.8 us (5%)
    ppermute x128, starting transfers between devices, shifted(): return lax.ppermute(block, axis, route)  315 us
    ppermute x128, waiting for transfers between devices, shifted(): return lax.ppermute(block, axis, route)  130 us
    dot_general x96, matrix products, contract_last(): lax.dot_general(left, right, (((1,), (1,)), ((), ())), preferred_element_...  27.5 us
    dynamic_slice x33, local copies, waits for them, and re-layouts, slice_meta(): lax.dynamic_slice_in_dim(modality, start, length)  25.7 us
    select_n x64, other arithmetic, local_tile(): same_unit = key_pos[None, :] // UNIT == q_pos[:, None] // UNIT  25.1 us
    dot_general x64, matrix products, contract_first(): lax.dot_general(left, right, (((0,), (0,)), ((), ())), preferred_element_...  17.4 us
    ppermute x4, starting transfers between devices, partner(): return lax.ppermute(value, axis, pairs)  14.7 us
  transfers between devices with their start and end apart: 132, of which 67 were waited for; matrix products, arithmetic and copies ran while one was open for 20% of the time, Pallas kernels for 0%

commit v1 on v0

v1 whole, which is shorter than its diff:
```python
import functools
import jax
import jax.numpy as jnp
from jax import lax
from jax.experimental import pallas as pl
from jax.experimental.pallas import tpu as pltpu
from jax.sharding import Mesh, PartitionSpec as P

UNIT = 64
TOK = 128
HEADS = 4
DIM = 128
WIDE = HEADS * DIM
MSG = 2 * WIDE + DIM
NZ = 4
NY = 8
KEYS = 2 * NY * TOK
QUNITS = 2 * NZ
KUNITS = KEYS // UNIT
GROUP = 8
ROWS = HEADS * UNIT
AXES = ("y", "zlo", "core", "x", "zhh", "zhl")
bf16 = jnp.bfloat16
f32 = jnp.float32


def pack_kernel(q_ref, d_ref, o_ref, lse_ref, msg_ref):
    msg_ref[:, :WIDE] = q_ref[...]
    msg_ref[:, WIDE : 2 * WIDE] = d_ref[...]
    lane = lax.broadcasted_iota(jnp.int32, (TOK, DIM), 1)
    extra = jnp.zeros((TOK, DIM), f32)
    for h in range(HEADS):
        cut = slice(h * DIM, (h + 1) * DIM)
        delta = jnp.sum(d_ref[:, cut].astype(f32) * o_ref[:, cut].astype(f32), axis=1, keepdims=True)
        for base, col in ((h, lse_ref[:, h : h + 1]), (3 * HEADS + h, delta)):
            rest = jnp.broadcast_to(col, (TOK, DIM))
            for part in range(3):
                low = rest.astype(bf16).astype(f32)
                extra = jnp.where(lane == base + part * HEADS, low, extra)
                rest = rest - low
    msg_ref[:, 2 * WIDE :] = extra.astype(bf16)


def nt(left, right):
    return lax.dot_general(left, right, (((1,), (1,)), ((), ())), preferred_element_type=f32)


def tn(left, right):
    return lax.dot_general(left, right, (((0,), (0,)), ((), ())), preferred_element_type=f32)


def nn(left, right):
    return lax.dot_general(left, right, (((1,), (0,)), ((), ())), preferred_element_type=f32)


def tile_kernel(
    order, need, full, m0, m1, m2, m3, kvo, kvx, kcode, qlim,
    g0, g1, g2, g3, gkvo, gkvx,
    qs, ds, lse, delta, kv, kc, gk, gv, gq,
):
    for a, m in enumerate((m0, m1, m2, m3)):
        meta = m[:, 2 * WIDE :].astype(f32).T
        for half in range(2):
            u = 2 * a + half
            rows = slice(half * UNIT, (half + 1) * UNIT)
            for h in range(HEADS):
                dst = slice(u * ROWS + h * UNIT, u * ROWS + (h + 1) * UNIT)
                qs[dst, :] = m[rows, h * DIM : (h + 1) * DIM]
                ds[dst, :] = m[rows, WIDE + h * DIM : WIDE + (h + 1) * DIM]
            for ref, base in ((lse, 0), (delta, 3 * HEADS)):
                ref[u] = jnp.concatenate(
                    [
                        meta[base + h : base + h + 1, rows]
                        + meta[base + HEADS + h : base + HEADS + h + 1, rows]
                        + meta[base + 2 * HEADS + h : base + 2 * HEADS + h + 1, rows]
                        for h in range(HEADS)
                    ],
                    axis=1,
                )
    half_keys = KEYS // 2
    kv[:half_keys, :] = kvo[...]
    kv[half_keys:, :] = kvx[...]
    for b in range(2 * NY):
        kc[b * TOK : (b + 1) * TOK, :] = jnp.broadcast_to(kcode[b : b + 1, :], (TOK, TOK)).T
    gk[...] = jnp.zeros_like(gk)
    gv[...] = jnp.zeros_like(gv)
    gq[...] = jnp.zeros_like(gq)
    score_scale = DIM ** (-0.5)

    def step(u, c, masked):
        offs = [pl.multiple_of(order[c * GROUP + i] * UNIT, UNIT) for i in range(GROUP)]
        keys = jnp.concatenate([kv[pl.ds(o, UNIT), :DIM] for o in offs], axis=0)
        vals = jnp.concatenate([kv[pl.ds(o, UNIT), DIM:] for o in offs], axis=0)
        at = pl.multiple_of(u * ROWS, ROWS)
        q = qs[pl.ds(at, ROWS), :]
        d = ds[pl.ds(at, ROWS), :]
        probs = jnp.exp(nt(keys, q) * score_scale - lse[u])
        if masked:
            code = jnp.concatenate([kc[pl.ds(o, UNIT), :] for o in offs], axis=0)
            code = jnp.concatenate([code] * (ROWS // TOK), axis=1)
            mod = code & 3
            lim = qlim[u]
            bound = jnp.where(mod == 0, lim[0:1], jnp.where(mod == 1, lim[1:2], lim[2:3]))
            probs = jnp.where((code >> 2) <= bound, probs, 0.0)
        grads = probs * (nt(vals, d) - delta[u])
        plow = probs.astype(bf16)
        glow = grads.astype(bf16)
        pv = nn(plow, d)
        pk = nn(glow, q)
        for i, o in enumerate(offs):
            gv[pl.ds(o, UNIT), :] += pv[i * UNIT : (i + 1) * UNIT]
            gk[pl.ds(o, UNIT), :] += pk[i * UNIT : (i + 1) * UNIT]
        gq[u] += tn(glow, keys)

    def unit(u, _):
        plain = full[u] // GROUP
        last = (need[u] + GROUP - 1) // GROUP

        def plain_step(c, _):
            step(u, c, False)
            return 0

        def masked_step(c, _):
            step(u, c, True)
            return 0

        lax.fori_loop(0, plain, plain_step, 0)
        lax.fori_loop(plain, last, masked_step, 0)
        return 0

    lax.fori_loop(0, QUNITS, unit, 0)
    for a, g in enumerate((g0, g1, g2, g3)):
        for half in range(2):
            rows = slice(half * UNIT, (half + 1) * UNIT)
            for h in range(HEADS):
                part = gq[2 * a + half, h * UNIT : (h + 1) * UNIT, :]
                g[rows, h * DIM : (h + 1) * DIM] = part.astype(g.dtype)
    gkvo[:, :DIM] = gk[:half_keys, :]
    gkvo[:, DIM:] = gv[:half_keys, :]
    gkvx[:, :DIM] = gk[half_keys:, :].astype(bf16)
    gkvx[:, DIM:] = gv[half_keys:, :].astype(bf16)


def plan(position, modality, table):
    code = (position * 4 + modality).reshape(8, 2, 2, 4, 2, 2, TOK)
    y, zlo, core, x, zhh, zhl = (lax.axis_index(a) for a in AXES)
    kcode = lax.dynamic_slice(code, (0, zlo, 0, x, zhh, zhl, 0), (8, 1, 2, 1, 1, 1, TOK))
    kcode = kcode.reshape(8, 2, TOK)
    kcode = jnp.where(core == 0, jnp.stack([kcode[:, 0], kcode[:, 1]]), jnp.stack([kcode[:, 1], kcode[:, 0]]))
    qcode = lax.dynamic_slice(code, (y, 0, core, x, zhh, 0, 0), (1, 2, 1, 1, 1, 2, TOK)).reshape(4, TOK)
    own = zlo * 2 + zhl
    pick = (own ^ jnp.arange(4))[:, None, None] == jnp.arange(4)[None, :, None]
    qcode = jnp.sum(jnp.where(pick, qcode[None], 0), axis=1)
    qpos, qmod = (qcode >> 2).reshape(QUNITS, UNIT), (qcode & 3).reshape(QUNITS, UNIT)
    bids = [
        jnp.where(qmod == 0, table[0, m], jnp.where(qmod == 1, table[1, m], table[2, m])) for m in range(3)
    ]
    lim = jnp.stack([jnp.where(b == 1, qpos | (UNIT - 1), qpos) for b in bids], axis=1)
    qlim = jnp.concatenate([lim] * HEADS, axis=2)
    kunit = (kcode >> 2).reshape(KUNITS, UNIT)
    low, high = jnp.min(kunit, axis=1), jnp.max(kunit, axis=1)
    index = jnp.arange(KUNITS)
    before = (low[None, :] < low[:, None]) | ((low[None, :] == low[:, None]) & (index[None, :] < index[:, None]))
    rank = jnp.sum(before.astype(jnp.int32), axis=1)
    order = jnp.sum(jnp.where(rank[None, :] == index[:, None], index[None, :], 0), axis=1)
    qlow, qhigh = jnp.min(qpos, axis=1), jnp.max(qpos, axis=1)
    need = jnp.sum((low[None, :] // UNIT <= qhigh[:, None] // UNIT).astype(jnp.int32), axis=1)
    full = jnp.min(jnp.where(high[None, :] > qlow[:, None], rank[None, :], KUNITS), axis=1)
    return order, need, full, kcode.reshape(2 * NY, TOK), qlim


def shards(queries, grad_out, attn_out, key_states, value_states, log_norm, position, modality, table):
    msg = pl.pallas_call(
        pack_kernel, out_shape=jax.ShapeDtypeStruct((TOK, MSG), bf16), name="pack"
    )(queries, grad_out, attn_out, log_norm)

    def along_z(value, mask):
        return lax.ppermute(value, ("zlo", "zhl"), [(i, i ^ mask) for i in range(NZ)])

    def other_core(value):
        return lax.ppermute(value, "core", [(0, 1), (1, 0)])

    def over_y(value):
        return lax.all_to_all(value, "y", 0, 0)

    msgs = [along_z(msg, mask) for mask in (1, 2, 3)]
    pair = jnp.concatenate([key_states, value_states], axis=1)
    kvo = over_y(jnp.broadcast_to(pair[None], (NY, TOK, 2 * DIM))).reshape(NY * TOK, 2 * DIM)
    kvx = other_core(kvo)
    order, need, full, kcode, qlim = plan(position, modality, table)
    smem = pl.BlockSpec(memory_space=pltpu.SMEM)
    vmem = pl.BlockSpec(memory_space=pltpu.VMEM)
    part = jax.ShapeDtypeStruct((TOK, WIDE), bf16)
    g0, g1, g2, g3, gkvo, gkvx = pl.pallas_call(
        tile_kernel,
        in_specs=[smem] * 3 + [vmem] * 8,
        out_specs=[vmem] * 6,
        out_shape=[
            jax.ShapeDtypeStruct((TOK, WIDE), f32),
            part,
            part,
            part,
            jax.ShapeDtypeStruct((NY * TOK, 2 * DIM), f32),
            jax.ShapeDtypeStruct((NY * TOK, 2 * DIM), bf16),
        ],
        scratch_shapes=[
            pltpu.VMEM((QUNITS * ROWS, DIM), bf16),
            pltpu.VMEM((QUNITS * ROWS, DIM), bf16),
            pltpu.VMEM((QUNITS, 1, ROWS), f32),
            pltpu.VMEM((QUNITS, 1, ROWS), f32),
            pltpu.VMEM((KEYS, 2 * DIM), bf16),
            pltpu.VMEM((KEYS, DIM), jnp.int32),
            pltpu.VMEM((KEYS, DIM), f32),
            pltpu.VMEM((KEYS, DIM), f32),
            pltpu.VMEM((QUNITS, ROWS, DIM), f32),
        ],
        name="tile",
    )(order, need, full, msg, *msgs, kvo, kvx, kcode, qlim)
    got = other_core(gkvx)
    back = [along_z(g, mask) for g, mask in ((g1, 1), (g2, 2), (g3, 3))]
    paired = (gkvo + got.astype(f32)).astype(bf16).reshape(NY, TOK, 2 * DIM)
    summed = jnp.sum(over_y(paired).astype(f32), axis=0)
    score_scale = DIM ** (-0.5)
    grad_q = (g0 + back[0].astype(f32) + back[1].astype(f32) + back[2].astype(f32)) * score_scale
    return (
        grad_q.astype(bf16),
        (summed[:, :DIM] * score_scale).astype(bf16),
        summed[:, DIM:].astype(bf16),
    )


def solution(mesh):
    fine = Mesh(mesh.devices.reshape(8, 2, 2, 4, 2, 2), AXES)
    tokens = P(AXES, None)
    return jax.shard_map(
        shards,
        mesh=fine,
        in_specs=(tokens,) * 6 + (P(), P(), P()),
        out_specs=(tokens,) * 3,
        check_vma=False,
    )
```

time: 597 us -> 92.6 us (0.16)
  starting transfers between devices: 330 us -> 37.2 us
  waiting for transfers between devices: 135 us -> 16.9 us
  matrix products: 51.8 us -> 0 us
  local copies, waits for them, and re-layouts: 37 us -> 5.45 us
  other arithmetic: 30.8 us -> 12.6 us
  Pallas kernels: 0 us -> 17.8 us
    ppermute x132 -> x8, starting transfers between devices: 330 us -> 26.3 us  [the longest x6 22.4 us: along_z(): lax.ppermute(value, ('zlo', 'zhl'), [(i, i ^ mask) for i in range(NZ)])]
    ppermute x132 -> x8, waiting for transfers between devices: 135 us -> 9.53 us  [the longest x6 6.57 us: along_z(): lax.ppermute(value, ('zlo', 'zhl'), [(i, i ^ mask) for i in range(NZ)])]
    dot_general x192 -> x0, matrix products: 51.8 us -> none  [the longest x96 27.5 us: contract_last(): lax.dot_general(left, right, (((1,), (1,)), ((), ())), preferred_element_...]
    dynamic_slice x35 -> x3, local copies, waits for them, and re-layouts: 25.7 us -> 0.04 us  [the longest x2 0.03 us: plan(): lax.dynamic_slice(code, (0, zlo, 0, x, zhh, zhl, 0), (8, 1, 2, 1, 1, 1, T...]
    select_n x65 -> x4, other arithmetic: 25.1 us -> 0.64 us  [the longest x1 0.6 us: plan(): jnp.where(core == 0, jnp.stack([kcode[:, 0], kcode[:, 1]]), jnp.stack([kc...]
    pallas_call x0 -> x2, Pallas kernels: none -> 17.8 us  [the longest x1 15.7 us: shards(): pl.pallas_call(tile_kernel, in_specs=[smem] * 3 + [vmem] * 8, out_specs=[...]
    all_to_all x0 -> x2, starting transfers between devices: none -> 10.9 us  [over_y(): return lax.all_to_all(value, 'y', 0, 0)]
    all_to_all x0 -> x2, waiting for transfers between devices: none -> 7.37 us  [over_y(): return lax.all_to_all(value, 'y', 0, 0)]
  transfers between devices with their start and end apart: 132 -> 10, of which waited for: 67 -> 7; matrix products, arithmetic and copies ran while one was open for 20% -> 13% of each run, Pallas kernels for 0% -> 0%
where the time goes in v1:
time: 92.6 us; the launch traced here: 90.9 us
  starting transfers between devices  37.2 us (40%)
  Pallas kernels  17.8 us (19%)
  waiting for transfers between devices  16.9 us (18%)
  other arithmetic  12.6 us (14%)
  local copies, waits for them, and re-layouts  5.45 us (6%)
    ppermute x6, starting transfers between devices, along_z(): lax.ppermute(value, ('zlo', 'zhl'), [(i, i ^ mask) for i in range(NZ)])  22.4 us
    pallas_call x1, Pallas kernels, shards(): pl.pallas_call(tile_kernel, in_specs=[smem] * 3 + [vmem] * 8, out_specs=[...  15.7 us
    all_to_all x2, starting transfers between devices, over_y(): return lax.all_to_all(value, 'y', 0, 0)  10.9 us
    all_to_all x2, waiting for transfers between devices, over_y(): return lax.all_to_all(value, 'y', 0, 0)  7.37 us
    ppermute x6, waiting for transfers between devices, along_z(): lax.ppermute(value, ('zlo', 'zhl'), [(i, i ^ mask) for i in range(NZ)])  6.57 us
    eq x2, other arithmetic, plan(): b == 1  5.6 us
    ppermute x2, starting transfers between devices, other_core(): return lax.ppermute(value, 'core', [(0, 1), (1, 0)])  3.94 us
    ppermute x2, waiting for transfers between devices, other_core(): return lax.ppermute(value, 'core', [(0, 1), (1, 0)])  2.96 us
  transfers between devices with their start and end apart: 10, of which 7 were waited for; matrix products, arithmetic and copies ran while one was open for 13% of the time, Pallas kernels for 0%

profile of v1, /device:TPU:6, one launch (start us, length us, event | category | flops | bytes accessed | tf_op | source)
XLA Modules:
  0.0 90.9 jit_solution(14302228368274291941)
XLA Ops:
  0.6 1.4 %copy.23.lse_ref = f32[128,4]{1,0:T(8,128)} copy(f32[128,4]{0,1:T(4,128)} %param.14) | data formatting | bytes 4096 | tf_op args[5]
  2.1 2.1 %pack.1.m0 = bf16[128,1152]{1,0:T(8,128)(2,1)} custom-call(bf16[128,512]{1,0:T(8,128)(2,1)} %q_ref.1, bf16[128,512]{1,0:T(8,128)(2,1)} %d_ref.1, bf16[128,512]{1,0:T(8,128)(2,1)} %o_ref.1, f32[128,4]{1,0:T(8,128)} %copy.23.lse_ref), custom_call_target="tpu_custom_call" | custom-call | tf_op jit(solution)/shard_map/pack/pallas_call | solution.py:173
  4.2 7.9 %collective-permute-start.2 = (bf16[128,1152]{1,0:T(8,128)(2,1)}, bf16[128,1152]{1,0:T(8,128)(2,1)S(1)}, u32[]{:S(2)}, u32[]{:S(2)}) collective-permute-start(bf16[128,1152]{1,0:T(8,128)(2,1)} %pack.1.m0), channel_id=1, source_target_pairs={{0,33},{1,32},{32,1},{33,0},{2,35},{3,34},{34,3},{35,2},{4,37},{5,... | collective-permute-start | bytes 884744 | tf_op jit(solution)/shard_map/ppermute | solution.py:178
  12.1 1.9 %collective-permute-start.1 = (bf16[128,1152]{1,0:T(8,128)(2,1)}, bf16[128,1152]{1,0:T(8,128)(2,1)S(1)}, u32[]{:S(2)}, u32[]{:S(2)}) collective-permute-start(bf16[128,1152]{1,0:T(8,128)(2,1)} %pack.1.m0), channel_id=1, source_target_pairs={{0,32},{1,33},{32,0},{33,1},{2,34},{3,35},{34,2},{35,3},{4,36},{5,... | collective-permute-start | bytes 884744 | tf_op jit(solution)/shard_map/ppermute | solution.py:178
  14.0 2.5 %collective-permute-start = (bf16[128,1152]{1,0:T(8,128)(2,1)}, bf16[128,1152]{1,0:T(8,128)(2,1)S(1)}, u32[]{:S(2)}, u32[]{:S(2)}) collective-permute-start(bf16[128,1152]{1,0:T(8,128)(2,1)} %pack.1.m0), channel_id=1, source_target_pairs={{0,1},{1,0},{32,33},{33,32},{2,3},{3,2},{34,35},{35,34},{4,5},{5,4... | collective-permute-start | bytes 884744 | tf_op jit(solution)/shard_map/ppermute | solution.py:178
  16.5 0.8 broadcast_in_dim.103
  17.4 7.2 %all-to-all-start = ((bf16[8,128,256]{2,1,0:T(8,128)(2,1)}), bf16[8,128,256]{2,1,0:T(8,128)(2,1)S(1)}, u32[]{:S(2)}, u32[]{:S(2)}) async-start(bf16[8,128,256]{2,1,0:T(8,128)(2,1)} %broadcast_in_dim.103), calls=%async_computation | async-start | bytes 1048576 | tf_op jit(solution)/shard_map/all_to_all | solution.py:184
  24.6 0.1 iota_compare_fusion.2
  24.7 0.6 copy-done.10
  25.3 0.6 fusion.7
  26.0 0.1 select_reduce_fusion.1
  26.1 1.9 %select_compare_fusion.2 = (pred[4,128]{1,0:T(4,128)(4,1)S(1)}, pred[4,128]{1,0:T(4,128)(4,1)S(1)}, pred[4,128]{1,0:T(4,128)(4,1)S(1)}) fusion(s32[]{:T(128)} %bitcast.9, s32[]{:T(128)} %bitcast.8, s32[]{:T(128)} %bitcast.7, s32[4,128]{1,0:T(4,128)S(1)} %select_reduce_fusion.1), kind=kLoop, calls=%fused_computation.29 | loop fusion | flops 3072 | bytes 3596 | tf_op jit(solution)/shard_map/eq | solution.py:158
  28.0 3.7 %select_compare_fusion.1 = (pred[4,128]{1,0:T(4,128)(4,1)S(1)}, pred[4,128]{1,0:T(4,128)(4,1)S(1)}) fusion(pred[4,128]{1,0:T(4,128)(4,1)S(1)} %get-tuple-element.21, pred[4,128]{1,0:T(4,128)(4,1)S(1)} %get-tuple-element.20, s32[]{:T(128)} %bitcast.12, s32[]{:T(128)} %bitcast.11, s32[]{:T(128)} %bitcast.10, s32[]{:T(128)} %bitcast.15, s32[]{:T(128)} %bitcast.14, ...), kind=kLoop, calls=%fused_computation.28 | loop fusion | flops 3072 | bytes 2072 | tf_op jit(solution)/shard_map/eq | solution.py:158
  31.7 0.1 shift_right_arithmetic.44
  31.8 0.1 shift_right_arithmetic.43
  31.9 0.1 reshape.256
  32.0 0.1 reshape.255
  32.1 0.1 reshape.257
  32.2 0.6 fusion.3
  32.8 0.1 shift_right_arithmetic.40
  32.8 0.1 fusion.6
  33.0 0.1 fusion.5
  33.1 0.2 convert_reduce_fusion.1
  33.3 0.6 select_reduce_fusion.order
  33.9 0.8 add_add_fusion.qlim
  34.7 6.9 %all-to-all-done = bf16[8,128,256]{2,1,0:T(8,128)(2,1)S(1)} async-done(((bf16[8,128,256]{2,1,0:T(8,128)(2,1)}), bf16[8,128,256]{2,1,0:T(8,128)(2,1)S(1)}, u32[]{:S(2)}, u32[]{:S(2)}) %all-to-all-start) | async-done | bytes 524320 | tf_op jit(solution)/shard_map/all_to_all | solution.py:184
  41.5 1.9 %collective-permute-start.3 = (bf16[1024,256]{1,0:T(8,128)(2,1)S(1)}, bf16[1024,256]{1,0:T(8,128)(2,1)S(1)}, u32[]{:S(2)}, u32[]{:S(2)}) collective-permute-start(bf16[1024,256]{1,0:T(8,128)(2,1)S(1)} %bitcast.22), channel_id=1, source_target_pairs={{0,16},{16,0},{1,17},{17,1},{2,18},{18,2},{3,19},{19,3},{4,20},{20... | collective-permute-start | bytes 1572872 | tf_op jit(solution)/shard_map/ppermute | solution.py:181
  43.5 0.8 select_reduce_fusion.2
  44.3 0.0 collective-permute-done.2.m3
  44.3 0.0 collective-permute-done.1.m2
  44.3 1.0 %collective-permute-done.3.kvx = bf16[1024,256]{1,0:T(8,128)(2,1)S(1)} collective-permute-done((bf16[1024,256]{1,0:T(8,128)(2,1)S(1)}, bf16[1024,256]{1,0:T(8,128)(2,1)S(1)}, u32[]{:S(2)}, u32[]{:S(2)}) %collective-permute-start.3) | collective-permute-done | bytes 524320 | tf_op jit(solution)/shard_map/ppermute | solution.py:181
  45.4 0.8 copy-done.1
  46.1 15.7 %tile.1 = (f32[128,512]{1,0:T(8,128)}, bf16[128,512]{1,0:T(8,128)(2,1)}, bf16[128,512]{1,0:T(8,128)(2,1)}, bf16[128,512]{1,0:T(8,128)(2,1)}, f32[1024,256]{1,0:T(8,128)}, /*index=5*/bf16[1024,256]{1,0:T(8,128)(2,1)}) custom-call(s32[32]{0:T(128)} %select_reduce_fusion.order, s32[8]{0:T(128)} %get-tuple-element.41.need, s32[8]{0:T(128)} %get-tuple-element.40.full, ...), custom_call_target="tpu_custom_call" | custom-call | tf_op jit(solution)/shard_map/tile/pallas_call | solution.py:194
  61.8 2.0 %collective-permute-start.7 = (bf16[1024,256]{1,0:T(8,128)(2,1)}, bf16[1024,256]{1,0:T(8,128)(2,1)S(1)}, u32[]{:S(2)}, u32[]{:S(2)}) collective-permute-start(bf16[1024,256]{1,0:T(8,128)(2,1)} %get-tuple-element.14), channel_id=1, source_target_pairs={{0,16},{16,0},{1,17},{17,1},{2,18},{18,2},{3,19},{19,3},{4,20},{20... | collective-permute-start | bytes 1572872 | tf_op jit(solution)/shard_map/ppermute | solution.py:181
  63.8 2.0 %collective-permute-done.7 = bf16[1024,256]{1,0:T(8,128)(2,1)S(1)} collective-permute-done((bf16[1024,256]{1,0:T(8,128)(2,1)}, bf16[1024,256]{1,0:T(8,128)(2,1)S(1)}, u32[]{:S(2)}, u32[]{:S(2)}) %collective-permute-start.7) | collective-permute-done | bytes 524320 | tf_op jit(solution)/shard_map/ppermute | solution.py:181
  65.8 2.1 %add_convert_fusion = bf16[1024,256]{1,0:T(8,128)(2,1)} fusion(f32[1024,256]{1,0:T(8,128)} %get-tuple-element.13, bf16[1024,256]{1,0:T(8,128)(2,1)S(1)} %collective-permute-done.7), kind=kLoop, calls=%fused_computation.1 | loop fusion | flops 786432 | bytes 2097152 | tf_op jit(solution)/shard_map/convert_element_type | solution.py:221
  68.0 3.6 %all-to-all-start.1 = ((bf16[8,128,256]{2,1,0:T(8,128)(2,1)}), bf16[8,128,256]{2,1,0:T(8,128)(2,1)S(1)}, u32[]{:S(2)}, u32[]{:S(2)}) async-start(bf16[8,128,256]{2,1,0:T(8,128)(2,1)} %bitcast.16), calls=%async_computation.1 | async-start | bytes 1048576 | tf_op jit(solution)/shard_map/all_to_all | solution.py:184
  71.6 4.3 %collective-permute-start.4 = (bf16[128,512]{1,0:T(8,128)(2,1)S(1)}, bf16[128,512]{1,0:T(8,128)(2,1)S(1)}, u32[]{:S(2)}, u32[]{:S(2)}) collective-permute-start(bf16[128,512]{1,0:T(8,128)(2,1)S(1)} %copy-done.13), channel_id=1, source_target_pairs={{0,1},{1,0},{32,33},{33,32},{2,3},{3,2},{34,35},{35,34},{4,5},{5,4... | collective-permute-start | bytes 393224 | tf_op jit(solution)/shard_map/ppermute | solution.py:178
  75.9 3.6 %collective-permute-start.5 = (bf16[128,512]{1,0:T(8,128)(2,1)S(1)}, bf16[128,512]{1,0:T(8,128)(2,1)S(1)}, u32[]{:S(2)}, u32[]{:S(2)}) collective-permute-start(bf16[128,512]{1,0:T(8,128)(2,1)S(1)} %copy-done.12), channel_id=1, source_target_pairs={{0,32},{1,33},{32,0},{33,1},{2,34},{3,35},{34,2},{35,3},{4,36},{5,... | collective-permute-start | bytes 393224 | tf_op jit(solution)/shard_map/ppermute | solution.py:178
  79.6 2.2 %collective-permute-start.6 = (bf16[128,512]{1,0:T(8,128)(2,1)S(1)}, bf16[128,512]{1,0:T(8,128)(2,1)S(1)}, u32[]{:S(2)}, u32[]{:S(2)}) collective-permute-start(bf16[128,512]{1,0:T(8,128)(2,1)S(1)} %copy-done.11), channel_id=1, source_target_pairs={{0,33},{1,32},{32,1},{33,0},{2,35},{3,34},{34,3},{35,2},{4,37},{5,... | collective-permute-start | bytes 393224 | tf_op jit(solution)/shard_map/ppermute | solution.py:178
  81.8 1.1 %collective-permute-done.4 = bf16[128,512]{1,0:T(8,128)(2,1)S(1)} collective-permute-done((bf16[128,512]{1,0:T(8,128)(2,1)S(1)}, bf16[128,512]{1,0:T(8,128)(2,1)S(1)}, u32[]{:S(2)}, u32[]{:S(2)}) %collective-permute-start.4) | collective-permute-done | bytes 131104 | tf_op jit(solution)/shard_map/ppermute | solution.py:178
  82.9 2.0 %collective-permute-done.5 = bf16[128,512]{1,0:T(8,128)(2,1)S(1)} collective-permute-done((bf16[128,512]{1,0:T(8,128)(2,1)S(1)}, bf16[128,512]{1,0:T(8,128)(2,1)S(1)}, u32[]{:S(2)}, u32[]{:S(2)}) %collective-permute-start.5) | collective-permute-done | bytes 131104 | tf_op jit(solution)/shard_map/ppermute | solution.py:178
  84.9 3.5 %collective-permute-done.6 = bf16[128,512]{1,0:T(8,128)(2,1)S(1)} collective-permute-done((bf16[128,512]{1,0:T(8,128)(2,1)S(1)}, bf16[128,512]{1,0:T(8,128)(2,1)S(1)}, u32[]{:S(2)}, u32[]{:S(2)}) %collective-permute-start.6) | collective-permute-done | bytes 131104 | tf_op jit(solution)/shard_map/ppermute | solution.py:178
  88.3 0.7 multiply_convert_fusion
  89.1 0.5 all-to-all-done.1
  89.6 0.1 convert_reduce_fusion
  89.7 0.6 slice.65
  90.3 0.6 fusion
  (38 shorter events, 0.2 us)
Async XLA Ops:
  2.0 14.5 %copy-start.8 = (bf16[128,128]{1,0:T(8,128)(2,1)S(1)}, bf16[128,128]{1,0:T(8,128)(2,1)}, u32[]{:S(2)}) copy-start(bf16[128,128]{1,0:T(8,128)(2,1)} %param.13) | copy-start | bytes 98308
  2.0 14.5 %copy-start.9 = (bf16[128,128]{1,0:T(8,128)(2,1)S(1)}, bf16[128,128]{1,0:T(8,128)(2,1)}, u32[]{:S(2)}) copy-start(bf16[128,128]{1,0:T(8,128)(2,1)} %param.12) | copy-start | bytes 98308
  4.2 40.1 %collective-permute-start.2 = (bf16[128,1152]{1,0:T(8,128)(2,1)}, bf16[128,1152]{1,0:T(8,128)(2,1)S(1)}, u32[]{:S(2)}, u32[]{:S(2)}) collective-permute-start(bf16[128,1152]{1,0:T(8,128)(2,1)} %pack.1.m0), channel_id=1, source_target_pairs={{0,33},{1,32},{32,1},{33,0},{2,35},{3,34},{34,3},{35,2},{4,37},{5,... | collective-permute-start | bytes 884744 | tf_op jit(solution)/shard_map/ppermute | solution.py:178
  12.1 32.2 %collective-permute-start.1 = (bf16[128,1152]{1,0:T(8,128)(2,1)}, bf16[128,1152]{1,0:T(8,128)(2,1)S(1)}, u32[]{:S(2)}, u32[]{:S(2)}) collective-permute-start(bf16[128,1152]{1,0:T(8,128)(2,1)} %pack.1.m0), channel_id=1, source_target_pairs={{0,32},{1,33},{32,0},{33,1},{2,34},{3,35},{34,2},{35,3},{4,36},{5,... | collective-permute-start | bytes 884744 | tf_op jit(solution)/shard_map/ppermute | solution.py:178
  14.0 30.3 %collective-permute-start = (bf16[128,1152]{1,0:T(8,128)(2,1)}, bf16[128,1152]{1,0:T(8,128)(2,1)S(1)}, u32[]{:S(2)}, u32[]{:S(2)}) collective-permute-start(bf16[128,1152]{1,0:T(8,128)(2,1)} %pack.1.m0), channel_id=1, source_target_pairs={{0,1},{1,0},{32,33},{33,32},{2,3},{3,2},{34,35},{35,34},{4,5},{5,4... | collective-permute-start | bytes 884744 | tf_op jit(solution)/shard_map/ppermute | solution.py:178
  17.4 8.6 %copy-start.5 = (s32[65536]{0:T(1024)S(1)}, s32[65536]{0:T(1024)}, u32[]{:S(2)}) copy-start(s32[65536]{0:T(1024)} %param.16) | copy-start | bytes 786436
  17.4 8.6 %copy-start.6 = (s32[65536]{0:T(1024)S(1)}, s32[65536]{0:T(1024)}, u32[]{:S(2)}) copy-start(s32[65536]{0:T(1024)} %param.15) | copy-start | bytes 786436
  17.4 24.2 %all-to-all-start = ((bf16[8,128,256]{2,1,0:T(8,128)(2,1)}), bf16[8,128,256]{2,1,0:T(8,128)(2,1)S(1)}, u32[]{:S(2)}, u32[]{:S(2)}) async-start(bf16[8,128,256]{2,1,0:T(8,128)(2,1)} %broadcast_in_dim.103), calls=%async_computation | async-start | bytes 1048576 | tf_op jit(solution)/shard_map/all_to_all | solution.py:184
  24.6 0.7 copy-start.10
  41.5 3.8 %copy-start = (bf16[8,128,256]{2,1,0:T(8,128)(2,1)}, bf16[8,128,256]{2,1,0:T(8,128)(2,1)S(1)}, u32[]{:S(2)}) copy-start(bf16[8,128,256]{2,1,0:T(8,128)(2,1)S(1)} %all-to-all-done) | copy-start | bytes 1572868
  41.5 3.8 %collective-permute-start.3 = (bf16[1024,256]{1,0:T(8,128)(2,1)S(1)}, bf16[1024,256]{1,0:T(8,128)(2,1)S(1)}, u32[]{:S(2)}, u32[]{:S(2)}) collective-permute-start(bf16[1024,256]{1,0:T(8,128)(2,1)S(1)} %bitcast.22), channel_id=1, source_target_pairs={{0,16},{16,0},{1,17},{17,1},{2,18},{18,2},{3,19},{19,3},{4,20},{20... | collective-permute-start | bytes 1572872 | tf_op jit(solution)/shard_map/ppermute | solution.py:181
  44.3 1.0 %copy-start.2 = (bf16[128,1152]{1,0:T(8,128)(2,1)}, bf16[128,1152]{1,0:T(8,128)(2,1)S(1)}, u32[]{:S(2)}) copy-start(bf16[128,1152]{1,0:T(8,128)(2,1)S(1)} %collective-permute-done.2.m3) | copy-start | bytes 884740
  44.3 1.0 %copy-start.3 = (bf16[128,1152]{1,0:T(8,128)(2,1)}, bf16[128,1152]{1,0:T(8,128)(2,1)S(1)}, u32[]{:S(2)}) copy-start(bf16[128,1152]{1,0:T(8,128)(2,1)S(1)} %collective-permute-done.1.m2) | copy-start | bytes 884740
  44.3 1.0 %copy-start.4 = (bf16[128,1152]{1,0:T(8,128)(2,1)}, bf16[128,1152]{1,0:T(8,128)(2,1)S(1)}, u32[]{:S(2)}) copy-start(bf16[128,1152]{1,0:T(8,128)(2,1)S(1)} %collective-permute-done.m1) | copy-start | bytes 884740
  45.3 0.8 copy-start.1
  61.8 4.0 %collective-permute-start.7 = (bf16[1024,256]{1,0:T(8,128)(2,1)}, bf16[1024,256]{1,0:T(8,128)(2,1)S(1)}, u32[]{:S(2)}, u32[]{:S(2)}) collective-permute-start(bf16[1024,256]{1,0:T(8,128)(2,1)} %get-tuple-element.14), channel_id=1, source_target_pairs={{0,16},{16,0},{1,17},{17,1},{2,18},{18,2},{3,19},{19,3},{4,20},{20... | collective-permute-start | bytes 1572872 | tf_op jit(solution)/shard_map/ppermute | solution.py:181
  67.9 3.7 %copy-start.13 = (bf16[128,512]{1,0:T(8,128)(2,1)S(1)}, bf16[128,512]{1,0:T(8,128)(2,1)}, u32[]{:S(2)}) copy-start(bf16[128,512]{1,0:T(8,128)(2,1)} %get-tuple-element.10) | copy-start | bytes 393220
  67.9 7.9 %copy-start.12 = (bf16[128,512]{1,0:T(8,128)(2,1)S(1)}, bf16[128,512]{1,0:T(8,128)(2,1)}, u32[]{:S(2)}) copy-start(bf16[128,512]{1,0:T(8,128)(2,1)} %get-tuple-element.11) | copy-start | bytes 393220
  67.9 11.6 %copy-start.11 = (bf16[128,512]{1,0:T(8,128)(2,1)S(1)}, bf16[128,512]{1,0:T(8,128)(2,1)}, u32[]{:S(2)}) copy-start(bf16[128,512]{1,0:T(8,128)(2,1)} %get-tuple-element.12) | copy-start | bytes 393220
  68.0 20.4 %copy-start.7 = (f32[128,512]{1,0:T(8,128)S(1)}, f32[128,512]{1,0:T(8,128)}, u32[]{:S(2)}) copy-start(f32[128,512]{1,0:T(8,128)} %get-tuple-element.9) | copy-start | bytes 786436
  68.0 21.6 %all-to-all-start.1 = ((bf16[8,128,256]{2,1,0:T(8,128)(2,1)}), bf16[8,128,256]{2,1,0:T(8,128)(2,1)S(1)}, u32[]{:S(2)}, u32[]{:S(2)}) async-start(bf16[8,128,256]{2,1,0:T(8,128)(2,1)} %bitcast.16), calls=%async_computation.1 | async-start | bytes 1048576 | tf_op jit(solution)/shard_map/all_to_all | solution.py:184
  71.6 11.2 %collective-permute-start.4 = (bf16[128,512]{1,0:T(8,128)(2,1)S(1)}, bf16[128,512]{1,0:T(8,128)(2,1)S(1)}, u32[]{:S(2)}, u32[]{:S(2)}) collective-permute-start(bf16[128,512]{1,0:T(8,128)(2,1)S(1)} %copy-done.13), channel_id=1, source_target_pairs={{0,1},{1,0},{32,33},{33,32},{2,3},{3,2},{34,35},{35,34},{4,5},{5,4... | collective-permute-start | bytes 393224 | tf_op jit(solution)/shard_map/ppermute | solution.py:178
  75.9 9.0 %collective-permute-start.5 = (bf16[128,512]{1,0:T(8,128)(2,1)S(1)}, bf16[128,512]{1,0:T(8,128)(2,1)S(1)}, u32[]{:S(2)}, u32[]{:S(2)}) collective-permute-start(bf16[128,512]{1,0:T(8,128)(2,1)S(1)} %copy-done.12), channel_id=1, source_target_pairs={{0,32},{1,33},{32,0},{33,1},{2,34},{3,35},{34,2},{35,3},{4,36},{5,... | collective-permute-start | bytes 393224 | tf_op jit(solution)/shard_map/ppermute | solution.py:178
  79.6 8.8 %collective-permute-start.6 = (bf16[128,512]{1,0:T(8,128)(2,1)S(1)}, bf16[128,512]{1,0:T(8,128)(2,1)S(1)}, u32[]{:S(2)}, u32[]{:S(2)}) collective-permute-start(bf16[128,512]{1,0:T(8,128)(2,1)S(1)} %copy-done.11), channel_id=1, source_target_pairs={{0,33},{1,32},{32,1},{33,0},{2,35},{3,34},{34,3},{35,2},{4,37},{5,... | collective-permute-start | bytes 393224 | tf_op jit(solution)/shard_map/ppermute | solution.py:178

commit v2 on v1

--- a/solution.py
+++ b/solution.py
@@ -1,4 +1,3 @@
-import functools
 import jax
 import jax.numpy as jnp
 from jax import lax
@@ -28,17 +27,19 @@
     msg_ref[:, :WIDE] = q_ref[...]
     msg_ref[:, WIDE : 2 * WIDE] = d_ref[...]
     lane = lax.broadcasted_iota(jnp.int32, (TOK, DIM), 1)
-    extra = jnp.zeros((TOK, DIM), f32)
+    delta = jnp.zeros((TOK, DIM), f32)
     for h in range(HEADS):
         cut = slice(h * DIM, (h + 1) * DIM)
-        delta = jnp.sum(d_ref[:, cut].astype(f32) * o_ref[:, cut].astype(f32), axis=1, keepdims=True)
-        for base, col in ((h, lse_ref[:, h : h + 1]), (3 * HEADS + h, delta)):
-            rest = jnp.broadcast_to(col, (TOK, DIM))
-            for part in range(3):
-                low = rest.astype(bf16).astype(f32)
-                extra = jnp.where(lane == base + part * HEADS, low, extra)
-                rest = rest - low
-    msg_ref[:, 2 * WIDE :] = extra.astype(bf16)
+        column = jnp.sum(d_ref[:, cut].astype(f32) * o_ref[:, cut].astype(f32), axis=1, keepdims=True)
+        delta = jnp.where(lane == h, column, delta)
+    rest = jnp.concatenate([lse_ref[...], delta.T[:HEADS]], axis=0)
+    parts = []
+    for _ in range(3):
+        low = rest.astype(bf16).astype(f32)
+        parts.append(low)
+        rest = rest - low
+    parts.append(jnp.zeros((TOK - 6 * HEADS, DIM), f32))
+    msg_ref[:, 2 * WIDE :] = jnp.concatenate(parts, axis=0).astype(bf16)
 
 
 def nt(left, right):
@@ -59,7 +60,8 @@
     qs, ds, lse, delta, kv, kc, gk, gv, gq,
 ):
     for a, m in enumerate((m0, m1, m2, m3)):
-        meta = m[:, 2 * WIDE :].astype(f32).T
+        meta = m[: 8 * HEADS, 2 * WIDE :].astype(f32)
+        meta = meta[: 2 * HEADS] + meta[2 * HEADS : 4 * HEADS] + meta[4 * HEADS : 6 * HEADS]
         for half in range(2):
             u = 2 * a + half
             rows = slice(half * UNIT, (half + 1) * UNIT)
@@ -67,16 +69,8 @@
                 dst = slice(u * ROWS + h * UNIT, u * ROWS + (h + 1) * UNIT)
                 qs[dst, :] = m[rows, h * DIM : (h + 1) * DIM]
                 ds[dst, :] = m[rows, WIDE + h * DIM : WIDE + (h + 1) * DIM]
-            for ref, base in ((lse, 0), (delta, 3 * HEADS)):
-                ref[u] = jnp.concatenate(
-                    [
-                        meta[base + h : base + h + 1, rows]
-                        + meta[base + HEADS + h : base + HEADS + h + 1, rows]
-                        + meta[base + 2 * HEADS + h : base + 2 * HEADS + h + 1, rows]
-                        for h in range(HEADS)
-                    ],
-                    axis=1,
-                )
+            for ref, base in ((lse, 0), (delta, HEADS)):
+                ref[u] = jnp.concatenate([meta[base + h : base + h + 1, rows] for h in range(HEADS)], axis=1)
     half_keys = KEYS // 2
     kv[:half_keys, :] = kvo[...]
     kv[half_keys:, :] = kvx[...]
@@ -170,10 +164,6 @@
 
 
 def shards(queries, grad_out, attn_out, key_states, value_states, log_norm, position, modality, table):
-    msg = pl.pallas_call(
-        pack_kernel, out_shape=jax.ShapeDtypeStruct((TOK, MSG), bf16), name="pack"
-    )(queries, grad_out, attn_out, log_norm)
-
     def along_z(value, mask):
         return lax.ppermute(value, ("zlo", "zhl"), [(i, i ^ mask) for i in range(NZ)])
 
@@ -183,25 +173,30 @@
     def over_y(value):
         return lax.all_to_all(value, "y", 0, 0)
 
+    pair = jnp.concatenate([key_states, value_states], axis=1)
+    copies = jnp.broadcast_to(pair[None], (NY, TOK, 2 * DIM))
+    copies, queries = lax.optimization_barrier((copies, queries))
+    msg = pl.pallas_call(
+        pack_kernel, out_shape=pltpu.VMEM((TOK, MSG), bf16), compiler_params=pltpu.CompilerParams(vmem_limit_bytes=8 << 20), name="pack"
+    )(queries, grad_out, attn_out, log_norm.T)
+    kvo = over_y(copies).reshape(NY * TOK, 2 * DIM)
     msgs = [along_z(msg, mask) for mask in (1, 2, 3)]
-    pair = jnp.concatenate([key_states, value_states], axis=1)
-    kvo = over_y(jnp.broadcast_to(pair[None], (NY, TOK, 2 * DIM))).reshape(NY * TOK, 2 * DIM)
     kvx = other_core(kvo)
     order, need, full, kcode, qlim = plan(position, modality, table)
     smem = pl.BlockSpec(memory_space=pltpu.SMEM)
     vmem = pl.BlockSpec(memory_space=pltpu.VMEM)
-    part = jax.ShapeDtypeStruct((TOK, WIDE), bf16)
+    part = pltpu.VMEM((TOK, WIDE), bf16)
     g0, g1, g2, g3, gkvo, gkvx = pl.pallas_call(
         tile_kernel,
         in_specs=[smem] * 3 + [vmem] * 8,
         out_specs=[vmem] * 6,
         out_shape=[
-            jax.ShapeDtypeStruct((TOK, WIDE), f32),
+            pltpu.VMEM((TOK, WIDE), f32),
             part,
             part,
             part,
-            jax.ShapeDtypeStruct((NY * TOK, 2 * DIM), f32),
-            jax.ShapeDtypeStruct((NY * TOK, 2 * DIM), bf16),
+            pltpu.VMEM((NY * TOK, 2 * DIM), f32),
+            pltpu.VMEM((NY * TOK, 2 * DIM), bf16),
         ],
         scratch_shapes=[
             pltpu.VMEM((QUNITS * ROWS, DIM), bf16),
@@ -214,8 +209,9 @@
             pltpu.VMEM((KEYS, DIM), f32),
             pltpu.VMEM((QUNITS, ROWS, DIM), f32),
         ],
+        compiler_params=pltpu.CompilerParams(vmem_limit_bytes=28 << 20),
         name="tile",
-    )(order, need, full, msg, *msgs, kvo, kvx, kcode, qlim)
+    )(order, need, full, *[pltpu.with_memory_space_constraint(v, pltpu.VMEM) for v in (msg, *msgs, kvo, kvx, kcode, qlim)])
     got = other_core(gkvx)
     back = [along_z(g, mask) for g, mask in ((g1, 1), (g2, 2), (g3, 3))]
     paired = (gkvo + got.astype(f32)).astype(bf16).reshape(NY, TOK, 2 * DIM)
@@ -232,6 +228,7 @@
 def solution(mesh):
     fine = Mesh(mesh.devices.reshape(8, 2, 2, 4, 2, 2), AXES)
     tokens = P(AXES, None)
+
     return jax.shard_map(
         shards,
         mesh=fine,

time: 92.6 us -> 85.8 us (0.927)
  the two profiles are of different devices: /device:TPU:6 before, /device:TPU:1 now
where the time goes in v2:
time: 85.8 us; the launch traced here: 85.1 us
  starting transfers between devices  38.1 us (44%)
  waiting for transfers between devices  19 us (22%)
  Pallas kernels  13.5 us (16%)
  other arithmetic  10 us (12%)
  local copies, waits for them, and re-layouts  3.63 us (4%)
  between operations  0.9 us (1%)
    ppermute x6, starting transfers between devices, along_z(): lax.ppermute(value, ('zlo', 'zhl'), [(i, i ^ mask) for i in range(NZ)])  21.8 us
    pallas_call x1, Pallas kernels, shards(): pl.pallas_call(tile_kernel, in_specs=[smem] * 3 + [vmem] * 8, out_specs=[...  13.3 us
    all_to_all x2, starting transfers between devices, over_y(): return lax.all_to_all(value, 'y', 0, 0)  10.5 us
    all_to_all x2, waiting for transfers between devices, over_y(): return lax.all_to_all(value, 'y', 0, 0)  9.67 us
    ppermute x6, waiting for transfers between devices, along_z(): lax.ppermute(value, ('zlo', 'zhl'), [(i, i ^ mask) for i in range(NZ)])  6.22 us
    ppermute x2, starting transfers between devices, other_core(): return lax.ppermute(value, 'core', [(0, 1), (1, 0)])  5.79 us
    eq x2, other arithmetic, plan(): b == 1  5.68 us
    ppermute x2, waiting for transfers between devices, other_core(): return lax.ppermute(value, 'core', [(0, 1), (1, 0)])  3.11 us
  transfers between devices with their start and end apart: 10, of which 7 were waited for; matrix products, arithmetic and copies ran while one was open for 10% of the time, Pallas kernels for 0%

profile of v2, /device:TPU:1, one launch (start us, length us, event | category | flops | bytes accessed | tf_op | source)
XLA Modules:
  0.0 85.1 jit_solution(6042181652805249517)
XLA Ops:
  0.6 0.8 pad_maximum_fusion
  1.4 0.0 copy-start.1
  1.5 0.8 broadcast_in_dim.103
  2.3 0.0 copy-done
  2.3 0.1 copy-done.1
  2.5 0.2 copy-done.2
  2.6 0.2 pack.1.m0
  2.8 8.4 %collective-permute-start.2 = (bf16[128,1152]{1,0:T(8,128)(2,1)S(1)}, bf16[128,1152]{1,0:T(8,128)(2,1)S(1)}, u32[]{:S(2)}, u32[]{:S(2)}) collective-permute-start(bf16[128,1152]{1,0:T(8,128)(2,1)S(1)} %pack.1.m0), channel_id=1, source_target_pairs={{0,33},{1,32},{32,1},{33,0},{2,35},{3,34},{34,3},{35,2},{4,37},{5,... | collective-permute-start | bytes 884744 | tf_op jit(solution)/shard_map/ppermute | solution.py:168
  11.3 1.9 %collective-permute-start.1 = (bf16[128,1152]{1,0:T(8,128)(2,1)S(1)}, bf16[128,1152]{1,0:T(8,128)(2,1)S(1)}, u32[]{:S(2)}, u32[]{:S(2)}) collective-permute-start(bf16[128,1152]{1,0:T(8,128)(2,1)S(1)} %pack.1.m0), channel_id=1, source_target_pairs={{0,32},{1,33},{32,0},{33,1},{2,34},{3,35},{34,2},{35,3},{4,36},{5,... | collective-permute-start | bytes 884744 | tf_op jit(solution)/shard_map/ppermute | solution.py:168
  13.2 2.2 %collective-permute-start = (bf16[128,1152]{1,0:T(8,128)(2,1)S(1)}, bf16[128,1152]{1,0:T(8,128)(2,1)S(1)}, u32[]{:S(2)}, u32[]{:S(2)}) collective-permute-start(bf16[128,1152]{1,0:T(8,128)(2,1)S(1)} %pack.1.m0), channel_id=1, source_target_pairs={{0,1},{1,0},{32,33},{33,32},{2,3},{3,2},{34,35},{35,34},{4,5},{5,4... | collective-permute-start | bytes 884744 | tf_op jit(solution)/shard_map/ppermute | solution.py:168
  15.4 7.0 %all-to-all-start = ((bf16[8,128,256]{2,1,0:T(8,128)(2,1)}), bf16[8,128,256]{2,1,0:T(8,128)(2,1)S(1)}, u32[]{:S(2)}, u32[]{:S(2)}) async-start(bf16[8,128,256]{2,1,0:T(8,128)(2,1)} %broadcast_in_dim.103), calls=%async_computation | async-start | bytes 1048576 | tf_op jit(solution)/shard_map/all_to_all | solution.py:174
  22.4 0.1 iota_compare_fusion.2
  22.5 0.6 copy-done.6
  23.1 0.7 fusion.7
  23.9 0.1 select_reduce_fusion.1
  24.0 1.8 %select_compare_fusion.2 = (pred[4,128]{1,0:T(4,128)(4,1)S(1)}, pred[4,128]{1,0:T(4,128)(4,1)S(1)}, pred[4,128]{1,0:T(4,128)(4,1)S(1)}) fusion(s32[]{:T(128)} %bitcast.10, s32[]{:T(128)} %bitcast.9, s32[]{:T(128)} %bitcast.8, s32[4,128]{1,0:T(4,128)S(1)} %select_reduce_fusion.1), kind=kLoop, calls=%fused_computation.29 | loop fusion | flops 3072 | bytes 3596 | tf_op jit(solution)/shard_map/eq | solution.py:152
  25.8 3.9 %select_compare_fusion.1 = (pred[4,128]{1,0:T(4,128)(4,1)S(1)}, pred[4,128]{1,0:T(4,128)(4,1)S(1)}) fusion(pred[4,128]{1,0:T(4,128)(4,1)S(1)} %get-tuple-element.25, pred[4,128]{1,0:T(4,128)(4,1)S(1)} %get-tuple-element.24, s32[]{:T(128)} %bitcast.13, s32[]{:T(128)} %bitcast.12, s32[]{:T(128)} %bitcast.11, s32[]{:T(128)} %bitcast.16, s32[]{:T(128)} %bitcast.15, ...), kind=kLoop, calls=%fused_computation.28 | loop fusion | flops 3072 | bytes 2072 | tf_op jit(solution)/shard_map/eq | solution.py:152
  29.7 0.1 shift_right_arithmetic.44
  29.7 0.1 shift_right_arithmetic.43
  29.8 0.1 reshape.256
  29.9 0.1 reshape.255
  30.0 0.1 reshape.257
  30.1 0.1 shift_right_arithmetic.40
  30.2 0.1 fusion.6
  30.3 0.1 fusion.5
  30.4 0.2 convert_reduce_fusion.1
  30.6 0.1 select_reduce_fusion.order
  30.8 0.1 add_add_fusion.qlim
  30.9 8.0 %all-to-all-done = bf16[8,128,256]{2,1,0:T(8,128)(2,1)S(1)} async-done(((bf16[8,128,256]{2,1,0:T(8,128)(2,1)}), bf16[8,128,256]{2,1,0:T(8,128)(2,1)S(1)}, u32[]{:S(2)}, u32[]{:S(2)}) %all-to-all-start) | async-done | bytes 524320 | tf_op jit(solution)/shard_map/all_to_all | solution.py:174
  38.9 3.9 %collective-permute-start.3 = (bf16[1024,256]{1,0:T(8,128)(2,1)S(1)}, bf16[1024,256]{1,0:T(8,128)(2,1)S(1)}, u32[]{:S(2)}, u32[]{:S(2)}) collective-permute-start(bf16[1024,256]{1,0:T(8,128)(2,1)S(1)} %bitcast.23), channel_id=1, source_target_pairs={{0,16},{16,0},{1,17},{17,1},{2,18},{18,2},{3,19},{19,3},{4,20},{20... | collective-permute-start | bytes 1572872 | tf_op jit(solution)/shard_map/ppermute | solution.py:171
  42.8 0.2 select_reduce_fusion.2
  43.0 1.2 %collective-permute-done.3.kvx = bf16[1024,256]{1,0:T(8,128)(2,1)S(1)} collective-permute-done((bf16[1024,256]{1,0:T(8,128)(2,1)S(1)}, bf16[1024,256]{1,0:T(8,128)(2,1)S(1)}, u32[]{:S(2)}, u32[]{:S(2)}) %collective-permute-start.3) | collective-permute-done | bytes 524320 | tf_op jit(solution)/shard_map/ppermute | solution.py:171
  44.3 13.3 %tile.1 = (f32[128,512]{1,0:T(8,128)S(1)}, bf16[128,512]{1,0:T(8,128)(2,1)S(1)}, bf16[128,512]{1,0:T(8,128)(2,1)S(1)}, bf16[128,512]{1,0:T(8,128)(2,1)S(1)}, f32...) custom-call(s32[32]{0:T(128)S(1)} %select_reduce_fusion.order, s32[8]{0:T(128)S(1)} %get-tuple-element.45.need, ...), custom_call_target="tpu_custom_call" | custom-call | tf_op jit(solution)/shard_map/tile/pallas_call | solution.py:189
  57.6 1.9 %collective-permute-start.7 = (bf16[1024,256]{1,0:T(8,128)(2,1)S(1)}, bf16[1024,256]{1,0:T(8,128)(2,1)S(1)}, u32[]{:S(2)}, u32[]{:S(2)}) collective-permute-start(bf16[1024,256]{1,0:T(8,128)(2,1)S(1)} %get-tuple-element.18), channel_id=1, source_target_pairs={{0,16},{16,0},{1,17},{17,1},{2,18},{18,2},{3,19},{19,3},{4,20},{20... | collective-permute-start | bytes 1572872 | tf_op jit(solution)/shard_map/ppermute | solution.py:171
  59.5 1.9 %collective-permute-done.7 = bf16[1024,256]{1,0:T(8,128)(2,1)S(1)} collective-permute-done((bf16[1024,256]{1,0:T(8,128)(2,1)S(1)}, bf16[1024,256]{1,0:T(8,128)(2,1)S(1)}, u32[]{:S(2)}, u32[]{:S(2)}) %collective-permute-start.7) | collective-permute-done | bytes 524320 | tf_op jit(solution)/shard_map/ppermute | solution.py:171
  61.4 1.0 %add_convert_fusion = bf16[1024,256]{1,0:T(8,128)(2,1)} fusion(f32[1024,256]{1,0:T(8,128)S(1)} %get-tuple-element.17, bf16[1024,256]{1,0:T(8,128)(2,1)S(1)} %collective-permute-done.7), kind=kLoop, calls=%fused_computation.1 | loop fusion | flops 786432 | bytes 2097152 | tf_op jit(solution)/shard_map/convert_element_type | solution.py:217
  62.3 3.5 %all-to-all-start.1 = ((bf16[8,128,256]{2,1,0:T(8,128)(2,1)}), bf16[8,128,256]{2,1,0:T(8,128)(2,1)S(1)}, u32[]{:S(2)}, u32[]{:S(2)}) async-start(bf16[8,128,256]{2,1,0:T(8,128)(2,1)} %bitcast.17), calls=%async_computation.1 | async-start | bytes 1048576 | tf_op jit(solution)/shard_map/all_to_all | solution.py:174
  65.8 4.0 %collective-permute-start.4 = (bf16[128,512]{1,0:T(8,128)(2,1)S(1)}, bf16[128,512]{1,0:T(8,128)(2,1)S(1)}, u32[]{:S(2)}, u32[]{:S(2)}) collective-permute-start(bf16[128,512]{1,0:T(8,128)(2,1)S(1)} %get-tuple-element.14), channel_id=1, source_target_pairs={{0,1},{1,0},{32,33},{33,32},{2,3},{3,2},{34,35},{35,34},{4,5},{5,4... | collective-permute-start | bytes 393224 | tf_op jit(solution)/shard_map/ppermute | solution.py:168
  69.8 3.4 %collective-permute-start.5 = (bf16[128,512]{1,0:T(8,128)(2,1)S(1)}, bf16[128,512]{1,0:T(8,128)(2,1)S(1)}, u32[]{:S(2)}, u32[]{:S(2)}) collective-permute-start(bf16[128,512]{1,0:T(8,128)(2,1)S(1)} %get-tuple-element.15), channel_id=1, source_target_pairs={{0,32},{1,33},{32,0},{33,1},{2,34},{3,35},{34,2},{35,3},{4,36},{5,... | collective-permute-start | bytes 393224 | tf_op jit(solution)/shard_map/ppermute | solution.py:168
  73.2 1.9 %collective-permute-start.6 = (bf16[128,512]{1,0:T(8,128)(2,1)S(1)}, bf16[128,512]{1,0:T(8,128)(2,1)S(1)}, u32[]{:S(2)}, u32[]{:S(2)}) collective-permute-start(bf16[128,512]{1,0:T(8,128)(2,1)S(1)} %get-tuple-element.16), channel_id=1, source_target_pairs={{0,33},{1,32},{32,1},{33,0},{2,35},{3,34},{34,3},{35,2},{4,37},{5,... | collective-permute-start | bytes 393224 | tf_op jit(solution)/shard_map/ppermute | solution.py:168
  75.1 1.2 %collective-permute-done.4 = bf16[128,512]{1,0:T(8,128)(2,1)S(1)} collective-permute-done((bf16[128,512]{1,0:T(8,128)(2,1)S(1)}, bf16[128,512]{1,0:T(8,128)(2,1)S(1)}, u32[]{:S(2)}, u32[]{:S(2)}) %collective-permute-start.4) | collective-permute-done | bytes 131104 | tf_op jit(solution)/shard_map/ppermute | solution.py:168
  76.4 2.1 %collective-permute-done.5 = bf16[128,512]{1,0:T(8,128)(2,1)S(1)} collective-permute-done((bf16[128,512]{1,0:T(8,128)(2,1)S(1)}, bf16[128,512]{1,0:T(8,128)(2,1)S(1)}, u32[]{:S(2)}, u32[]{:S(2)}) %collective-permute-start.5) | collective-permute-done | bytes 131104 | tf_op jit(solution)/shard_map/ppermute | solution.py:168
  78.5 2.9 %collective-permute-done.6 = bf16[128,512]{1,0:T(8,128)(2,1)S(1)} collective-permute-done((bf16[128,512]{1,0:T(8,128)(2,1)S(1)}, bf16[128,512]{1,0:T(8,128)(2,1)S(1)}, u32[]{:S(2)}, u32[]{:S(2)}) %collective-permute-start.6) | collective-permute-done | bytes 131104 | tf_op jit(solution)/shard_map/ppermute | solution.py:168
  81.4 0.7 multiply_convert_fusion
  82.1 1.7 %all-to-all-done.1 = bf16[8,128,256]{2,1,0:T(8,128)(2,1)S(1)} async-done(((bf16[8,128,256]{2,1,0:T(8,128)(2,1)}), bf16[8,128,256]{2,1,0:T(8,128)(2,1)S(1)}, u32[]{:S(2)}, u32[]{:S(2)}) %all-to-all-start.1) | async-done | bytes 524320 | tf_op jit(solution)/shard_map/all_to_all | solution.py:174
  83.8 0.1 convert_reduce_fusion
  83.9 0.6 slice.65
  84.5 0.6 fusion
  (23 shorter events, 0.2 us)
Async XLA Ops:
  1.4 0.9 %copy-start = (bf16[128,512]{1,0:T(8,128)(2,1)S(1)}, bf16[128,512]{1,0:T(8,128)(2,1)}, u32[]{:S(2)}) copy-start(bf16[128,512]{1,0:T(8,128)(2,1)} %q_ref) | copy-start | bytes 393220
  1.4 1.0 %copy-start.1 = (bf16[128,512]{1,0:T(8,128)(2,1)S(1)}, bf16[128,512]{1,0:T(8,128)(2,1)}, u32[]{:S(2)}) copy-start(bf16[128,512]{1,0:T(8,128)(2,1)} %d_ref.1) | copy-start | bytes 393220
  1.4 1.2 %copy-start.2 = (bf16[128,512]{1,0:T(8,128)(2,1)S(1)}, bf16[128,512]{1,0:T(8,128)(2,1)}, u32[]{:S(2)}) copy-start(bf16[128,512]{1,0:T(8,128)(2,1)} %o_ref.1) | copy-start | bytes 393220
  1.4 1.2 %copy-start.3 = (f32[128,4]{0,1:T(4,128)S(1)}, f32[128,4]{0,1:T(4,128)}, u32[]{:S(2)}) copy-start(f32[128,4]{0,1:T(4,128)} %param.14) | copy-start | bytes 6148
  2.8 40.2 %collective-permute-start.2 = (bf16[128,1152]{1,0:T(8,128)(2,1)S(1)}, bf16[128,1152]{1,0:T(8,128)(2,1)S(1)}, u32[]{:S(2)}, u32[]{:S(2)}) collective-permute-start(bf16[128,1152]{1,0:T(8,128)(2,1)S(1)} %pack.1.m0), channel_id=1, source_target_pairs={{0,33},{1,32},{32,1},{33,0},{2,35},{3,34},{34,3},{35,2},{4,37},{5,... | collective-permute-start | bytes 884744 | tf_op jit(solution)/shard_map/ppermute | solution.py:168
  11.3 31.7 %collective-permute-start.1 = (bf16[128,1152]{1,0:T(8,128)(2,1)S(1)}, bf16[128,1152]{1,0:T(8,128)(2,1)S(1)}, u32[]{:S(2)}, u32[]{:S(2)}) collective-permute-start(bf16[128,1152]{1,0:T(8,128)(2,1)S(1)} %pack.1.m0), channel_id=1, source_target_pairs={{0,32},{1,33},{32,0},{33,1},{2,34},{3,35},{34,2},{35,3},{4,36},{5,... | collective-permute-start | bytes 884744 | tf_op jit(solution)/shard_map/ppermute | solution.py:168
  13.2 29.8 %collective-permute-start = (bf16[128,1152]{1,0:T(8,128)(2,1)S(1)}, bf16[128,1152]{1,0:T(8,128)(2,1)S(1)}, u32[]{:S(2)}, u32[]{:S(2)}) collective-permute-start(bf16[128,1152]{1,0:T(8,128)(2,1)S(1)} %pack.1.m0), channel_id=1, source_target_pairs={{0,1},{1,0},{32,33},{33,32},{2,3},{3,2},{34,35},{35,34},{4,5},{5,4... | collective-permute-start | bytes 884744 | tf_op jit(solution)/shard_map/ppermute | solution.py:168
  15.4 8.3 %copy-start.4 = (s32[65536]{0:T(1024)S(1)}, s32[65536]{0:T(1024)}, u32[]{:S(2)}) copy-start(s32[65536]{0:T(1024)} %param.16) | copy-start | bytes 786436
  15.4 8.3 %copy-start.5 = (s32[65536]{0:T(1024)S(1)}, s32[65536]{0:T(1024)}, u32[]{:S(2)}) copy-start(s32[65536]{0:T(1024)} %param.15) | copy-start | bytes 786436
  15.4 23.4 %all-to-all-start = ((bf16[8,128,256]{2,1,0:T(8,128)(2,1)}), bf16[8,128,256]{2,1,0:T(8,128)(2,1)S(1)}, u32[]{:S(2)}, u32[]{:S(2)}) async-start(bf16[8,128,256]{2,1,0:T(8,128)(2,1)} %broadcast_in_dim.103), calls=%async_computation | async-start | bytes 1048576 | tf_op jit(solution)/shard_map/all_to_all | solution.py:174
  22.4 0.7 copy-start.6
  38.9 5.4 %collective-permute-start.3 = (bf16[1024,256]{1,0:T(8,128)(2,1)S(1)}, bf16[1024,256]{1,0:T(8,128)(2,1)S(1)}, u32[]{:S(2)}, u32[]{:S(2)}) collective-permute-start(bf16[1024,256]{1,0:T(8,128)(2,1)S(1)} %bitcast.23), channel_id=1, source_target_pairs={{0,16},{16,0},{1,17},{17,1},{2,18},{18,2},{3,19},{19,3},{4,20},{20... | collective-permute-start | bytes 1572872 | tf_op jit(solution)/shard_map/ppermute | solution.py:171
  57.6 3.8 %collective-permute-start.7 = (bf16[1024,256]{1,0:T(8,128)(2,1)S(1)}, bf16[1024,256]{1,0:T(8,128)(2,1)S(1)}, u32[]{:S(2)}, u32[]{:S(2)}) collective-permute-start(bf16[1024,256]{1,0:T(8,128)(2,1)S(1)} %get-tuple-element.18), channel_id=1, source_target_pairs={{0,16},{16,0},{1,17},{17,1},{2,18},{18,2},{3,19},{19,3},{4,20},{20... | collective-permute-start | bytes 1572872 | tf_op jit(solution)/shard_map/ppermute | solution.py:171
  62.3 21.5 %all-to-all-start.1 = ((bf16[8,128,256]{2,1,0:T(8,128)(2,1)}), bf16[8,128,256]{2,1,0:T(8,128)(2,1)S(1)}, u32[]{:S(2)}, u32[]{:S(2)}) async-start(bf16[8,128,256]{2,1,0:T(8,128)(2,1)} %bitcast.17), calls=%async_computation.1 | async-start | bytes 1048576 | tf_op jit(solution)/shard_map/all_to_all | solution.py:174
  65.8 10.5 %collective-permute-start.4 = (bf16[128,512]{1,0:T(8,128)(2,1)S(1)}, bf16[128,512]{1,0:T(8,128)(2,1)S(1)}, u32[]{:S(2)}, u32[]{:S(2)}) collective-permute-start(bf16[128,512]{1,0:T(8,128)(2,1)S(1)} %get-tuple-element.14), channel_id=1, source_target_pairs={{0,1},{1,0},{32,33},{33,32},{2,3},{3,2},{34,35},{35,34},{4,5},{5,4... | collective-permute-start | bytes 393224 | tf_op jit(solution)/shard_map/ppermute | solution.py:168
  69.8 8.6 %collective-permute-start.5 = (bf16[128,512]{1,0:T(8,128)(2,1)S(1)}, bf16[128,512]{1,0:T(8,128)(2,1)S(1)}, u32[]{:S(2)}, u32[]{:S(2)}) collective-permute-start(bf16[128,512]{1,0:T(8,128)(2,1)S(1)} %get-tuple-element.15), channel_id=1, source_target_pairs={{0,32},{1,33},{32,0},{33,1},{2,34},{3,35},{34,2},{35,3},{4,36},{5,... | collective-permute-start | bytes 393224 | tf_op jit(solution)/shard_map/ppermute | solution.py:168
  73.2 8.1 %collective-permute-start.6 = (bf16[128,512]{1,0:T(8,128)(2,1)S(1)}, bf16[128,512]{1,0:T(8,128)(2,1)S(1)}, u32[]{:S(2)}, u32[]{:S(2)}) collective-permute-start(bf16[128,512]{1,0:T(8,128)(2,1)S(1)} %get-tuple-element.16), channel_id=1, source_target_pairs={{0,33},{1,32},{32,1},{33,0},{2,35},{3,34},{34,3},{35,2},{4,37},{5,... | collective-permute-start | bytes 393224 | tf_op jit(solution)/shard_map/ppermute | solution.py:168

commit v3 on v2

v3 whole, which is shorter than its diff:
```python
import jax
import jax.numpy as jnp
from jax import lax
from jax.experimental import pallas as pl
from jax.experimental.pallas import tpu as pltpu
from jax.sharding import Mesh, PartitionSpec as P

UNIT = 64
TOK = 128
HEADS = 4
DIM = 128
WIDE = HEADS * DIM
NZ = 4
NY = 8
QUNITS = 2 * NZ
KUNITS = NY * TOK // UNIT
GROUP = 8
MASKS = (0, 2, 1, 3)
ROWS = HEADS * UNIT
AXES = ("y", "zlo", "core", "x", "zhh", "zhl")
bf16 = jnp.bfloat16
f32 = jnp.float32


def pack_kernel(q_ref, d_ref, o_ref, lse_ref, msg_ref):
    msg_ref[:TOK, :WIDE] = q_ref[...]
    msg_ref[:TOK, WIDE:] = d_ref[...]
    lane = lax.broadcasted_iota(jnp.int32, (TOK, DIM), 1)
    delta = jnp.zeros((TOK, DIM), f32)
    for h in range(HEADS):
        cut = slice(h * DIM, (h + 1) * DIM)
        column = jnp.sum(d_ref[:, cut].astype(f32) * o_ref[:, cut].astype(f32), axis=1, keepdims=True)
        delta = jnp.where(lane == h, column, delta)
    delta = delta.T
    line = [lse_ref[h : h + 1, :] for h in range(HEADS)] + [delta[h : h + 1, :] for h in range(HEADS)]
    rest = jnp.concatenate(line, axis=1)
    parts = []
    for _ in range(3):
        low = rest.astype(bf16).astype(f32)
        parts.append(low)
        rest = rest - low
    parts.append(jnp.zeros((5, 2 * WIDE), f32))
    msg_ref[TOK:, :] = jnp.concatenate(parts, axis=0).astype(bf16)


def nt(left, right):
    return lax.dot_general(left, right, (((1,), (1,)), ((), ())), preferred_element_type=f32)


def tn(left, right):
    return lax.dot_general(left, right, (((0,), (0,)), ((), ())), preferred_element_type=f32)


def nn(left, right):
    return lax.dot_general(left, right, (((1,), (0,)), ((), ())), preferred_element_type=f32)


def tile_kernel(count, sets, chained, *refs):
    it = iter(refs)

    def take(n):
        return [next(it) for _ in range(n)]

    order, need, full = take(3)
    msgs = take(count)
    kvs = take(len(sets))
    kcode, qlim = take(2)
    olds = take(len(sets)) if chained is not None else []
    oldq = next(it) if chained == "last" else None
    gqs = take(1 if chained == "first" else count)
    gkvs = take(len(sets))
    qs, ds, lse, delta, kc, gk, gv, gq = it
    base = 0 if chained is None else QUNITS - 2 * count
    for a, m in enumerate(msgs):
        meta = m[TOK : TOK + 8].astype(f32)
        meta = meta[0:1] + meta[1:2] + meta[2:3]
        for half in range(2):
            u = 2 * a + half
            rows = slice(half * UNIT, (half + 1) * UNIT)
            for h in range(HEADS):
                dst = slice(u * ROWS + h * UNIT, u * ROWS + (h + 1) * UNIT)
                qs[dst, :] = m[rows, h * DIM : (h + 1) * DIM]
                ds[dst, :] = m[rows, WIDE + h * DIM : WIDE + (h + 1) * DIM]
            for ref, first in ((lse, 0), (delta, WIDE)):
                cuts = [first + h * TOK + half * UNIT for h in range(HEADS)]
                ref[u] = jnp.concatenate([meta[:, c : c + UNIT] for c in cuts], axis=1)
    gq[...] = jnp.zeros_like(gq) if oldq is None else oldq[...]
    score_scale = DIM ** (-0.5)
    for which, s in enumerate(sets):
        kv = kvs[which]
        for b in range(NY):
            row = kcode[s * NY + b : s * NY + b + 1, :]
            kc[b * TOK : (b + 1) * TOK, :] = jnp.broadcast_to(row, (TOK, TOK)).T
        if chained is None:
            gk[...] = jnp.zeros_like(gk)
            gv[...] = jnp.zeros_like(gv)
        else:
            gk[...] = olds[which][:, :DIM]
            gv[...] = olds[which][:, DIM:]

        def step(u, c, masked, s=s, kv=kv):
            offs = [pl.multiple_of(order[s * KUNITS + c * GROUP + i] * UNIT, UNIT) for i in range(GROUP)]
            keys = jnp.concatenate([kv[pl.ds(o, UNIT), :DIM] for o in offs], axis=0)
            vals = jnp.concatenate([kv[pl.ds(o, UNIT), DIM:] for o in offs], axis=0)
            at = pl.multiple_of(u * ROWS, ROWS)
            q = qs[pl.ds(at, ROWS), :]
            d = ds[pl.ds(at, ROWS), :]
            probs = jnp.exp(nt(keys, q) * score_scale - lse[u])
            if masked:
                code = jnp.concatenate([kc[pl.ds(o, UNIT), :] for o in offs], axis=0)
                code = jnp.concatenate([code] * (ROWS // TOK), axis=1)
                mod = code & 3
                lim = qlim[base + u]
                bound = jnp.where(mod == 0, lim[0:1], jnp.where(mod == 1, lim[1:2], lim[2:3]))
                probs = jnp.where((code >> 2) <= bound, probs, 0.0)
            grads = probs * (nt(vals, d) - delta[u])
            plow = probs.astype(bf16)
            glow = grads.astype(bf16)
            pv = nn(plow, d)
            pk = nn(glow, q)
            for i, o in enumerate(offs):
                gv[pl.ds(o, UNIT), :] += pv[i * UNIT : (i + 1) * UNIT]
                gk[pl.ds(o, UNIT), :] += pk[i * UNIT : (i + 1) * UNIT]
            gq[u] += tn(glow, keys)

        def unit(u, _, s=s, step=step):
            plain = full[s * QUNITS + base + u] // GROUP
            last = (need[s * QUNITS + base + u] + GROUP - 1) // GROUP

            def plain_step(c, _):
                step(u, c, False)
                return 0

            def masked_step(c, _):
                step(u, c, True)
                return 0

            lax.fori_loop(0, plain, plain_step, 0)
            lax.fori_loop(plain, last, masked_step, 0)
            return 0

        lax.fori_loop(0, 2 * count, unit, 0)
        out = gkvs[which]
        out[:, :DIM] = gk[...].astype(out.dtype)
        out[:, DIM:] = gv[...].astype(out.dtype)
    if chained == "first":
        gqs[0][...] = gq[...]
        return
    for a, g in enumerate(gqs):
        for half in range(2):
            rows = slice(half * UNIT, (half + 1) * UNIT)
            for h in range(HEADS):
                part = gq[2 * a + half, h * UNIT : (h + 1) * UNIT, :]
                g[rows, h * DIM : (h + 1) * DIM] = part.astype(g.dtype)


def in_vmem(value):
    return pltpu.with_memory_space_constraint(value, pltpu.VMEM)


def tile(tables, msgs, kvs, kcode, qlim, sets, chained=None, olds=(), oldq=None, gq_types=(), gkv_types=()):
    count = len(msgs)
    smem = pl.BlockSpec(memory_space=pltpu.SMEM)
    vmem = pl.BlockSpec(memory_space=pltpu.VMEM)
    arrays = [*msgs, *kvs, kcode, qlim, *olds] + ([] if oldq is None else [oldq])
    raw = pltpu.VMEM((2 * count, ROWS, DIM), f32)
    outs = [raw] if chained == "first" else [pltpu.VMEM((TOK, WIDE), t) for t in gq_types]
    outs += [pltpu.VMEM((NY * TOK, 2 * DIM), t) for t in gkv_types]

    def body(*refs):
        tile_kernel(count, sets, chained, *refs)

    return pl.pallas_call(
        body,
        in_specs=[smem] * 3 + [vmem] * len(arrays),
        out_specs=[vmem] * len(outs),
        out_shape=outs,
        scratch_shapes=[
            pltpu.VMEM((2 * count * ROWS, DIM), bf16),
            pltpu.VMEM((2 * count * ROWS, DIM), bf16),
            pltpu.VMEM((2 * count, 1, ROWS), f32),
            pltpu.VMEM((2 * count, 1, ROWS), f32),
            pltpu.VMEM((NY * TOK, DIM), jnp.int32),
            pltpu.VMEM((NY * TOK, DIM), f32),
            pltpu.VMEM((NY * TOK, DIM), f32),
            pltpu.VMEM((2 * count, ROWS, DIM), f32),
        ],
        compiler_params=pltpu.CompilerParams(vmem_limit_bytes=20 << 20),
    )(*tables, *[in_vmem(v) for v in arrays])


def plan(position, modality, table):
    code = (position * 4 + modality).reshape(8, 2, 2, 4, 2, 2, TOK)
    y, zlo, core, x, zhh, zhl = (lax.axis_index(a) for a in AXES)
    kcode = lax.dynamic_slice(code, (0, zlo, 0, x, zhh, zhl, 0), (8, 1, 2, 1, 1, 1, TOK))
    kcode = kcode.reshape(8, 2, TOK)
    kcode = jnp.where(core == 0, jnp.stack([kcode[:, 0], kcode[:, 1]]), jnp.stack([kcode[:, 1], kcode[:, 0]]))
    qcode = lax.dynamic_slice(code, (y, 0, core, x, zhh, 0, 0), (1, 2, 1, 1, 1, 2, TOK)).reshape(4, TOK)
    return tables_of(kcode, qcode, zlo * 2 + zhl, table)


def tables_of(kcode, qcode, own, table):
    masks = jnp.array(MASKS)
    pick = (own ^ masks)[:, None, None] == jnp.arange(4)[None, :, None]
    qcode = jnp.sum(jnp.where(pick, qcode[None], 0), axis=1)
    qpos, qmod = (qcode >> 2).reshape(QUNITS, UNIT), (qcode & 3).reshape(QUNITS, UNIT)
    bids = [
        jnp.where(qmod == 0, table[0, m], jnp.where(qmod == 1, table[1, m], table[2, m])) for m in range(3)
    ]
    lim = jnp.stack([jnp.where(b == 1, qpos | (UNIT - 1), qpos) for b in bids], axis=1)
    qlim = jnp.concatenate([lim] * HEADS, axis=2)
    kunit = (kcode >> 2).reshape(2, KUNITS, UNIT)
    low, high = jnp.min(kunit, axis=2), jnp.max(kunit, axis=2)
    index = jnp.arange(KUNITS)
    a, b = low[:, None, :], low[:, :, None]
    before = (a < b) | ((a == b) & (index[None, None, :] < index[None, :, None]))
    rank = jnp.sum(before.astype(jnp.int32), axis=2)
    order = jnp.sum(jnp.where(rank[:, None, :] == index[None, :, None], index[None, None, :], 0), axis=2)
    qlow, qhigh = jnp.min(qpos, axis=1), jnp.max(qpos, axis=1)
    need = jnp.sum((a // UNIT <= qhigh[None, :, None] // UNIT).astype(jnp.int32), axis=2)
    full = jnp.min(jnp.where(high[:, None, :] > qlow[None, :, None], rank[:, None, :], KUNITS), axis=2)
    return (order.reshape(-1), need.reshape(-1), full.reshape(-1)), kcode.reshape(2 * NY, TOK), qlim


def shards(queries, grad_out, attn_out, key_states, value_states, log_norm, position, modality, table):
    def along_z(value, mask):
        return lax.ppermute(value, ("zlo", "zhl"), [(i, i ^ mask) for i in range(NZ)])

    def other_core(value):
        return lax.ppermute(value, "core", [(0, 1), (1, 0)])

    def over_y(value):
        return lax.all_to_all(value, "y", 0, 0)

    pair = jnp.concatenate([key_states, value_states], axis=1)
    copies = jnp.broadcast_to(pair[None], (NY, TOK, 2 * DIM))
    copies, queries = lax.optimization_barrier((copies, queries))
    msg = pl.pallas_call(
        pack_kernel, out_shape=pltpu.VMEM((TOK + 8, 2 * WIDE), bf16), compiler_params=pltpu.CompilerParams(vmem_limit_bytes=8 << 20), name="pack"
    )(queries, grad_out, attn_out, log_norm.T)
    kvo = over_y(copies).reshape(NY * TOK, 2 * DIM)
    near = along_z(msg, MASKS[1])
    far, last = along_z(msg, MASKS[2]), along_z(msg, MASKS[3])
    kvx = other_core(kvo)
    tables, kcode, qlim = plan(position, modality, table)
    own_q, near_q, old_own, old_oth = tile(
        tables, (msg, near), (kvo, kvx), kcode, qlim, (0, 1), gq_types=(f32, bf16), gkv_types=(f32, f32)
    )
    raw_q, gkvx = tile(
        tables, (far, last), (kvx,), kcode, qlim, (1,), "first", (old_oth,), gkv_types=(bf16,)
    )
    got = other_core(gkvx)
    far_q, last_q, gkvo = tile(
        tables, (far, last), (kvo,), kcode, qlim, (0,), "last", (old_own,), raw_q, (bf16, bf16), (f32,)
    )
    paired = (gkvo + got.astype(f32)).astype(bf16).reshape(NY, TOK, 2 * DIM)
    summed = jnp.sum(over_y(paired).astype(f32), axis=0)
    back = [along_z(near_q, MASKS[1])]
    back += [along_z(far_q, MASKS[2]), along_z(last_q, MASKS[3])]
    g0 = own_q
    score_scale = DIM ** (-0.5)
    grad_q = (g0 + back[0].astype(f32) + back[1].astype(f32) + back[2].astype(f32)) * score_scale
    return (
        grad_q.astype(bf16),
        (summed[:, :DIM] * score_scale).astype(bf16),
        summed[:, DIM:].astype(bf16),
    )


def solution(mesh):
    fine = Mesh(mesh.devices.reshape(8, 2, 2, 4, 2, 2), AXES)
    tokens = P(AXES, None)

    return jax.shard_map(
        shards,
        mesh=fine,
        in_specs=(tokens,) * 6 + (P(), P(), P()),
        out_specs=(tokens,) * 3,
        check_vma=False,
    )
```

time: 85.8 us -> 89 us (1.037)
  the two profiles are of different devices: /device:TPU:1 before, /device:TPU:6 now
where the time goes in v3:
time: 89 us; the launch traced here: 87.5 us
  starting transfers between devices  37.4 us (42%)
  Pallas kernels  17.5 us (20%)
  waiting for transfers between devices  16.9 us (19%)
  other arithmetic  10.2 us (11%)
  local copies, waits for them, and re-layouts  4.59 us (5%)
  between operations  0.94 us (1%)
    ppermute x6, starting transfers between devices, along_z(): lax.ppermute(value, ('zlo', 'zhl'), [(i, i ^ mask) for i in range(NZ)])  22.7 us
    pallas_call x3, Pallas kernels, tile(): pl.pallas_call(body, in_specs=[smem] * 3 + [vmem] * len(arrays), out_spec...  17.3 us
    all_to_all x2, starting transfers between devices, over_y(): return lax.all_to_all(value, 'y', 0, 0)  10.7 us
    ppermute x6, waiting for transfers between devices, along_z(): lax.ppermute(value, ('zlo', 'zhl'), [(i, i ^ mask) for i in range(NZ)])  8 us
    all_to_all x2, waiting for transfers between devices, over_y(): return lax.all_to_all(value, 'y', 0, 0)  7.56 us
    eq x2, other arithmetic, tables_of(): b == 1  5.67 us
    ppermute x2, starting transfers between devices, other_core(): return lax.ppermute(value, 'core', [(0, 1), (1, 0)])  3.95 us
  transfers between devices with their start and end apart: 10, of which 3 were waited for; matrix products, arithmetic and copies ran while one was open for 11% of the time, Pallas kernels for 14%

profile of v3, /device:TPU:6, one launch (start us, length us, event | category | flops | bytes accessed | tf_op | source)
XLA Modules:
  0.0 87.5 jit_solution(9450605771908913841)
XLA Ops:
  0.6 0.8 pad_maximum_fusion
  1.5 0.8 broadcast_in_dim.103
  2.3 0.1 copy-done.1
  2.5 0.2 copy-done.2
  2.6 0.2 pack.1.refs_3_
  2.8 7.9 %collective-permute-start.4 = (bf16[136,1024]{1,0:T(8,128)(2,1)S(1)}, bf16[136,1024]{1,0:T(8,128)(2,1)S(1)}, u32[]{:S(2)}, u32[]{:S(2)}) collective-permute-start(bf16[136,1024]{1,0:T(8,128)(2,1)S(1)} %pack.1.refs_3_), channel_id=1, source_target_pairs={{0,33},{1,32},{32,1},{33,0},{2,35},{3,34},{34,3},{35,2},{4,37},{5,... | collective-permute-start | bytes 835592 | tf_op jit(solution)/shard_map/ppermute | solution.py:227
  10.7 1.9 %collective-permute-start.3 = (bf16[136,1024]{1,0:T(8,128)(2,1)S(1)}, bf16[136,1024]{1,0:T(8,128)(2,1)S(1)}, u32[]{:S(2)}, u32[]{:S(2)}) collective-permute-start(bf16[136,1024]{1,0:T(8,128)(2,1)S(1)} %pack.1.refs_3_), channel_id=1, source_target_pairs={{0,1},{1,0},{32,33},{33,32},{2,3},{3,2},{34,35},{35,34},{4,5},{5,4... | collective-permute-start | bytes 835592 | tf_op jit(solution)/shard_map/ppermute | solution.py:227
  12.7 2.5 %collective-permute-start = (bf16[136,1024]{1,0:T(8,128)(2,1)S(1)}, bf16[136,1024]{1,0:T(8,128)(2,1)S(1)}, u32[]{:S(2)}, u32[]{:S(2)}) collective-permute-start(bf16[136,1024]{1,0:T(8,128)(2,1)S(1)} %pack.1.refs_3_), channel_id=1, source_target_pairs={{0,32},{1,33},{32,0},{33,1},{2,34},{3,35},{34,2},{35,3},{4,36},{5,... | collective-permute-start | bytes 835592 | tf_op jit(solution)/shard_map/ppermute | solution.py:227
  15.2 7.2 %all-to-all-start = ((bf16[8,128,256]{2,1,0:T(8,128)(2,1)}), bf16[8,128,256]{2,1,0:T(8,128)(2,1)S(1)}, u32[]{:S(2)}, u32[]{:S(2)}) async-start(bf16[8,128,256]{2,1,0:T(8,128)(2,1)} %broadcast_in_dim.103), calls=%async_computation | async-start | bytes 1048576 | tf_op jit(solution)/shard_map/all_to_all | solution.py:233
  22.4 0.6 copy-done.7
  23.1 0.1 iota_compare_fusion.2
  23.1 0.6 copy-done.6
  23.7 0.7 fusion.6
  24.5 0.1 select_reduce_fusion.2
  24.6 1.8 %select_compare_fusion.2 = (pred[4,128]{1,0:T(4,128)(4,1)S(1)}, pred[4,128]{1,0:T(4,128)(4,1)S(1)}, pred[4,128]{1,0:T(4,128)(4,1)S(1)}) fusion(s32[]{:T(128)} %bitcast.10, s32[]{:T(128)} %bitcast.9, s32[]{:T(128)} %bitcast.8, s32[4,128]{1,0:T(4,128)S(1)} %select_reduce_fusion.2), kind=kLoop, calls=%fused_computation.28 | loop fusion | flops 3072 | bytes 3596 | tf_op jit(solution)/shard_map/eq | solution.py:210
  26.4 3.9 %select_compare_fusion.1 = (pred[4,128]{1,0:T(4,128)(4,1)S(1)}, pred[4,128]{1,0:T(4,128)(4,1)S(1)}) fusion(pred[4,128]{1,0:T(4,128)(4,1)S(1)} %get-tuple-element.31, pred[4,128]{1,0:T(4,128)(4,1)S(1)} %get-tuple-element.30, s32[]{:T(128)} %bitcast.13, s32[]{:T(128)} %bitcast.12, s32[]{:T(128)} %bitcast.11, s32[]{:T(128)} %bitcast.16, s32[]{:T(128)} %bitcast.15, ...), kind=kLoop, calls=%fused_computation.27 | loop fusion | flops 3072 | bytes 2072 | tf_op jit(solution)/shard_map/eq | solution.py:210
  30.3 0.1 shift_right_arithmetic.40
  30.4 0.1 shift_right_arithmetic.39
  30.5 0.1 reshape.282
  30.6 0.1 reshape.281
  30.7 0.1 reshape.283
  30.8 0.1 stack.21
  30.9 0.2 fusion.2
  31.0 0.2 fusion.5
  31.2 0.2 convert_reduce_fusion.2
  31.4 0.2 convert_reduce_fusion.1
  31.6 0.2 select_reduce_fusion.1
  31.8 7.6 %all-to-all-done = bf16[8,128,256]{2,1,0:T(8,128)(2,1)S(1)} async-done(((bf16[8,128,256]{2,1,0:T(8,128)(2,1)}), bf16[8,128,256]{2,1,0:T(8,128)(2,1)S(1)}, u32[]{:S(2)}, u32[]{:S(2)}) %all-to-all-start) | async-done | bytes 524320 | tf_op jit(solution)/shard_map/all_to_all | solution.py:233
  39.3 1.9 %collective-permute-start.1 = (bf16[1024,256]{1,0:T(8,128)(2,1)S(1)}, bf16[1024,256]{1,0:T(8,128)(2,1)S(1)}, u32[]{:S(2)}, u32[]{:S(2)}) collective-permute-start(bf16[1024,256]{1,0:T(8,128)(2,1)S(1)} %bitcast.27), channel_id=1, source_target_pairs={{0,16},{16,0},{1,17},{17,1},{2,18},{18,2},{3,19},{19,3},{4,20},{20... | collective-permute-start | bytes 1572872 | tf_op jit(solution)/shard_map/ppermute | solution.py:230
  41.3 0.1 select_reduce_fusion
  41.4 0.1 reshape.272.refs_2_
  41.5 0.1 reshape.270.refs_0_
  41.6 0.1 reshape.271.refs_1_
  41.6 0.1 add_add_fusion.refs_8_.refs_7_
  41.8 1.3 %collective-permute-done.1.refs_6_.refs_5_ = bf16[1024,256]{1,0:T(8,128)(2,1)S(1)} collective-permute-done((bf16[1024,256]{1,0:T(8,128)(2,1)S(1)}, bf16[1024,256]{1,0:T(8,128)(2,1)S(1)}, u32[]{:S(2)}, u32[]{:S(2)}) %collective-permute-start.1) | collective-permute-done | bytes 524320 | tf_op jit(solution)/shard_map/ppermute | solution.py:230
  43.1 8.0 %shard_map.121 = (f32[128,512]{1,0:T(8,128)S(1)}, bf16[128,512]{1,0:T(8,128)(2,1)S(1)}, f32[1024,256]{1,0:T(8,128)S(1)}, f32[1024,256]{1,0:T(8,128)S(1)}) custom-call(s32[32]{0:T(128)S(1)} %reshape.270.refs_0_, s32[16]{0:T(128)S(1)} %reshape.271.refs_1_, s32[16]{0:T(128)S(1)} %reshape.272.refs_2_, bf16[136,1024]{1,0:T(8,128)(2,1)S(1)} %pack.1.refs_3_, ...), custom_call_target="tpu_custom_call" | custom-call | tf_op jit(solution)/shard_map/pallas_call | solution.py:173
  51.1 4.7 %shard_map.122 = (f32[4,256,128]{2,1,0:T(8,128)S(1)}, bf16[1024,256]{1,0:T(8,128)(2,1)S(1)}) custom-call(s32[32]{0:T(128)S(1)} %reshape.270.refs_0_, s32[16]{0:T(128)S(1)} %reshape.271.refs_1_, s32[16]{0:T(128)S(1)} %reshape.272.refs_2_, bf16[136,1024]{1,0:T(8,128)(2,1)S(1)} %collective-permute-done.3.refs_3_, ...), custom_call_target="tpu_custom_call" | custom-call | tf_op jit(solution)/shard_map/pallas_call | solution.py:173
  55.8 2.0 %collective-permute-start.7 = (bf16[1024,256]{1,0:T(8,128)(2,1)S(1)}, bf16[1024,256]{1,0:T(8,128)(2,1)S(1)}, u32[]{:S(2)}, u32[]{:S(2)}) collective-permute-start(bf16[1024,256]{1,0:T(8,128)(2,1)S(1)} %get-tuple-element.24), channel_id=1, source_target_pairs={{0,16},{16,0},{1,17},{17,1},{2,18},{18,2},{3,19},{19,3},{4,20},{20... | collective-permute-start | bytes 1572872 | tf_op jit(solution)/shard_map/ppermute | solution.py:230
  57.9 4.7 %shard_map.123 = (bf16[128,512]{1,0:T(8,128)(2,1)S(1)}, bf16[128,512]{1,0:T(8,128)(2,1)S(1)}, f32[1024,256]{1,0:T(8,128)S(1)}) custom-call(s32[32]{0:T(128)S(1)} %reshape.270.refs_0_, s32[16]{0:T(128)S(1)} %reshape.271.refs_1_, s32[16]{0:T(128)S(1)} %reshape.272.refs_2_, bf16[136,1024]{1,0:T(8,128)(2,1)S(1)} %collective-permute-done.3.refs_3_, ...), custom_call_target="tpu_custom_call" | custom-call | tf_op jit(solution)/shard_map/pallas_call | solution.py:173
  62.6 1.0 %add_convert_fusion = bf16[1024,256]{1,0:T(8,128)(2,1)} fusion(f32[1024,256]{1,0:T(8,128)S(1)} %get-tuple-element.23, bf16[1024,256]{1,0:T(8,128)(2,1)S(1)} %collective-permute-done.7), kind=kLoop, calls=%fused_computation.1 | loop fusion | flops 786432 | bytes 2097152 | tf_op jit(solution)/shard_map/convert_element_type | solution.py:256
  63.6 3.5 %all-to-all-start.1 = ((bf16[8,128,256]{2,1,0:T(8,128)(2,1)}), bf16[8,128,256]{2,1,0:T(8,128)(2,1)S(1)}, u32[]{:S(2)}, u32[]{:S(2)}) async-start(bf16[8,128,256]{2,1,0:T(8,128)(2,1)} %bitcast.17), calls=%async_computation.1 | async-start | bytes 1048576 | tf_op jit(solution)/shard_map/all_to_all | solution.py:233
  67.1 3.9 %collective-permute-start.2 = (bf16[128,512]{1,0:T(8,128)(2,1)S(1)}, bf16[128,512]{1,0:T(8,128)(2,1)S(1)}, u32[]{:S(2)}, u32[]{:S(2)}) collective-permute-start(bf16[128,512]{1,0:T(8,128)(2,1)S(1)} %get-tuple-element.17), channel_id=1, source_target_pairs={{0,32},{1,33},{32,0},{33,1},{2,34},{3,35},{34,2},{35,3},{4,36},{5,... | collective-permute-start | bytes 393224 | tf_op jit(solution)/shard_map/ppermute | solution.py:227
  71.0 4.5 %collective-permute-start.5 = (bf16[128,512]{1,0:T(8,128)(2,1)S(1)}, bf16[128,512]{1,0:T(8,128)(2,1)S(1)}, u32[]{:S(2)}, u32[]{:S(2)}) collective-permute-start(bf16[128,512]{1,0:T(8,128)(2,1)S(1)} %get-tuple-element.21), channel_id=1, source_target_pairs={{0,1},{1,0},{32,33},{33,32},{2,3},{3,2},{34,35},{35,34},{4,5},{5,4... | collective-permute-start | bytes 393224 | tf_op jit(solution)/shard_map/ppermute | solution.py:227
  75.6 1.9 %collective-permute-start.6 = (bf16[128,512]{1,0:T(8,128)(2,1)S(1)}, bf16[128,512]{1,0:T(8,128)(2,1)S(1)}, u32[]{:S(2)}, u32[]{:S(2)}) collective-permute-start(bf16[128,512]{1,0:T(8,128)(2,1)S(1)} %get-tuple-element.22), channel_id=1, source_target_pairs={{0,33},{1,32},{32,1},{33,0},{2,35},{3,34},{34,3},{35,2},{4,37},{5,... | collective-permute-start | bytes 393224 | tf_op jit(solution)/shard_map/ppermute | solution.py:227
  77.5 8.0 %collective-permute-done.5 = bf16[128,512]{1,0:T(8,128)(2,1)S(1)} collective-permute-done((bf16[128,512]{1,0:T(8,128)(2,1)S(1)}, bf16[128,512]{1,0:T(8,128)(2,1)S(1)}, u32[]{:S(2)}, u32[]{:S(2)}) %collective-permute-start.5) | collective-permute-done | bytes 131104 | tf_op jit(solution)/shard_map/ppermute | solution.py:227
  85.5 0.7 multiply_convert_fusion
  86.3 0.6 slice.65
  86.9 0.6 fusion
  (33 shorter events, 0.4 us)
Async XLA Ops:
  1.4 0.9 %copy-start = (bf16[128,512]{1,0:T(8,128)(2,1)S(1)}, bf16[128,512]{1,0:T(8,128)(2,1)}, u32[]{:S(2)}) copy-start(bf16[128,512]{1,0:T(8,128)(2,1)} %q_ref) | copy-start | bytes 393220
  1.4 1.0 %copy-start.1 = (bf16[128,512]{1,0:T(8,128)(2,1)S(1)}, bf16[128,512]{1,0:T(8,128)(2,1)}, u32[]{:S(2)}) copy-start(bf16[128,512]{1,0:T(8,128)(2,1)} %d_ref.1) | copy-start | bytes 393220
  1.4 1.2 %copy-start.2 = (bf16[128,512]{1,0:T(8,128)(2,1)S(1)}, bf16[128,512]{1,0:T(8,128)(2,1)}, u32[]{:S(2)}) copy-start(bf16[128,512]{1,0:T(8,128)(2,1)} %o_ref.1) | copy-start | bytes 393220
  1.4 1.2 %copy-start.3 = (f32[128,4]{0,1:T(4,128)S(1)}, f32[128,4]{0,1:T(4,128)}, u32[]{:S(2)}) copy-start(f32[128,4]{0,1:T(4,128)} %param.15) | copy-start | bytes 6148
  2.8 48.3 %collective-permute-start.4 = (bf16[136,1024]{1,0:T(8,128)(2,1)S(1)}, bf16[136,1024]{1,0:T(8,128)(2,1)S(1)}, u32[]{:S(2)}, u32[]{:S(2)}) collective-permute-start(bf16[136,1024]{1,0:T(8,128)(2,1)S(1)} %pack.1.refs_3_), channel_id=1, source_target_pairs={{0,33},{1,32},{32,1},{33,0},{2,35},{3,34},{34,3},{35,2},{4,37},{5,... | collective-permute-start | bytes 835592 | tf_op jit(solution)/shard_map/ppermute | solution.py:227
  10.7 40.4 %collective-permute-start.3 = (bf16[136,1024]{1,0:T(8,128)(2,1)S(1)}, bf16[136,1024]{1,0:T(8,128)(2,1)S(1)}, u32[]{:S(2)}, u32[]{:S(2)}) collective-permute-start(bf16[136,1024]{1,0:T(8,128)(2,1)S(1)} %pack.1.refs_3_), channel_id=1, source_target_pairs={{0,1},{1,0},{32,33},{33,32},{2,3},{3,2},{34,35},{35,34},{4,5},{5,4... | collective-permute-start | bytes 835592 | tf_op jit(solution)/shard_map/ppermute | solution.py:227
  12.7 29.2 %collective-permute-start = (bf16[136,1024]{1,0:T(8,128)(2,1)S(1)}, bf16[136,1024]{1,0:T(8,128)(2,1)S(1)}, u32[]{:S(2)}, u32[]{:S(2)}) collective-permute-start(bf16[136,1024]{1,0:T(8,128)(2,1)S(1)} %pack.1.refs_3_), channel_id=1, source_target_pairs={{0,32},{1,33},{32,0},{33,1},{2,34},{3,35},{34,2},{35,3},{4,36},{5,... | collective-permute-start | bytes 835592 | tf_op jit(solution)/shard_map/ppermute | solution.py:227
  15.1 9.3 %copy-start.4 = (s32[65536]{0:T(1024)S(1)}, s32[65536]{0:T(1024)}, u32[]{:S(2)}) copy-start(s32[65536]{0:T(1024)} %param.17) | copy-start | bytes 786436
  15.1 9.3 %copy-start.5 = (s32[65536]{0:T(1024)S(1)}, s32[65536]{0:T(1024)}, u32[]{:S(2)}) copy-start(s32[65536]{0:T(1024)} %param.16) | copy-start | bytes 786436
  15.2 24.2 %all-to-all-start = ((bf16[8,128,256]{2,1,0:T(8,128)(2,1)}), bf16[8,128,256]{2,1,0:T(8,128)(2,1)S(1)}, u32[]{:S(2)}, u32[]{:S(2)}) async-start(bf16[8,128,256]{2,1,0:T(8,128)(2,1)} %broadcast_in_dim.103), calls=%async_computation | async-start | bytes 1048576 | tf_op jit(solution)/shard_map/all_to_all | solution.py:233
  22.4 0.7 copy-start.7
  23.1 0.7 copy-start.6
  39.3 3.8 %collective-permute-start.1 = (bf16[1024,256]{1,0:T(8,128)(2,1)S(1)}, bf16[1024,256]{1,0:T(8,128)(2,1)S(1)}, u32[]{:S(2)}, u32[]{:S(2)}) collective-permute-start(bf16[1024,256]{1,0:T(8,128)(2,1)S(1)} %bitcast.27), channel_id=1, source_target_pairs={{0,16},{16,0},{1,17},{17,1},{2,18},{18,2},{3,19},{19,3},{4,20},{20... | collective-permute-start | bytes 1572872 | tf_op jit(solution)/shard_map/ppermute | solution.py:230
  55.8 6.8 %collective-permute-start.7 = (bf16[1024,256]{1,0:T(8,128)(2,1)S(1)}, bf16[1024,256]{1,0:T(8,128)(2,1)S(1)}, u32[]{:S(2)}, u32[]{:S(2)}) collective-permute-start(bf16[1024,256]{1,0:T(8,128)(2,1)S(1)} %get-tuple-element.24), channel_id=1, source_target_pairs={{0,16},{16,0},{1,17},{17,1},{2,18},{18,2},{3,19},{19,3},{4,20},{20... | collective-permute-start | bytes 1572872 | tf_op jit(solution)/shard_map/ppermute | solution.py:230
  63.6 22.7 %all-to-all-start.1 = ((bf16[8,128,256]{2,1,0:T(8,128)(2,1)}), bf16[8,128,256]{2,1,0:T(8,128)(2,1)S(1)}, u32[]{:S(2)}, u32[]{:S(2)}) async-start(bf16[8,128,256]{2,1,0:T(8,128)(2,1)} %bitcast.17), calls=%async_computation.1 | async-start | bytes 1048576 | tf_op jit(solution)/shard_map/all_to_all | solution.py:233
  67.1 10.4 %collective-permute-start.2 = (bf16[128,512]{1,0:T(8,128)(2,1)S(1)}, bf16[128,512]{1,0:T(8,128)(2,1)S(1)}, u32[]{:S(2)}, u32[]{:S(2)}) collective-permute-start(bf16[128,512]{1,0:T(8,128)(2,1)S(1)} %get-tuple-element.17), channel_id=1, source_target_pairs={{0,32},{1,33},{32,0},{33,1},{2,34},{3,35},{34,2},{35,3},{4,36},{5,... | collective-permute-start | bytes 393224 | tf_op jit(solution)/shard_map/ppermute | solution.py:227
  71.0 14.5 %collective-permute-start.5 = (bf16[128,512]{1,0:T(8,128)(2,1)S(1)}, bf16[128,512]{1,0:T(8,128)(2,1)S(1)}, u32[]{:S(2)}, u32[]{:S(2)}) collective-permute-start(bf16[128,512]{1,0:T(8,128)(2,1)S(1)} %get-tuple-element.21), channel_id=1, source_target_pairs={{0,1},{1,0},{32,33},{33,32},{2,3},{3,2},{34,35},{35,34},{4,5},{5,4... | collective-permute-start | bytes 393224 | tf_op jit(solution)/shard_map/ppermute | solution.py:227
  75.6 9.9 %collective-permute-start.6 = (bf16[128,512]{1,0:T(8,128)(2,1)S(1)}, bf16[128,512]{1,0:T(8,128)(2,1)S(1)}, u32[]{:S(2)}, u32[]{:S(2)}) collective-permute-start(bf16[128,512]{1,0:T(8,128)(2,1)S(1)} %get-tuple-element.22), channel_id=1, source_target_pairs={{0,33},{1,32},{32,1},{33,0},{2,35},{3,34},{34,3},{35,2},{4,37},{5,... | collective-permute-start | bytes 393224 | tf_op jit(solution)/shard_map/ppermute | solution.py:227

commit v4 on v3

v4 whole, which is shorter than its diff:
```python
import jax
import jax.numpy as jnp
from jax import lax
from jax.experimental import pallas as pl
from jax.experimental.pallas import tpu as pltpu
from jax.sharding import Mesh, PartitionSpec as P

UNIT = 64
TOK = 128
HEADS = 4
DIM = 128
WIDE = HEADS * DIM
NZ = 4
NY = 8
QUNITS = 2 * NZ
KUNITS = NY * TOK // UNIT
GROUP = 8
PAR = 2
MASKS = (0, 2, 1, 3)
ROWS = HEADS * UNIT
AXES = ("y", "zlo", "core", "x", "zhh", "zhl")
bf16 = jnp.bfloat16
f32 = jnp.float32


def pack_kernel(q_ref, d_ref, o_ref, lse_ref, msg_ref):
    msg_ref[:TOK, :WIDE] = q_ref[...]
    msg_ref[:TOK, WIDE:] = d_ref[...]
    lane = lax.broadcasted_iota(jnp.int32, (TOK, DIM), 1)
    delta = jnp.zeros((TOK, DIM), f32)
    for h in range(HEADS):
        cut = slice(h * DIM, (h + 1) * DIM)
        column = jnp.sum(d_ref[:, cut].astype(f32) * o_ref[:, cut].astype(f32), axis=1, keepdims=True)
        delta = jnp.where(lane == h, column, delta)
    delta = delta.T
    line = [lse_ref[h : h + 1, :] for h in range(HEADS)] + [delta[h : h + 1, :] for h in range(HEADS)]
    rest = jnp.concatenate(line, axis=1)
    parts = []
    for _ in range(3):
        low = rest.astype(bf16).astype(f32)
        parts.append(low)
        rest = rest - low
    parts.append(jnp.zeros((5, 2 * WIDE), f32))
    msg_ref[TOK:, :] = jnp.concatenate(parts, axis=0).astype(bf16)


def nt(left, right):
    return lax.dot_general(left, right, (((1,), (1,)), ((), ())), preferred_element_type=f32)


def nn(left, right):
    return lax.dot_general(left, right, (((1,), (0,)), ((), ())), preferred_element_type=f32)


def tile_kernel(cfg, *refs):
    it = iter(refs)

    def take(n):
        return [next(it) for _ in range(n)]

    start, count, s, finals, raws, old_units, has_acc, spread_out = cfg
    rank, need = take(2)
    msgs = take(count)
    kv, kcode, qlim = take(3)
    oldq = next(it) if old_units else None
    old = next(it) if has_acc else None
    gqs = take(len(finals))
    rawq = next(it) if raws else None
    out = next(it)
    qs, ds, lse, delta, ks, kt, kc, gq, work = take(9)
    acc = next(it) if spread_out else out
    base = 2 * start
    units = 2 * count
    chunks = KUNITS // GROUP
    filled = jnp.int32(0)
    for u in range(units):
        for c in range(chunks):
            work[filled] = c * units + u
            active = c * GROUP < need[s * QUNITS + base + u]
            filled = filled + active.astype(jnp.int32)
    rounds = (filled + PAR - 1) // PAR
    for a, m in enumerate(msgs):
        meta = m[TOK : TOK + 8].astype(f32)
        meta = meta[0:1] + meta[1:2] + meta[2:3]
        for half in range(2):
            u = 2 * a + half
            rows = slice(half * UNIT, (half + 1) * UNIT)
            for h in range(HEADS):
                dst = slice(u * ROWS + h * UNIT, u * ROWS + (h + 1) * UNIT)
                qs[dst, :] = m[rows, h * DIM : (h + 1) * DIM]
                ds[dst, :] = m[rows, WIDE + h * DIM : WIDE + (h + 1) * DIM]
            for ref, first in ((lse, 0), (delta, WIDE)):
                cuts = [first + h * TOK + half * UNIT for h in range(HEADS)]
                ref[u] = jnp.concatenate([meta[:, c : c + UNIT] for c in cuts], axis=1)
    gq[...] = jnp.zeros_like(gq)
    if oldq is not None:
        gq[:old_units] = oldq[...]
    acc[...] = jnp.zeros_like(acc) if old is None else old[...]
    spots = []
    for b in range(NY):
        row = kcode[s * NY + b : s * NY + b + 1, :]
        wide = jnp.broadcast_to(row, (TOK, TOK)).T
        for half in range(2):
            i = 2 * b + half
            spot = pl.multiple_of(rank[s * KUNITS + i] * UNIT, UNIT)
            spots.append(spot)
            ks[pl.ds(spot, UNIT), :] = kv[i * UNIT : (i + 1) * UNIT, :]
            kc[pl.ds(spot, UNIT), :] = wide[half * UNIT : (half + 1) * UNIT]
    span = GROUP * UNIT
    for c in range(chunks):
        kt[c] = ks[c * span : (c + 1) * span, :DIM].astype(f32).T.astype(bf16)
    score_scale = DIM ** (-0.5)

    def item(index):
        code = jnp.where(index < filled, work[jnp.minimum(index, filled - 1)], 0)
        u = code % units
        c = code // units
        spot = pl.ds(pl.multiple_of(c * span, span), span)
        keys, vals = ks[spot, :DIM], ks[spot, DIM:]
        at = pl.ds(pl.multiple_of(u * ROWS, ROWS), ROWS)
        q, d = qs[at, :], ds[at, :]
        probs = jnp.exp(nt(keys, q) * score_scale - lse[u])
        kcodes = kc[spot, :]
        mod, pos = kcodes & 3, kcodes >> 2
        lim = jnp.where(index < filled, qlim[base + u], -1)
        bands = []
        for cut in (slice(0, DIM), slice(DIM, ROWS)):
            bound = jnp.where(mod == 0, lim[0:1, cut], jnp.where(mod == 1, lim[1:2, cut], lim[2:3, cut]))
            bands.append(jnp.where(pos <= bound, probs[:, cut], 0.0))
        probs = jnp.concatenate(bands, axis=1)
        grads = probs * (nt(vals, d) - delta[u])
        plow = probs.astype(bf16)
        glow = grads.astype(bf16)
        acc[spot, DIM:] += nn(plow, d)
        acc[spot, :DIM] += nn(glow, q)
        gq[u] += nn(kt[c], glow)

    def body(r, _):
        for j in range(PAR):
            item(r * PAR + j)
        return 0

    lax.fori_loop(0, rounds, body, 0)
    if spread_out:
        for i, spot in enumerate(spots):
            out[i * UNIT : (i + 1) * UNIT, :] = acc[pl.ds(spot, UNIT), :].astype(out.dtype)
    if rawq is not None:
        rawq[...] = gq[raws[0] : raws[1]]
    for (a, _), g in zip(finals, gqs):
        for half in range(2):
            rows = slice(half * UNIT, (half + 1) * UNIT)
            whole = gq[2 * a + half].T
            for h in range(HEADS):
                part = whole[h * UNIT : (h + 1) * UNIT, :]
                g[rows, h * DIM : (h + 1) * DIM] = part.astype(g.dtype)


def in_vmem(value):
    return pltpu.with_memory_space_constraint(value, pltpu.VMEM)


def tile(tables, start, msgs, kv, kcode, qlim, s, finals=(), raws=None, oldq=None, old=None, out_type=None):
    count = len(msgs)
    units = 2 * count
    keys = KUNITS * UNIT
    smem = pl.BlockSpec(memory_space=pltpu.SMEM)
    vmem = pl.BlockSpec(memory_space=pltpu.VMEM)
    arrays = [*msgs, kv, kcode, qlim] + [v for v in (oldq, old) if v is not None]
    outs = [pltpu.VMEM((TOK, WIDE), t) for _, t in finals]
    if raws:
        outs.append(pltpu.VMEM((raws[1] - raws[0], DIM, ROWS), f32))
    outs.append(pltpu.VMEM((keys, 2 * DIM), out_type or f32))
    scratch = [
        pltpu.VMEM((units * ROWS, DIM), bf16),
        pltpu.VMEM((units * ROWS, DIM), bf16),
        pltpu.VMEM((units, 1, ROWS), f32),
        pltpu.VMEM((units, 1, ROWS), f32),
        pltpu.VMEM((keys, 2 * DIM), bf16),
        pltpu.VMEM((KUNITS // GROUP, DIM, GROUP * UNIT), bf16),
        pltpu.VMEM((keys, DIM), jnp.int32),
        pltpu.VMEM((units, DIM, ROWS), f32),
        pltpu.SMEM((units * (KUNITS // GROUP) + 1,), jnp.int32),
    ]
    if out_type:
        scratch.append(pltpu.VMEM((keys, 2 * DIM), f32))
    cfg = (
        start, count, s, finals, raws, 0 if oldq is None else oldq.shape[0], old is not None, out_type is not None
    )

    def body(*refs):
        tile_kernel(cfg, *refs)

    return pl.pallas_call(
        body,
        in_specs=[smem] * 2 + [vmem] * len(arrays),
        out_specs=[vmem] * len(outs),
        out_shape=outs,
        scratch_shapes=scratch,
        compiler_params=pltpu.CompilerParams(vmem_limit_bytes=20 << 20),
    )(*tables, *[in_vmem(v) for v in arrays])


def finish_kernel(parts, key_ref, value_ref):
    total = jnp.sum(parts[...].astype(f32), axis=0)
    key_ref[...] = (total[:, :DIM] * DIM ** (-0.5)).astype(bf16)
    value_ref[...] = total[:, DIM:].astype(bf16)


def copies_kernel(key_ref, value_ref, out):
    for i in range(NY):
        out[i, :, :DIM] = key_ref[...]
        out[i, :, DIM:] = value_ref[...]


def plan(position, modality, table):
    code = (position * 4 + modality).reshape(8, 2, 2, 4, 2, 2, TOK)
    y, zlo, core, x, zhh, zhl = (lax.axis_index(a) for a in AXES)
    kcode = lax.dynamic_slice(code, (0, zlo, 0, x, zhh, zhl, 0), (8, 1, 2, 1, 1, 1, TOK))
    kcode = kcode.reshape(8, 2, TOK)
    kcode = jnp.where(core == 0, jnp.stack([kcode[:, 0], kcode[:, 1]]), jnp.stack([kcode[:, 1], kcode[:, 0]]))
    qcode = lax.dynamic_slice(code, (y, 0, core, x, zhh, 0, 0), (1, 2, 1, 1, 1, 2, TOK)).reshape(4, TOK)
    return tables_of(kcode, qcode, zlo * 2 + zhl, table)


def tables_of(kcode, qcode, own, table):
    masks = jnp.array(MASKS)
    pick = (own ^ masks)[:, None, None] == jnp.arange(4)[None, :, None]
    qcode = jnp.sum(jnp.where(pick, qcode[None], 0), axis=1)
    qpos, qmod = (qcode >> 2).reshape(QUNITS, UNIT), (qcode & 3).reshape(QUNITS, UNIT)
    bids = [
        jnp.where(qmod == 0, table[0, m], jnp.where(qmod == 1, table[1, m], table[2, m])) for m in range(3)
    ]
    lim = jnp.stack([jnp.where(b == 1, qpos | (UNIT - 1), qpos) for b in bids], axis=1)
    qlim = jnp.concatenate([lim] * HEADS, axis=2)
    kunit = (kcode >> 2).reshape(2, KUNITS, UNIT)
    low = jnp.min(kunit, axis=2)
    index = jnp.arange(KUNITS)
    a, b = low[:, None, :], low[:, :, None]
    before = (a < b) | ((a == b) & (index[None, None, :] < index[None, :, None]))
    rank = jnp.sum(before.astype(jnp.int32), axis=2)
    qhigh = jnp.max(qpos, axis=1)
    need = jnp.sum((a // UNIT <= qhigh[None, :, None] // UNIT).astype(jnp.int32), axis=2)
    return (rank.reshape(-1), need.reshape(-1)), kcode.reshape(2 * NY, TOK), qlim


def shards(queries, grad_out, attn_out, key_states, value_states, log_norm, position, modality, table):
    def along_z(value, mask):
        return lax.ppermute(value, ("zlo", "zhl"), [(i, i ^ mask) for i in range(NZ)])

    def other_core(value):
        return lax.ppermute(value, "core", [(0, 1), (1, 0)])

    def over_y(value):
        return lax.all_to_all(value, "y", 0, 0)

    copies = pl.pallas_call(
        copies_kernel,
        out_shape=jax.ShapeDtypeStruct((NY, TOK, 2 * DIM), bf16),
        compiler_params=pltpu.CompilerParams(vmem_limit_bytes=8 << 20),
        name="copies",
    )(key_states, value_states)
    copies, queries = lax.optimization_barrier((copies, queries))
    msg = pl.pallas_call(
        pack_kernel, out_shape=pltpu.VMEM((TOK + 8, 2 * WIDE), bf16), compiler_params=pltpu.CompilerParams(vmem_limit_bytes=8 << 20), name="pack"
    )(queries, grad_out, attn_out, log_norm.T)
    kvo = over_y(copies).reshape(NY * TOK, 2 * DIM)
    near = along_z(msg, MASKS[1])
    far, last = along_z(msg, MASKS[2]), along_z(msg, MASKS[3])
    tables, kcode, qlim = plan(position, modality, table)
    kvo, tables, kcode, qlim = lax.optimization_barrier((kvo, tables, kcode, qlim))
    kvx = other_core(kvo)
    raw_near, old = tile(tables, 0, (msg, near), kvo, kcode, qlim, 0, raws=(0, 4))
    own_q, near_q, raw_far, gkvx = tile(
        tables, 0, (msg, near, far, last), kvx, kcode, qlim, 1,
        ((0, f32), (1, bf16)), (4, 8), raw_near, None, bf16,
    )
    got = other_core(gkvx)
    far_q, last_q, gkvo = tile(
        tables, 2, (far, last), kvo, kcode, qlim, 0, ((0, bf16), (1, bf16)), None, raw_far, old, f32
    )
    paired = (gkvo + got.astype(f32)).astype(bf16).reshape(NY, TOK, 2 * DIM)
    summed = over_y(paired)
    narrow = jax.ShapeDtypeStruct((TOK, DIM), bf16)
    grad_key, grad_value = pl.pallas_call(
        finish_kernel, out_shape=[narrow] * 2, compiler_params=pltpu.CompilerParams(vmem_limit_bytes=8 << 20), name="finish"
    )(in_vmem(summed))
    back = [along_z(near_q, MASKS[1])]
    back += [along_z(far_q, MASKS[2]), along_z(last_q, MASKS[3])]
    g0 = own_q
    score_scale = DIM ** (-0.5)
    grad_q = (g0 + back[0].astype(f32) + back[1].astype(f32) + back[2].astype(f32)) * score_scale
    return grad_q.astype(bf16), grad_key, grad_value


def solution(mesh):
    fine = Mesh(mesh.devices.reshape(8, 2, 2, 4, 2, 2), AXES)
    tokens = P(AXES, None)

    return jax.shard_map(
        shards,
        mesh=fine,
        in_specs=(tokens,) * 6 + (P(), P(), P()),
        out_specs=(tokens,) * 3,
        check_vma=False,
    )
```

time: 89 us -> 102 us (1.15)
  waiting for transfers between devices: 16.9 us -> 34.8 us
  other arithmetic: 10.2 us -> 8.26 us
  Pallas kernels: 17.5 us -> 16.2 us
    ppermute x6, waiting for transfers between devices: 8 us -> 26 us  [along_z(): lax.ppermute(value, ('zlo', 'zhl'), [(i, i ^ mask) for i in range(NZ)])]
    pallas_call x3 -> x5, Pallas kernels: 17.3 us -> 16 us  [the longest x3 14.4 us: tile(): pl.pallas_call(body, in_specs=[smem] * 2 + [vmem] * len(arrays), out_spec...]
    ppermute x2, waiting for transfers between devices: 1.32 us -> 0.01 us  [other_core(): return lax.ppermute(value, 'core', [(0, 1), (1, 0)])]
    all_to_all x2, waiting for transfers between devices: 7.56 us -> 8.77 us  [over_y(): return lax.all_to_all(value, 'y', 0, 0)]
    unnamed x16 -> x20, local copies, waits for them, and re-layouts: 1.64 us -> 2.79 us
  transfers between devices with their start and end apart: 10 -> 10, of which waited for: 3 -> 5; matrix products, arithmetic and copies ran while one was open for 11% -> 9% of each run, Pallas kernels for 14% -> 8%
where the time goes in v4:
time: 102 us; the launch traced here: 101 us
  starting transfers between devices  37 us (36%)
  waiting for transfers between devices  34.8 us (34%)
  Pallas kernels  16.2 us (16%)
  other arithmetic  8.26 us (8%)
  local copies, waits for them, and re-layouts  4.19 us (4%)
    ppermute x6, waiting for transfers between devices, along_z(): lax.ppermute(value, ('zlo', 'zhl'), [(i, i ^ mask) for i in range(NZ)])  26 us
    ppermute x6, starting transfers between devices, along_z(): lax.ppermute(value, ('zlo', 'zhl'), [(i, i ^ mask) for i in range(NZ)])  22.4 us
    pallas_call x3, Pallas kernels, tile(): pl.pallas_call(body, in_specs=[smem] * 2 + [vmem] * len(arrays), out_spec...  14.4 us
    all_to_all x2, starting transfers between devices, over_y(): return lax.all_to_all(value, 'y', 0, 0)  10.7 us
    all_to_all x2, waiting for transfers between devices, over_y(): return lax.all_to_all(value, 'y', 0, 0)  8.77 us
    eq x2, other arithmetic, tables_of(): b == 1  5.61 us
    ppermute x2, starting transfers between devices, other_core(): return lax.ppermute(value, 'core', [(0, 1), (1, 0)])  3.83 us
    unnamed x20, local copies, waits for them, and re-layouts  2.79 us
  transfers between devices with their start and end apart: 10, of which 5 were waited for; matrix products, arithmetic and copies ran while one was open for 9% of the time, Pallas kernels for 8%

profile of v4, /device:TPU:6, one launch (start us, length us, event | category | flops | bytes accessed | tf_op | source)
XLA Modules:
  0.0 101.3 jit_solution(4817447633796475953)
XLA Ops:
  0.6 0.7 copy-done.3
  1.4 0.8 copy-done.4
  2.1 0.9 copies.1
  3.0 7.2 %all-to-all-start = ((bf16[8,128,256]{2,1,0:T(8,128)(2,1)}), bf16[8,128,256]{2,1,0:T(8,128)(2,1)S(1)}, u32[]{:S(2)}, u32[]{:S(2)}) async-start(bf16[8,128,256]{2,1,0:T(8,128)(2,1)} %copies.1), calls=%async_computation | async-start | bytes 1048576 | tf_op jit(solution)/shard_map/all_to_all | solution.py:254
  10.3 0.0 copy-start.9
  10.3 0.6 copy-done.9
  10.9 0.1 iota_compare_fusion.1
  11.1 0.1 select_reduce_fusion
  11.2 0.1 shift_right_arithmetic.40
  11.3 0.1 shift_right_arithmetic.39
  11.3 0.6 copy-done.8
  11.9 0.6 fusion.3
  12.6 0.0 copy-start
  12.6 1.9 %select_compare_fusion.2 = (pred[4,128]{1,0:T(4,128)(4,1)S(1)}, pred[4,128]{1,0:T(4,128)(4,1)S(1)}, pred[4,128]{1,0:T(4,128)(4,1)S(1)}) fusion(s32[]{:T(128)} %bitcast.9, s32[]{:T(128)} %bitcast.8, s32[]{:T(128)} %bitcast.7, s32[4,128]{1,0:T(4,128)S(1)} %select_reduce_fusion), kind=kLoop, calls=%fused_computation.19 | loop fusion | flops 3072 | bytes 3596 | tf_op jit(solution)/shard_map/eq | solution.py:233
  14.6 3.7 %select_compare_fusion.1 = (pred[4,128]{1,0:T(4,128)(4,1)S(1)}, pred[4,128]{1,0:T(4,128)(4,1)S(1)}) fusion(pred[4,128]{1,0:T(4,128)(4,1)S(1)} %get-tuple-element.41, pred[4,128]{1,0:T(4,128)(4,1)S(1)} %get-tuple-element.40, s32[]{:T(128)} %bitcast.12, s32[]{:T(128)} %bitcast.11, s32[]{:T(128)} %bitcast.10, s32[]{:T(128)} %bitcast.15, s32[]{:T(128)} %bitcast.14, ...), kind=kLoop, calls=%fused_computation.18 | loop fusion | flops 3072 | bytes 2072 | tf_op jit(solution)/shard_map/eq | solution.py:233
  18.3 0.1 reshape.274
  18.3 0.1 reshape.273
  18.4 0.1 reshape.275
  18.5 0.1 stack.21
  18.6 0.1 stack.20
  18.7 0.1 fusion.1
  18.8 0.2 convert_reduce_fusion
  19.0 0.1 reshape.264.refs_0_
  19.1 0.1 reduce_max.9
  19.2 0.2 convert_reduce_fusion.1
  19.4 0.1 reshape.265.refs_1_
  19.5 0.1 add_add_fusion.refs_6_.refs_8_
  19.6 8.1 %all-to-all-done = bf16[8,128,256]{2,1,0:T(8,128)(2,1)S(1)} async-done(((bf16[8,128,256]{2,1,0:T(8,128)(2,1)}), bf16[8,128,256]{2,1,0:T(8,128)(2,1)S(1)}, u32[]{:S(2)}, u32[]{:S(2)}) %all-to-all-start) | async-done | bytes 524320 | tf_op jit(solution)/shard_map/all_to_all | solution.py:254
  27.7 1.9 %collective-permute-start.3 = (bf16[1024,256]{1,0:T(8,128)(2,1)S(1)}, bf16[1024,256]{1,0:T(8,128)(2,1)S(1)}, u32[]{:S(2)}, u32[]{:S(2)}) collective-permute-start(bf16[1024,256]{1,0:T(8,128)(2,1)S(1)} %bitcast.27), channel_id=1, source_target_pairs={{0,16},{16,0},{1,17},{17,1},{2,18},{18,2},{3,19},{19,3},{4,20},{20... | collective-permute-start | bytes 1572872 | tf_op jit(solution)/shard_map/ppermute | solution.py:251
  29.7 0.2 pack.1.refs_2_
  29.9 4.3 %collective-permute-start = (bf16[136,1024]{1,0:T(8,128)(2,1)S(1)}, bf16[136,1024]{1,0:T(8,128)(2,1)S(1)}, u32[]{:S(2)}, u32[]{:S(2)}) collective-permute-start(bf16[136,1024]{1,0:T(8,128)(2,1)S(1)} %pack.1.refs_2_), channel_id=1, source_target_pairs={{0,32},{1,33},{32,0},{33,1},{2,34},{3,35},{34,2},{35,3},{4,36},{5,... | collective-permute-start | bytes 835592 | tf_op jit(solution)/shard_map/ppermute | solution.py:248
  34.2 5.5 %collective-permute-start.2 = (bf16[136,1024]{1,0:T(8,128)(2,1)S(1)}, bf16[136,1024]{1,0:T(8,128)(2,1)S(1)}, u32[]{:S(2)}, u32[]{:S(2)}) collective-permute-start(bf16[136,1024]{1,0:T(8,128)(2,1)S(1)} %pack.1.refs_2_), channel_id=1, source_target_pairs={{0,33},{1,32},{32,1},{33,0},{2,35},{3,34},{34,3},{35,2},{4,37},{5,... | collective-permute-start | bytes 835592 | tf_op jit(solution)/shard_map/ppermute | solution.py:248
  39.7 2.5 %collective-permute-start.1 = (bf16[136,1024]{1,0:T(8,128)(2,1)S(1)}, bf16[136,1024]{1,0:T(8,128)(2,1)S(1)}, u32[]{:S(2)}, u32[]{:S(2)}) collective-permute-start(bf16[136,1024]{1,0:T(8,128)(2,1)S(1)} %pack.1.refs_2_), channel_id=1, source_target_pairs={{0,1},{1,0},{32,33},{33,32},{2,3},{3,2},{34,35},{35,34},{4,5},{5,4... | collective-permute-start | bytes 835592 | tf_op jit(solution)/shard_map/ppermute | solution.py:248
  42.2 3.8 %shard_map.121 = (f32[4,128,256]{2,1,0:T(8,128)S(1)}, f32[1024,256]{1,0:T(8,128)S(1)}) custom-call(s32[32]{0:T(128)S(1)} %reshape.264.refs_0_, s32[16]{0:T(128)S(1)} %reshape.265.refs_1_, bf16[136,1024]{1,0:T(8,128)(2,1)S(1)} %pack.1.refs_2_, bf16[136,1024]{1,0:T(8,128)(2,1)S(1)} %collective-permute-done.refs_3_, bf16[1024,256]{1,0:T(8,128)(2,1)S(1)} %bitcast.28, ...), custom_call_target="tpu_custom_call" | custom-call | tf_op jit(solution)/shard_map/pallas_call | solution.py:193
  46.0 5.3 %collective-permute-done.2.refs_5_.refs_3_ = bf16[136,1024]{1,0:T(8,128)(2,1)S(1)} collective-permute-done((bf16[136,1024]{1,0:T(8,128)(2,1)S(1)}, bf16[136,1024]{1,0:T(8,128)(2,1)S(1)}, u32[]{:S(2)}, u32[]{:S(2)}) %collective-permute-start.2) | collective-permute-done | bytes 278560 | tf_op jit(solution)/shard_map/ppermute | solution.py:248
  51.4 13.8 %collective-permute-done.1.refs_4_.refs_2_ = bf16[136,1024]{1,0:T(8,128)(2,1)S(1)} collective-permute-done((bf16[136,1024]{1,0:T(8,128)(2,1)S(1)}, bf16[136,1024]{1,0:T(8,128)(2,1)S(1)}, u32[]{:S(2)}, u32[]{:S(2)}) %collective-permute-start.1) | collective-permute-done | bytes 278560 | tf_op jit(solution)/shard_map/ppermute | solution.py:248
  65.2 6.7 %shard_map.122 = (f32[128,512]{1,0:T(8,128)S(1)}, bf16[128,512]{1,0:T(8,128)(2,1)S(1)}, f32[4,128,256]{2,1,0:T(8,128)S(1)}, bf16[1024,256]{1,0:T(8,128)(2,1)S(1)}) custom-call(s32[32]{0:T(128)S(1)} %reshape.264.refs_0_, s32[16]{0:T(128)S(1)} %reshape.265.refs_1_, bf16[136,1024]{1,0:T(8,128)(2,1)S(1)} %pack.1.refs_2_, ...), custom_call_target="tpu_custom_call" | custom-call | tf_op jit(solution)/shard_map/pallas_call | solution.py:193
  71.9 1.9 %collective-permute-start.7 = (bf16[1024,256]{1,0:T(8,128)(2,1)S(1)}, bf16[1024,256]{1,0:T(8,128)(2,1)S(1)}, u32[]{:S(2)}, u32[]{:S(2)}) collective-permute-start(bf16[1024,256]{1,0:T(8,128)(2,1)S(1)} %get-tuple-element.36), channel_id=1, source_target_pairs={{0,16},{16,0},{1,17},{17,1},{2,18},{18,2},{3,19},{19,3},{4,20},{20... | collective-permute-start | bytes 1572872 | tf_op jit(solution)/shard_map/ppermute | solution.py:251
  73.8 3.9 %shard_map.123 = (bf16[128,512]{1,0:T(8,128)(2,1)S(1)}, bf16[128,512]{1,0:T(8,128)(2,1)S(1)}, f32[1024,256]{1,0:T(8,128)S(1)}) custom-call(s32[32]{0:T(128)S(1)} %reshape.264.refs_0_, s32[16]{0:T(128)S(1)} %reshape.265.refs_1_, bf16[136,1024]{1,0:T(8,128)(2,1)S(1)} %collective-permute-done.1.refs_4_.refs_2_, ...), custom_call_target="tpu_custom_call" | custom-call | tf_op jit(solution)/shard_map/pallas_call | solution.py:193
  77.8 0.9 add_convert_fusion
  78.7 3.5 %all-to-all-start.1 = ((bf16[8,128,256]{2,1,0:T(8,128)(2,1)}), bf16[8,128,256]{2,1,0:T(8,128)(2,1)S(1)}, u32[]{:S(2)}, u32[]{:S(2)}) async-start(bf16[8,128,256]{2,1,0:T(8,128)(2,1)} %bitcast.17), calls=%async_computation.1 | async-start | bytes 1048576 | tf_op jit(solution)/shard_map/all_to_all | solution.py:254
  82.2 1.9 %collective-permute-start.4 = (bf16[128,512]{1,0:T(8,128)(2,1)S(1)}, bf16[128,512]{1,0:T(8,128)(2,1)S(1)}, u32[]{:S(2)}, u32[]{:S(2)}) collective-permute-start(bf16[128,512]{1,0:T(8,128)(2,1)S(1)} %get-tuple-element.30), channel_id=1, source_target_pairs={{0,32},{1,33},{32,0},{33,1},{2,34},{3,35},{34,2},{35,3},{4,36},{5,... | collective-permute-start | bytes 393224 | tf_op jit(solution)/shard_map/ppermute | solution.py:248
  84.1 5.1 %collective-permute-start.5 = (bf16[128,512]{1,0:T(8,128)(2,1)S(1)}, bf16[128,512]{1,0:T(8,128)(2,1)S(1)}, u32[]{:S(2)}, u32[]{:S(2)}) collective-permute-start(bf16[128,512]{1,0:T(8,128)(2,1)S(1)} %get-tuple-element.33), channel_id=1, source_target_pairs={{0,1},{1,0},{32,33},{33,32},{2,3},{3,2},{34,35},{35,34},{4,5},{5,4... | collective-permute-start | bytes 393224 | tf_op jit(solution)/shard_map/ppermute | solution.py:248
  89.2 3.1 %collective-permute-start.6 = (bf16[128,512]{1,0:T(8,128)(2,1)S(1)}, bf16[128,512]{1,0:T(8,128)(2,1)S(1)}, u32[]{:S(2)}, u32[]{:S(2)}) collective-permute-start(bf16[128,512]{1,0:T(8,128)(2,1)S(1)} %get-tuple-element.34), channel_id=1, source_target_pairs={{0,33},{1,32},{32,1},{33,0},{2,35},{3,34},{34,3},{35,2},{4,37},{5,... | collective-permute-start | bytes 393224 | tf_op jit(solution)/shard_map/ppermute | solution.py:248
  92.3 6.8 %collective-permute-done.5 = bf16[128,512]{1,0:T(8,128)(2,1)S(1)} collective-permute-done((bf16[128,512]{1,0:T(8,128)(2,1)S(1)}, bf16[128,512]{1,0:T(8,128)(2,1)S(1)}, u32[]{:S(2)}, u32[]{:S(2)}) %collective-permute-start.5) | collective-permute-done | bytes 131104 | tf_op jit(solution)/shard_map/ppermute | solution.py:248
  99.2 0.7 multiply_convert_fusion
  99.9 0.7 all-to-all-done.1.parts
  100.6 0.7 finish.1
  (31 shorter events, 0.2 us)
Async XLA Ops:
  0.6 0.8 copy-start.3
  1.4 0.8 copy-start.4
  3.0 8.0 %copy-start.6 = (s32[65536]{0:T(1024)S(1)}, s32[65536]{0:T(1024)}, u32[]{:S(2)}) copy-start(s32[65536]{0:T(1024)} %param.17) | copy-start | bytes 786436
  3.0 8.0 %copy-start.7 = (s32[65536]{0:T(1024)S(1)}, s32[65536]{0:T(1024)}, u32[]{:S(2)}) copy-start(s32[65536]{0:T(1024)} %param.16) | copy-start | bytes 786436
  3.0 24.7 %all-to-all-start = ((bf16[8,128,256]{2,1,0:T(8,128)(2,1)}), bf16[8,128,256]{2,1,0:T(8,128)(2,1)S(1)}, u32[]{:S(2)}, u32[]{:S(2)}) async-start(bf16[8,128,256]{2,1,0:T(8,128)(2,1)} %copies.1), calls=%async_computation | async-start | bytes 1048576 | tf_op jit(solution)/shard_map/all_to_all | solution.py:254
  10.3 0.7 copy-start.9
  11.0 18.7 %copy-start.2 = (bf16[128,512]{1,0:T(8,128)(2,1)S(1)}, bf16[128,512]{1,0:T(8,128)(2,1)}, u32[]{:S(2)}) copy-start(bf16[128,512]{1,0:T(8,128)(2,1)} %o_ref.1) | copy-start | bytes 393220
  11.3 0.7 copy-start.8
  12.6 17.1 %copy-start.5 = (f32[128,4]{0,1:T(4,128)S(1)}, f32[128,4]{0,1:T(4,128)}, u32[]{:S(2)}) copy-start(f32[128,4]{0,1:T(4,128)} %param.15) | copy-start | bytes 6148
  12.6 17.1 %copy-start = (bf16[128,512]{1,0:T(8,128)(2,1)S(1)}, bf16[128,512]{1,0:T(8,128)(2,1)}, u32[]{:S(2)}) copy-start(bf16[128,512]{1,0:T(8,128)(2,1)} %q_ref) | copy-start | bytes 393220
  12.6 17.1 %copy-start.1 = (bf16[128,512]{1,0:T(8,128)(2,1)S(1)}, bf16[128,512]{1,0:T(8,128)(2,1)}, u32[]{:S(2)}) copy-start(bf16[128,512]{1,0:T(8,128)(2,1)} %d_ref.1) | copy-start | bytes 393220
  27.7 37.5 %collective-permute-start.3 = (bf16[1024,256]{1,0:T(8,128)(2,1)S(1)}, bf16[1024,256]{1,0:T(8,128)(2,1)S(1)}, u32[]{:S(2)}, u32[]{:S(2)}) collective-permute-start(bf16[1024,256]{1,0:T(8,128)(2,1)S(1)} %bitcast.27), channel_id=1, source_target_pairs={{0,16},{16,0},{1,17},{17,1},{2,18},{18,2},{3,19},{19,3},{4,20},{20... | collective-permute-start | bytes 1572872 | tf_op jit(solution)/shard_map/ppermute | solution.py:251
  29.9 12.3 %collective-permute-start = (bf16[136,1024]{1,0:T(8,128)(2,1)S(1)}, bf16[136,1024]{1,0:T(8,128)(2,1)S(1)}, u32[]{:S(2)}, u32[]{:S(2)}) collective-permute-start(bf16[136,1024]{1,0:T(8,128)(2,1)S(1)} %pack.1.refs_2_), channel_id=1, source_target_pairs={{0,32},{1,33},{32,0},{33,1},{2,34},{3,35},{34,2},{35,3},{4,36},{5,... | collective-permute-start | bytes 835592 | tf_op jit(solution)/shard_map/ppermute | solution.py:248
  34.2 17.2 %collective-permute-start.2 = (bf16[136,1024]{1,0:T(8,128)(2,1)S(1)}, bf16[136,1024]{1,0:T(8,128)(2,1)S(1)}, u32[]{:S(2)}, u32[]{:S(2)}) collective-permute-start(bf16[136,1024]{1,0:T(8,128)(2,1)S(1)} %pack.1.refs_2_), channel_id=1, source_target_pairs={{0,33},{1,32},{32,1},{33,0},{2,35},{3,34},{34,3},{35,2},{4,37},{5,... | collective-permute-start | bytes 835592 | tf_op jit(solution)/shard_map/ppermute | solution.py:248
  39.7 25.5 %collective-permute-start.1 = (bf16[136,1024]{1,0:T(8,128)(2,1)S(1)}, bf16[136,1024]{1,0:T(8,128)(2,1)S(1)}, u32[]{:S(2)}, u32[]{:S(2)}) collective-permute-start(bf16[136,1024]{1,0:T(8,128)(2,1)S(1)} %pack.1.refs_2_), channel_id=1, source_target_pairs={{0,1},{1,0},{32,33},{33,32},{2,3},{3,2},{34,35},{35,34},{4,5},{5,4... | collective-permute-start | bytes 835592 | tf_op jit(solution)/shard_map/ppermute | solution.py:248
  71.9 5.9 %collective-permute-start.7 = (bf16[1024,256]{1,0:T(8,128)(2,1)S(1)}, bf16[1024,256]{1,0:T(8,128)(2,1)S(1)}, u32[]{:S(2)}, u32[]{:S(2)}) collective-permute-start(bf16[1024,256]{1,0:T(8,128)(2,1)S(1)} %get-tuple-element.36), channel_id=1, source_target_pairs={{0,16},{16,0},{1,17},{17,1},{2,18},{18,2},{3,19},{19,3},{4,20},{20... | collective-permute-start | bytes 1572872 | tf_op jit(solution)/shard_map/ppermute | solution.py:251
  78.7 21.9 %all-to-all-start.1 = ((bf16[8,128,256]{2,1,0:T(8,128)(2,1)}), bf16[8,128,256]{2,1,0:T(8,128)(2,1)S(1)}, u32[]{:S(2)}, u32[]{:S(2)}) async-start(bf16[8,128,256]{2,1,0:T(8,128)(2,1)} %bitcast.17), calls=%async_computation.1 | async-start | bytes 1048576 | tf_op jit(solution)/shard_map/all_to_all | solution.py:254
  82.2 10.1 %collective-permute-start.4 = (bf16[128,512]{1,0:T(8,128)(2,1)S(1)}, bf16[128,512]{1,0:T(8,128)(2,1)S(1)}, u32[]{:S(2)}, u32[]{:S(2)}) collective-permute-start(bf16[128,512]{1,0:T(8,128)(2,1)S(1)} %get-tuple-element.30), channel_id=1, source_target_pairs={{0,32},{1,33},{32,0},{33,1},{2,34},{3,35},{34,2},{35,3},{4,36},{5,... | collective-permute-start | bytes 393224 | tf_op jit(solution)/shard_map/ppermute | solution.py:248
  84.1 15.1 %collective-permute-start.5 = (bf16[128,512]{1,0:T(8,128)(2,1)S(1)}, bf16[128,512]{1,0:T(8,128)(2,1)S(1)}, u32[]{:S(2)}, u32[]{:S(2)}) collective-permute-start(bf16[128,512]{1,0:T(8,128)(2,1)S(1)} %get-tuple-element.33), channel_id=1, source_target_pairs={{0,1},{1,0},{32,33},{33,32},{2,3},{3,2},{34,35},{35,34},{4,5},{5,4... | collective-permute-start | bytes 393224 | tf_op jit(solution)/shard_map/ppermute | solution.py:248
  89.2 10.0 %collective-permute-start.6 = (bf16[128,512]{1,0:T(8,128)(2,1)S(1)}, bf16[128,512]{1,0:T(8,128)(2,1)S(1)}, u32[]{:S(2)}, u32[]{:S(2)}) collective-permute-start(bf16[128,512]{1,0:T(8,128)(2,1)S(1)} %get-tuple-element.34), channel_id=1, source_target_pairs={{0,33},{1,32},{32,1},{33,0},{2,35},{3,34},{34,3},{35,2},{4,37},{5,... | collective-permute-start | bytes 393224 | tf_op jit(solution)/shard_map/ppermute | solution.py:248

commit v5 on v4

--- a/solution.py
+++ b/solution.py
@@ -206,10 +206,16 @@
     value_ref[...] = total[:, DIM:].astype(bf16)
 
 
-def copies_kernel(key_ref, value_ref, out):
+def copies_kernel(key_ref, value_ref, out, sems):
+    moves = []
     for i in range(NY):
-        out[i, :, :DIM] = key_ref[...]
-        out[i, :, DIM:] = value_ref[...]
+        for j, ref in enumerate((key_ref, value_ref)):
+            half = out.at[i, :, j * DIM : (j + 1) * DIM]
+            moves.append(pltpu.make_async_copy(ref, half, sems.at[2 * i + j]))
+    for move in moves:
+        move.start()
+    for move in moves:
+        move.wait()
 
 
 def plan(position, modality, table):
@@ -256,6 +262,9 @@
     copies = pl.pallas_call(
         copies_kernel,
         out_shape=jax.ShapeDtypeStruct((NY, TOK, 2 * DIM), bf16),
+        in_specs=[pl.BlockSpec(memory_space=pltpu.HBM)] * 2,
+        out_specs=pl.BlockSpec(memory_space=pltpu.HBM),
+        scratch_shapes=[pltpu.SemaphoreType.DMA((2 * NY,))],
         compiler_params=pltpu.CompilerParams(vmem_limit_bytes=8 << 20),
         name="copies",
     )(key_states, value_states)

time: 102 us -> 102 us (level)
  no operation moved by 1% of the time
where the time goes in v5:
time: 102 us; the launch traced here: 101 us
  starting transfers between devices  37 us (36%)
  waiting for transfers between devices  34.8 us (34%)
  Pallas kernels  16.3 us (16%)
  other arithmetic  8.26 us (8%)
  local copies, waits for them, and re-layouts  4.19 us (4%)
    ppermute x6, waiting for transfers between devices, along_z(): lax.ppermute(value, ('zlo', 'zhl'), [(i, i ^ mask) for i in range(NZ)])  26 us
    ppermute x6, starting transfers between devices, along_z(): lax.ppermute(value, ('zlo', 'zhl'), [(i, i ^ mask) for i in range(NZ)])  22.4 us
    pallas_call x3, Pallas kernels, tile(): pl.pallas_call(body, in_specs=[smem] * 2 + [vmem] * len(arrays), out_spec...  14.4 us
    all_to_all x2, starting transfers between devices, over_y(): return lax.all_to_all(value, 'y', 0, 0)  10.7 us
    all_to_all x2, waiting for transfers between devices, over_y(): return lax.all_to_all(value, 'y', 0, 0)  8.77 us
    eq x2, other arithmetic, tables_of(): b == 1  5.61 us
    ppermute x2, starting transfers between devices, other_core(): return lax.ppermute(value, 'core', [(0, 1), (1, 0)])  3.83 us
    unnamed x20, local copies, waits for them, and re-layouts  2.79 us
  transfers between devices with their start and end apart: 10, of which 5 were waited for; matrix products, arithmetic and copies ran while one was open for 9% of the time, Pallas kernels for 8%

profile of v5, /device:TPU:6, one launch (start us, length us, event | category | flops | bytes accessed | tf_op | source)
XLA Modules:
  0.0 101.4 jit_solution(10658088026167952790)
XLA Ops:
  0.6 0.7 copy-done.3
  1.4 0.8 copy-done.4
  2.1 0.9 copies.1
  3.1 0.0 copy-start.6
  3.1 7.2 %all-to-all-start = ((bf16[8,128,256]{2,1,0:T(8,128)(2,1)}), bf16[8,128,256]{2,1,0:T(8,128)(2,1)S(1)}, u32[]{:S(2)}, u32[]{:S(2)}) async-start(bf16[8,128,256]{2,1,0:T(8,128)(2,1)} %copies.1), calls=%async_computation | async-start | bytes 1048576 | tf_op jit(solution)/shard_map/all_to_all | solution.py:260
  10.4 0.0 copy-start.9
  10.4 0.6 copy-done.9
  11.0 0.1 iota_compare_fusion.1
  11.2 0.1 select_reduce_fusion
  11.3 0.1 shift_right_arithmetic.40
  11.4 0.1 shift_right_arithmetic.39
  11.4 0.6 copy-done.8
  12.1 0.6 fusion.3
  12.7 1.9 %select_compare_fusion.2 = (pred[4,128]{1,0:T(4,128)(4,1)S(1)}, pred[4,128]{1,0:T(4,128)(4,1)S(1)}, pred[4,128]{1,0:T(4,128)(4,1)S(1)}) fusion(s32[]{:T(128)} %bitcast.9, s32[]{:T(128)} %bitcast.8, s32[]{:T(128)} %bitcast.7, s32[4,128]{1,0:T(4,128)S(1)} %select_reduce_fusion), kind=kLoop, calls=%fused_computation.19 | loop fusion | flops 3072 | bytes 3596 | tf_op jit(solution)/shard_map/eq | solution.py:239
  14.7 3.7 %select_compare_fusion.1 = (pred[4,128]{1,0:T(4,128)(4,1)S(1)}, pred[4,128]{1,0:T(4,128)(4,1)S(1)}) fusion(pred[4,128]{1,0:T(4,128)(4,1)S(1)} %get-tuple-element.41, pred[4,128]{1,0:T(4,128)(4,1)S(1)} %get-tuple-element.40, s32[]{:T(128)} %bitcast.12, s32[]{:T(128)} %bitcast.11, s32[]{:T(128)} %bitcast.10, s32[]{:T(128)} %bitcast.15, s32[]{:T(128)} %bitcast.14, ...), kind=kLoop, calls=%fused_computation.18 | loop fusion | flops 3072 | bytes 2072 | tf_op jit(solution)/shard_map/eq | solution.py:239
  18.4 0.1 reshape.274
  18.5 0.1 reshape.273
  18.5 0.1 reshape.275
  18.6 0.1 stack.21
  18.7 0.1 stack.20
  18.8 0.1 fusion.1
  18.9 0.2 convert_reduce_fusion
  19.1 0.1 reshape.264.refs_0_
  19.2 0.1 reduce_max.9
  19.3 0.2 convert_reduce_fusion.1
  19.5 0.1 reshape.265.refs_1_
  19.6 0.1 add_add_fusion.refs_6_.refs_8_
  19.8 8.1 %all-to-all-done = bf16[8,128,256]{2,1,0:T(8,128)(2,1)S(1)} async-done(((bf16[8,128,256]{2,1,0:T(8,128)(2,1)}), bf16[8,128,256]{2,1,0:T(8,128)(2,1)S(1)}, u32[]{:S(2)}, u32[]{:S(2)}) %all-to-all-start) | async-done | bytes 524320 | tf_op jit(solution)/shard_map/all_to_all | solution.py:260
  27.9 1.9 %collective-permute-start.3 = (bf16[1024,256]{1,0:T(8,128)(2,1)S(1)}, bf16[1024,256]{1,0:T(8,128)(2,1)S(1)}, u32[]{:S(2)}, u32[]{:S(2)}) collective-permute-start(bf16[1024,256]{1,0:T(8,128)(2,1)S(1)} %bitcast.27), channel_id=1, source_target_pairs={{0,16},{16,0},{1,17},{17,1},{2,18},{18,2},{3,19},{19,3},{4,20},{20... | collective-permute-start | bytes 1572872 | tf_op jit(solution)/shard_map/ppermute | solution.py:257
  29.8 0.2 pack.1.refs_2_
  30.0 4.3 %collective-permute-start = (bf16[136,1024]{1,0:T(8,128)(2,1)S(1)}, bf16[136,1024]{1,0:T(8,128)(2,1)S(1)}, u32[]{:S(2)}, u32[]{:S(2)}) collective-permute-start(bf16[136,1024]{1,0:T(8,128)(2,1)S(1)} %pack.1.refs_2_), channel_id=1, source_target_pairs={{0,32},{1,33},{32,0},{33,1},{2,34},{3,35},{34,2},{35,3},{4,36},{5,... | collective-permute-start | bytes 835592 | tf_op jit(solution)/shard_map/ppermute | solution.py:254
  34.3 5.5 %collective-permute-start.2 = (bf16[136,1024]{1,0:T(8,128)(2,1)S(1)}, bf16[136,1024]{1,0:T(8,128)(2,1)S(1)}, u32[]{:S(2)}, u32[]{:S(2)}) collective-permute-start(bf16[136,1024]{1,0:T(8,128)(2,1)S(1)} %pack.1.refs_2_), channel_id=1, source_target_pairs={{0,33},{1,32},{32,1},{33,0},{2,35},{3,34},{34,3},{35,2},{4,37},{5,... | collective-permute-start | bytes 835592 | tf_op jit(solution)/shard_map/ppermute | solution.py:254
  39.8 2.5 %collective-permute-start.1 = (bf16[136,1024]{1,0:T(8,128)(2,1)S(1)}, bf16[136,1024]{1,0:T(8,128)(2,1)S(1)}, u32[]{:S(2)}, u32[]{:S(2)}) collective-permute-start(bf16[136,1024]{1,0:T(8,128)(2,1)S(1)} %pack.1.refs_2_), channel_id=1, source_target_pairs={{0,1},{1,0},{32,33},{33,32},{2,3},{3,2},{34,35},{35,34},{4,5},{5,4... | collective-permute-start | bytes 835592 | tf_op jit(solution)/shard_map/ppermute | solution.py:254
  42.3 3.8 %shard_map.121 = (f32[4,128,256]{2,1,0:T(8,128)S(1)}, f32[1024,256]{1,0:T(8,128)S(1)}) custom-call(s32[32]{0:T(128)S(1)} %reshape.264.refs_0_, s32[16]{0:T(128)S(1)} %reshape.265.refs_1_, bf16[136,1024]{1,0:T(8,128)(2,1)S(1)} %pack.1.refs_2_, bf16[136,1024]{1,0:T(8,128)(2,1)S(1)} %collective-permute-done.refs_3_, bf16[1024,256]{1,0:T(8,128)(2,1)S(1)} %bitcast.28, ...), custom_call_target="tpu_custom_call" | custom-call | tf_op jit(solution)/shard_map/pallas_call | solution.py:193
  46.1 5.3 %collective-permute-done.2.refs_5_.refs_3_ = bf16[136,1024]{1,0:T(8,128)(2,1)S(1)} collective-permute-done((bf16[136,1024]{1,0:T(8,128)(2,1)S(1)}, bf16[136,1024]{1,0:T(8,128)(2,1)S(1)}, u32[]{:S(2)}, u32[]{:S(2)}) %collective-permute-start.2) | collective-permute-done | bytes 278560 | tf_op jit(solution)/shard_map/ppermute | solution.py:254
  51.5 13.8 %collective-permute-done.1.refs_4_.refs_2_ = bf16[136,1024]{1,0:T(8,128)(2,1)S(1)} collective-permute-done((bf16[136,1024]{1,0:T(8,128)(2,1)S(1)}, bf16[136,1024]{1,0:T(8,128)(2,1)S(1)}, u32[]{:S(2)}, u32[]{:S(2)}) %collective-permute-start.1) | collective-permute-done | bytes 278560 | tf_op jit(solution)/shard_map/ppermute | solution.py:254
  65.3 6.7 %shard_map.122 = (f32[128,512]{1,0:T(8,128)S(1)}, bf16[128,512]{1,0:T(8,128)(2,1)S(1)}, f32[4,128,256]{2,1,0:T(8,128)S(1)}, bf16[1024,256]{1,0:T(8,128)(2,1)S(1)}) custom-call(s32[32]{0:T(128)S(1)} %reshape.264.refs_0_, s32[16]{0:T(128)S(1)} %reshape.265.refs_1_, bf16[136,1024]{1,0:T(8,128)(2,1)S(1)} %pack.1.refs_2_, ...), custom_call_target="tpu_custom_call" | custom-call | tf_op jit(solution)/shard_map/pallas_call | solution.py:193
  72.0 1.9 %collective-permute-start.7 = (bf16[1024,256]{1,0:T(8,128)(2,1)S(1)}, bf16[1024,256]{1,0:T(8,128)(2,1)S(1)}, u32[]{:S(2)}, u32[]{:S(2)}) collective-permute-start(bf16[1024,256]{1,0:T(8,128)(2,1)S(1)} %get-tuple-element.36), channel_id=1, source_target_pairs={{0,16},{16,0},{1,17},{17,1},{2,18},{18,2},{3,19},{19,3},{4,20},{20... | collective-permute-start | bytes 1572872 | tf_op jit(solution)/shard_map/ppermute | solution.py:257
  74.0 3.9 %shard_map.123 = (bf16[128,512]{1,0:T(8,128)(2,1)S(1)}, bf16[128,512]{1,0:T(8,128)(2,1)S(1)}, f32[1024,256]{1,0:T(8,128)S(1)}) custom-call(s32[32]{0:T(128)S(1)} %reshape.264.refs_0_, s32[16]{0:T(128)S(1)} %reshape.265.refs_1_, bf16[136,1024]{1,0:T(8,128)(2,1)S(1)} %collective-permute-done.1.refs_4_.refs_2_, ...), custom_call_target="tpu_custom_call" | custom-call | tf_op jit(solution)/shard_map/pallas_call | solution.py:193
  77.9 0.9 add_convert_fusion
  78.8 3.5 %all-to-all-start.1 = ((bf16[8,128,256]{2,1,0:T(8,128)(2,1)}), bf16[8,128,256]{2,1,0:T(8,128)(2,1)S(1)}, u32[]{:S(2)}, u32[]{:S(2)}) async-start(bf16[8,128,256]{2,1,0:T(8,128)(2,1)} %bitcast.17), calls=%async_computation.1 | async-start | bytes 1048576 | tf_op jit(solution)/shard_map/all_to_all | solution.py:260
  82.3 1.9 %collective-permute-start.4 = (bf16[128,512]{1,0:T(8,128)(2,1)S(1)}, bf16[128,512]{1,0:T(8,128)(2,1)S(1)}, u32[]{:S(2)}, u32[]{:S(2)}) collective-permute-start(bf16[128,512]{1,0:T(8,128)(2,1)S(1)} %get-tuple-element.30), channel_id=1, source_target_pairs={{0,32},{1,33},{32,0},{33,1},{2,34},{3,35},{34,2},{35,3},{4,36},{5,... | collective-permute-start | bytes 393224 | tf_op jit(solution)/shard_map/ppermute | solution.py:254
  84.2 5.1 %collective-permute-start.5 = (bf16[128,512]{1,0:T(8,128)(2,1)S(1)}, bf16[128,512]{1,0:T(8,128)(2,1)S(1)}, u32[]{:S(2)}, u32[]{:S(2)}) collective-permute-start(bf16[128,512]{1,0:T(8,128)(2,1)S(1)} %get-tuple-element.33), channel_id=1, source_target_pairs={{0,1},{1,0},{32,33},{33,32},{2,3},{3,2},{34,35},{35,34},{4,5},{5,4... | collective-permute-start | bytes 393224 | tf_op jit(solution)/shard_map/ppermute | solution.py:254
  89.3 3.1 %collective-permute-start.6 = (bf16[128,512]{1,0:T(8,128)(2,1)S(1)}, bf16[128,512]{1,0:T(8,128)(2,1)S(1)}, u32[]{:S(2)}, u32[]{:S(2)}) collective-permute-start(bf16[128,512]{1,0:T(8,128)(2,1)S(1)} %get-tuple-element.34), channel_id=1, source_target_pairs={{0,33},{1,32},{32,1},{33,0},{2,35},{3,34},{34,3},{35,2},{4,37},{5,... | collective-permute-start | bytes 393224 | tf_op jit(solution)/shard_map/ppermute | solution.py:254
  92.5 6.8 %collective-permute-done.5 = bf16[128,512]{1,0:T(8,128)(2,1)S(1)} collective-permute-done((bf16[128,512]{1,0:T(8,128)(2,1)S(1)}, bf16[128,512]{1,0:T(8,128)(2,1)S(1)}, u32[]{:S(2)}, u32[]{:S(2)}) %collective-permute-start.5) | collective-permute-done | bytes 131104 | tf_op jit(solution)/shard_map/ppermute | solution.py:254
  99.3 0.7 multiply_convert_fusion
  100.0 0.7 all-to-all-done.1.parts
  100.7 0.7 finish.1
  (31 shorter events, 0.2 us)
Async XLA Ops:
  0.6 0.8 copy-start.3
  1.4 0.8 copy-start.4
  3.1 8.0 %copy-start.6 = (s32[65536]{0:T(1024)S(1)}, s32[65536]{0:T(1024)}, u32[]{:S(2)}) copy-start(s32[65536]{0:T(1024)} %param.17) | copy-start | bytes 786436
  3.1 8.0 %copy-start.7 = (s32[65536]{0:T(1024)S(1)}, s32[65536]{0:T(1024)}, u32[]{:S(2)}) copy-start(s32[65536]{0:T(1024)} %param.16) | copy-start | bytes 786436
  3.1 24.7 %all-to-all-start = ((bf16[8,128,256]{2,1,0:T(8,128)(2,1)}), bf16[8,128,256]{2,1,0:T(8,128)(2,1)S(1)}, u32[]{:S(2)}, u32[]{:S(2)}) async-start(bf16[8,128,256]{2,1,0:T(8,128)(2,1)} %copies.1), calls=%async_computation | async-start | bytes 1048576 | tf_op jit(solution)/shard_map/all_to_all | solution.py:260
  10.4 0.7 copy-start.9
  11.1 18.7 %copy-start.2 = (bf16[128,512]{1,0:T(8,128)(2,1)S(1)}, bf16[128,512]{1,0:T(8,128)(2,1)}, u32[]{:S(2)}) copy-start(bf16[128,512]{1,0:T(8,128)(2,1)} %o_ref.1) | copy-start | bytes 393220
  11.4 0.7 copy-start.8
  12.7 17.1 %copy-start.5 = (f32[128,4]{0,1:T(4,128)S(1)}, f32[128,4]{0,1:T(4,128)}, u32[]{:S(2)}) copy-start(f32[128,4]{0,1:T(4,128)} %param.15) | copy-start | bytes 6148
  12.7 17.1 %copy-start = (bf16[128,512]{1,0:T(8,128)(2,1)S(1)}, bf16[128,512]{1,0:T(8,128)(2,1)}, u32[]{:S(2)}) copy-start(bf16[128,512]{1,0:T(8,128)(2,1)} %q_ref) | copy-start | bytes 393220
  12.7 17.1 %copy-start.1 = (bf16[128,512]{1,0:T(8,128)(2,1)S(1)}, bf16[128,512]{1,0:T(8,128)(2,1)}, u32[]{:S(2)}) copy-start(bf16[128,512]{1,0:T(8,128)(2,1)} %d_ref.1) | copy-start | bytes 393220
  27.9 37.5 %collective-permute-start.3 = (bf16[1024,256]{1,0:T(8,128)(2,1)S(1)}, bf16[1024,256]{1,0:T(8,128)(2,1)S(1)}, u32[]{:S(2)}, u32[]{:S(2)}) collective-permute-start(bf16[1024,256]{1,0:T(8,128)(2,1)S(1)} %bitcast.27), channel_id=1, source_target_pairs={{0,16},{16,0},{1,17},{17,1},{2,18},{18,2},{3,19},{19,3},{4,20},{20... | collective-permute-start | bytes 1572872 | tf_op jit(solution)/shard_map/ppermute | solution.py:257
  30.0 12.3 %collective-permute-start = (bf16[136,1024]{1,0:T(8,128)(2,1)S(1)}, bf16[136,1024]{1,0:T(8,128)(2,1)S(1)}, u32[]{:S(2)}, u32[]{:S(2)}) collective-permute-start(bf16[136,1024]{1,0:T(8,128)(2,1)S(1)} %pack.1.refs_2_), channel_id=1, source_target_pairs={{0,32},{1,33},{32,0},{33,1},{2,34},{3,35},{34,2},{35,3},{4,36},{5,... | collective-permute-start | bytes 835592 | tf_op jit(solution)/shard_map/ppermute | solution.py:254
  34.3 17.2 %collective-permute-start.2 = (bf16[136,1024]{1,0:T(8,128)(2,1)S(1)}, bf16[136,1024]{1,0:T(8,128)(2,1)S(1)}, u32[]{:S(2)}, u32[]{:S(2)}) collective-permute-start(bf16[136,1024]{1,0:T(8,128)(2,1)S(1)} %pack.1.refs_2_), channel_id=1, source_target_pairs={{0,33},{1,32},{32,1},{33,0},{2,35},{3,34},{34,3},{35,2},{4,37},{5,... | collective-permute-start | bytes 835592 | tf_op jit(solution)/shard_map/ppermute | solution.py:254
  39.8 25.5 %collective-permute-start.1 = (bf16[136,1024]{1,0:T(8,128)(2,1)S(1)}, bf16[136,1024]{1,0:T(8,128)(2,1)S(1)}, u32[]{:S(2)}, u32[]{:S(2)}) collective-permute-start(bf16[136,1024]{1,0:T(8,128)(2,1)S(1)} %pack.1.refs_2_), channel_id=1, source_target_pairs={{0,1},{1,0},{32,33},{33,32},{2,3},{3,2},{34,35},{35,34},{4,5},{5,4... | collective-permute-start | bytes 835592 | tf_op jit(solution)/shard_map/ppermute | solution.py:254
  72.0 5.9 %collective-permute-start.7 = (bf16[1024,256]{1,0:T(8,128)(2,1)S(1)}, bf16[1024,256]{1,0:T(8,128)(2,1)S(1)}, u32[]{:S(2)}, u32[]{:S(2)}) collective-permute-start(bf16[1024,256]{1,0:T(8,128)(2,1)S(1)} %get-tuple-element.36), channel_id=1, source_target_pairs={{0,16},{16,0},{1,17},{17,1},{2,18},{18,2},{3,19},{19,3},{4,20},{20... | collective-permute-start | bytes 1572872 | tf_op jit(solution)/shard_map/ppermute | solution.py:257
  78.8 21.9 %all-to-all-start.1 = ((bf16[8,128,256]{2,1,0:T(8,128)(2,1)}), bf16[8,128,256]{2,1,0:T(8,128)(2,1)S(1)}, u32[]{:S(2)}, u32[]{:S(2)}) async-start(bf16[8,128,256]{2,1,0:T(8,128)(2,1)} %bitcast.17), calls=%async_computation.1 | async-start | bytes 1048576 | tf_op jit(solution)/shard_map/all_to_all | solution.py:260
  82.3 10.1 %collective-permute-start.4 = (bf16[128,512]{1,0:T(8,128)(2,1)S(1)}, bf16[128,512]{1,0:T(8,128)(2,1)S(1)}, u32[]{:S(2)}, u32[]{:S(2)}) collective-permute-start(bf16[128,512]{1,0:T(8,128)(2,1)S(1)} %get-tuple-element.30), channel_id=1, source_target_pairs={{0,32},{1,33},{32,0},{33,1},{2,34},{3,35},{34,2},{35,3},{4,36},{5,... | collective-permute-start | bytes 393224 | tf_op jit(solution)/shard_map/ppermute | solution.py:254
  84.2 15.1 %collective-permute-start.5 = (bf16[128,512]{1,0:T(8,128)(2,1)S(1)}, bf16[128,512]{1,0:T(8,128)(2,1)S(1)}, u32[]{:S(2)}, u32[]{:S(2)}) collective-permute-start(bf16[128,512]{1,0:T(8,128)(2,1)S(1)} %get-tuple-element.33), channel_id=1, source_target_pairs={{0,1},{1,0},{32,33},{33,32},{2,3},{3,2},{34,35},{35,34},{4,5},{5,4... | collective-permute-start | bytes 393224 | tf_op jit(solution)/shard_map/ppermute | solution.py:254
  89.3 10.0 %collective-permute-start.6 = (bf16[128,512]{1,0:T(8,128)(2,1)S(1)}, bf16[128,512]{1,0:T(8,128)(2,1)S(1)}, u32[]{:S(2)}, u32[]{:S(2)}) collective-permute-start(bf16[128,512]{1,0:T(8,128)(2,1)S(1)} %get-tuple-element.34), channel_id=1, source_target_pairs={{0,33},{1,32},{32,1},{33,0},{2,35},{3,34},{34,3},{35,2},{4,37},{5,... | collective-permute-start | bytes 393224 | tf_op jit(solution)/shard_map/ppermute | solution.py:254

commit v6 on v5

--- a/solution.py
+++ b/solution.py
@@ -59,7 +59,7 @@
         return [next(it) for _ in range(n)]
 
     start, count, s, finals, raws, old_units, has_acc, spread_out = cfg
-    rank, need = take(2)
+    tab = next(it)
     msgs = take(count)
     kv, kcode, qlim = take(3)
     oldq = next(it) if old_units else None
@@ -76,11 +76,11 @@
     for u in range(units):
         for c in range(chunks):
             work[filled] = c * units + u
-            active = c * GROUP < need[s * QUNITS + base + u]
+            active = c * GROUP < tab[2 * KUNITS + s * QUNITS + base + u, 0]
             filled = filled + active.astype(jnp.int32)
     rounds = (filled + PAR - 1) // PAR
     for a, m in enumerate(msgs):
-        meta = m[TOK : TOK + 8].astype(f32)
+        meta = m[TOK : TOK + 8, :].astype(f32)
         meta = meta[0:1] + meta[1:2] + meta[2:3]
         for half in range(2):
             u = 2 * a + half
@@ -101,10 +101,11 @@
         row = kcode[s * NY + b : s * NY + b + 1, :]
         wide = jnp.broadcast_to(row, (TOK, TOK)).T
         for half in range(2):
-            i = 2 * b + half
-            spot = pl.multiple_of(rank[s * KUNITS + i] * UNIT, UNIT)
-            spots.append(spot)
-            ks[pl.ds(spot, UNIT), :] = kv[i * UNIT : (i + 1) * UNIT, :]
+            i = half * NY + b
+            spot = pl.multiple_of(tab[s * KUNITS + i, 0] * UNIT, UNIT)
+            nat = slice(b * TOK + half * UNIT, b * TOK + (half + 1) * UNIT)
+            spots.append((nat, spot))
+            ks[pl.ds(spot, UNIT), :] = kv[nat, :]
             kc[pl.ds(spot, UNIT), :] = wide[half * UNIT : (half + 1) * UNIT]
     span = GROUP * UNIT
     for c in range(chunks):
@@ -142,8 +143,8 @@
 
     lax.fori_loop(0, rounds, body, 0)
     if spread_out:
-        for i, spot in enumerate(spots):
-            out[i * UNIT : (i + 1) * UNIT, :] = acc[pl.ds(spot, UNIT), :].astype(out.dtype)
+        for nat, spot in spots:
+            out[nat, :] = acc[pl.ds(spot, UNIT), :].astype(out.dtype)
     if rawq is not None:
         rawq[...] = gq[raws[0] : raws[1]]
     for (a, _), g in zip(finals, gqs):
@@ -159,7 +160,7 @@
     return pltpu.with_memory_space_constraint(value, pltpu.VMEM)
 
 
-def tile(tables, start, msgs, kv, kcode, qlim, s, finals=(), raws=None, oldq=None, old=None, out_type=None):
+def tile(tab, start, msgs, kv, kcode, qlim, s, finals=(), raws=None, oldq=None, old=None, out_type=None):
     count = len(msgs)
     units = 2 * count
     keys = KUNITS * UNIT
@@ -192,12 +193,12 @@
 
     return pl.pallas_call(
         body,
-        in_specs=[smem] * 2 + [vmem] * len(arrays),
+        in_specs=[smem] + [vmem] * len(arrays),
         out_specs=[vmem] * len(outs),
         out_shape=outs,
         scratch_shapes=scratch,
         compiler_params=pltpu.CompilerParams(vmem_limit_bytes=20 << 20),
-    )(*tables, *[in_vmem(v) for v in arrays])
+    )(tab, *[in_vmem(v) for v in arrays])
 
 
 def finish_kernel(parts, key_ref, value_ref):
@@ -206,47 +207,84 @@
     value_ref[...] = total[:, DIM:].astype(bf16)
 
 
-def copies_kernel(key_ref, value_ref, out, sems):
+def unit_low(value, fold, fill):
+    lane = lax.broadcasted_iota(jnp.int32, value.shape, 1)
+    first = fold(jnp.where(lane < UNIT, value, fill), axis=1, keepdims=True)
+    second = fold(jnp.where(lane < UNIT, fill, value), axis=1, keepdims=True)
+    return first, second
+
+
+def plan_kernel(table, position, modality, tab, kcode, qlim, rows, sems):
+    y, zlo, core, x, zhh, zhl = (lax.axis_index(a) for a in AXES)
+
+    def line(y, zlo, core, zhl):
+        return ((((y * 2 + zlo) * 2 + core) * 4 + x) * 2 + zhh) * 2 + zhl
+
+    lines = [line(b, zlo, core ^ s, zhl) for s in range(2) for b in range(NY)]
+    lines += [line(y, zlo ^ (mask >> 1), core, zhl ^ (mask & 1)) for mask in MASKS]
     moves = []
-    for i in range(NY):
-        for j, ref in enumerate((key_ref, value_ref)):
-            half = out.at[i, :, j * DIM : (j + 1) * DIM]
-            moves.append(pltpu.make_async_copy(ref, half, sems.at[2 * i + j]))
+    for i, at in enumerate(lines):
+        for j, ref in enumerate((position, modality)):
+            moves.append(pltpu.make_async_copy(ref.at[at], rows.at[j, i], sems.at[j, i]))
     for move in moves:
         move.start()
     for move in moves:
         move.wait()
+    pos = jnp.concatenate([rows[0, i] for i in range(len(lines))], axis=0)
+    mod = jnp.concatenate([rows[1, i] for i in range(len(lines))], axis=0)
+    keys = 2 * NY
+    kcode[...] = pos[:keys] * 4 + mod[:keys]
+    low = unit_low(pos[:keys], jnp.min, 1 << 20)
+    high = unit_low(pos[keys:], jnp.max, -1)
+    qlast = jnp.concatenate(
+        [high[half][a : a + 1] for a in range(NZ) for half in range(2)], axis=0
+    )
+    qlast = jnp.broadcast_to(qlast, (QUNITS, TOK)) >> 6
+    lane = lax.broadcasted_iota(jnp.int32, (KUNITS, TOK), 1)
+    index = lax.broadcasted_iota(jnp.int32, (KUNITS, TOK), 0)
+    for s in range(2):
+        part = slice(s * NY, (s + 1) * NY)
+        column = jnp.broadcast_to(jnp.concatenate([low[0][part], low[1][part]], axis=0), (KUNITS, TOK))
+        square = jnp.concatenate([column, jnp.zeros((TOK - KUNITS, TOK), jnp.int32)], axis=0).T
+        across = square[:KUNITS]
+        before = ((across < column) | ((across == column) & (lane < index))) & (lane < KUNITS)
+        rank = jnp.sum(before.astype(jnp.int32), axis=1, keepdims=True)
+        tab[s * KUNITS : (s + 1) * KUNITS, :] = jnp.broadcast_to(rank, (KUNITS, TOK))
+        seen = ((across[:QUNITS] >> 6) <= qlast) & (lane[:QUNITS] < KUNITS)
+        need = jnp.sum(seen.astype(jnp.int32), axis=1, keepdims=True)
+        at = 2 * KUNITS + s * QUNITS
+        tab[at : at + QUNITS, :] = jnp.broadcast_to(need, (QUNITS, TOK))
+    qpos, qmod = pos[keys:], mod[keys:]
+    for m in range(3):
+        bid = jnp.where(qmod == 0, table[0, m], jnp.where(qmod == 1, table[1, m], table[2, m]))
+        lim = jnp.where(bid == 1, qpos | (UNIT - 1), qpos)
+        for a in range(NZ):
+            for half in range(2):
+                cut = lim[a : a + 1, half * UNIT : (half + 1) * UNIT]
+                qlim[2 * a + half, m : m + 1, :] = jnp.concatenate([cut] * HEADS, axis=1)
 
 
 def plan(position, modality, table):
-    code = (position * 4 + modality).reshape(8, 2, 2, 4, 2, 2, TOK)
-    y, zlo, core, x, zhh, zhl = (lax.axis_index(a) for a in AXES)
-    kcode = lax.dynamic_slice(code, (0, zlo, 0, x, zhh, zhl, 0), (8, 1, 2, 1, 1, 1, TOK))
-    kcode = kcode.reshape(8, 2, TOK)
-    kcode = jnp.where(core == 0, jnp.stack([kcode[:, 0], kcode[:, 1]]), jnp.stack([kcode[:, 1], kcode[:, 0]]))
-    qcode = lax.dynamic_slice(code, (y, 0, core, x, zhh, 0, 0), (1, 2, 1, 1, 1, 2, TOK)).reshape(4, TOK)
-    return tables_of(kcode, qcode, zlo * 2 + zhl, table)
-
-
-def tables_of(kcode, qcode, own, table):
-    masks = jnp.array(MASKS)
-    pick = (own ^ masks)[:, None, None] == jnp.arange(4)[None, :, None]
-    qcode = jnp.sum(jnp.where(pick, qcode[None], 0), axis=1)
-    qpos, qmod = (qcode >> 2).reshape(QUNITS, UNIT), (qcode & 3).reshape(QUNITS, UNIT)
-    bids = [
-        jnp.where(qmod == 0, table[0, m], jnp.where(qmod == 1, table[1, m], table[2, m])) for m in range(3)
-    ]
-    lim = jnp.stack([jnp.where(b == 1, qpos | (UNIT - 1), qpos) for b in bids], axis=1)
-    qlim = jnp.concatenate([lim] * HEADS, axis=2)
-    kunit = (kcode >> 2).reshape(2, KUNITS, UNIT)
-    low = jnp.min(kunit, axis=2)
-    index = jnp.arange(KUNITS)
-    a, b = low[:, None, :], low[:, :, None]
-    before = (a < b) | ((a == b) & (index[None, None, :] < index[None, :, None]))
-    rank = jnp.sum(before.astype(jnp.int32), axis=2)
-    qhigh = jnp.max(qpos, axis=1)
-    need = jnp.sum((a // UNIT <= qhigh[None, :, None] // UNIT).astype(jnp.int32), axis=2)
-    return (rank.reshape(-1), need.reshape(-1)), kcode.reshape(2 * NY, TOK), qlim
+    hbm = pl.BlockSpec(memory_space=pltpu.HBM)
+    vmem = pl.BlockSpec(memory_space=pltpu.VMEM)
+    count = 2 * NY + NZ
+    lines = position.shape[0] // TOK
+    return pl.pallas_call(
+        plan_kernel,
+        in_specs=[pl.BlockSpec(memory_space=pltpu.SMEM), hbm, hbm],
+        out_specs=[vmem] * 3,
+        out_shape=[
+            jax.ShapeDtypeStruct((2 * KUNITS + 2 * QUNITS, TOK), jnp.int32),
+            pltpu.VMEM((2 * NY, TOK), jnp.int32),
+            pltpu.VMEM((QUNITS, 3, ROWS), jnp.int32),
+        ],
+        scratch_shapes=[
+            pltpu.VMEM((2, count, 1, TOK), jnp.int32),
+            pltpu.SemaphoreType.DMA((2, count)),
+        ],
+        compiler_params=pltpu.CompilerParams(vmem_limit_bytes=8 << 20),
+        name="plan",
+    )(table, position.reshape(lines, 1, TOK), modality.reshape(lines, 1, TOK))
 
 
 def shards(queries, grad_out, attn_out, key_states, value_states, log_norm, position, modality, table):
@@ -259,33 +297,24 @@
     def over_y(value):
         return lax.all_to_all(value, "y", 0, 0)
 
-    copies = pl.pallas_call(
-        copies_kernel,
-        out_shape=jax.ShapeDtypeStruct((NY, TOK, 2 * DIM), bf16),
-        in_specs=[pl.BlockSpec(memory_space=pltpu.HBM)] * 2,
-        out_specs=pl.BlockSpec(memory_space=pltpu.HBM),
-        scratch_shapes=[pltpu.SemaphoreType.DMA((2 * NY,))],
-        compiler_params=pltpu.CompilerParams(vmem_limit_bytes=8 << 20),
-        name="copies",
-    )(key_states, value_states)
-    copies, queries = lax.optimization_barrier((copies, queries))
+    pair = jnp.concatenate([key_states, value_states], axis=1)
+    copies = jnp.broadcast_to(pair[None], (NY, TOK, 2 * DIM))
     msg = pl.pallas_call(
         pack_kernel, out_shape=pltpu.VMEM((TOK + 8, 2 * WIDE), bf16), compiler_params=pltpu.CompilerParams(vmem_limit_bytes=8 << 20), name="pack"
     )(queries, grad_out, attn_out, log_norm.T)
+    far, last = along_z(msg, MASKS[2]), along_z(msg, MASKS[3])
     kvo = over_y(copies).reshape(NY * TOK, 2 * DIM)
     near = along_z(msg, MASKS[1])
-    far, last = along_z(msg, MASKS[2]), along_z(msg, MASKS[3])
-    tables, kcode, qlim = plan(position, modality, table)
-    kvo, tables, kcode, qlim = lax.optimization_barrier((kvo, tables, kcode, qlim))
+    tab, kcode, qlim = plan(position, modality, table)
     kvx = other_core(kvo)
-    raw_near, old = tile(tables, 0, (msg, near), kvo, kcode, qlim, 0, raws=(0, 4))
+    raw_near, old = tile(tab, 0, (msg, near), kvo, kcode, qlim, 0, raws=(0, 4))
     own_q, near_q, raw_far, gkvx = tile(
-        tables, 0, (msg, near, far, last), kvx, kcode, qlim, 1,
+        tab, 0, (msg, near, far, last), kvx, kcode, qlim, 1,
         ((0, f32), (1, bf16)), (4, 8), raw_near, None, bf16,
     )
     got = other_core(gkvx)
     far_q, last_q, gkvo = tile(
-        tables, 2, (far, last), kvo, kcode, qlim, 0, ((0, bf16), (1, bf16)), None, raw_far, old, f32
+        tab, 2, (far, last), kvo, kcode, qlim, 0, ((0, bf16), (1, bf16)), None, raw_far, old, f32
     )
     paired = (gkvo + got.astype(f32)).astype(bf16).reshape(NY, TOK, 2 * DIM)
     summed = over_y(paired)
@@ -293,11 +322,8 @@
     grad_key, grad_value = pl.pallas_call(
         finish_kernel, out_shape=[narrow] * 2, compiler_params=pltpu.CompilerParams(vmem_limit_bytes=8 << 20), name="finish"
     )(in_vmem(summed))
-    back = [along_z(near_q, MASKS[1])]
-    back += [along_z(far_q, MASKS[2]), along_z(last_q, MASKS[3])]
-    g0 = own_q
-    score_scale = DIM ** (-0.5)
-    grad_q = (g0 + back[0].astype(f32) + back[1].astype(f32) + back[2].astype(f32)) * score_scale
+    back = [along_z(g, mask) for g, mask in zip((near_q, far_q, last_q), MASKS[1:])]
+    grad_q = (own_q + back[0].astype(f32) + back[1].astype(f32) + back[2].astype(f32)) * DIM ** (-0.5)
     return grad_q.astype(bf16), grad_key, grad_value
 
 

time: 102 us -> 101 us (level)
  blocking collectives: 0 us -> 24.5 us
  waiting for transfers between devices: 34.8 us -> 24.8 us
  starting transfers between devices: 37 us -> 30 us
  other arithmetic: 8.26 us -> 2.44 us
  local copies, waits for them, and re-layouts: 4.19 us -> 0.07 us
  Pallas kernels: 16.3 us -> 18 us
    all_to_all x0 -> x1, blocking collectives: none -> 24.5 us  [over_y(): return lax.all_to_all(value, 'y', 0, 0)]
    all_to_all x2 -> x1, waiting for transfers between devices: 8.77 us -> 0.68 us  [over_y(): return lax.all_to_all(value, 'y', 0, 0)]
    all_to_all x2 -> x1, starting transfers between devices: 10.7 us -> 3.49 us  [over_y(): return lax.all_to_all(value, 'y', 0, 0)]
    eq x3 -> x0, other arithmetic: 5.69 us -> none  [the longest x2 5.61 us: tables_of(): b == 1]
    unnamed x20 -> x14, local copies, waits for them, and re-layouts: 2.79 us -> 0.04 us
    ppermute x6, waiting for transfers between devices: 26 us -> 24.1 us  [along_z(): lax.ppermute(value, ('zlo', 'zhl'), [(i, i ^ mask) for i in range(NZ)])]
    pallas_call x4, Pallas kernels: 15.4 us -> 17.1 us  [the longest x3 15.6 us: tile(): pl.pallas_call(body, in_specs=[smem] + [vmem] * len(arrays), out_specs=[v...]
  transfers between devices with their start and end apart: 10 -> 9, of which waited for: 5 -> 4; matrix products, arithmetic and copies ran while one was open for 9% -> 1% of each run, Pallas kernels for 8% -> 10%
where the time goes in v6:
time: 101 us
  starting transfers between devices  30 us (30%)
  waiting for transfers between devices  24.8 us (25%)
  blocking collectives  24.5 us (24%)
  Pallas kernels  18 us (18%)
  other arithmetic  2.44 us (2%)
    all_to_all x1, blocking collectives, over_y(): return lax.all_to_all(value, 'y', 0, 0)  24.5 us
    ppermute x6, waiting for transfers between devices, along_z(): lax.ppermute(value, ('zlo', 'zhl'), [(i, i ^ mask) for i in range(NZ)])  24.1 us
    ppermute x6, starting transfers between devices, along_z(): lax.ppermute(value, ('zlo', 'zhl'), [(i, i ^ mask) for i in range(NZ)])  22.5 us
    pallas_call x3, Pallas kernels, tile(): pl.pallas_call(body, in_specs=[smem] + [vmem] * len(arrays), out_specs=[v...  15.6 us
    ppermute x2, starting transfers between devices, other_core(): return lax.ppermute(value, 'core', [(0, 1), (1, 0)])  3.96 us
    all_to_all x1, starting transfers between devices, over_y(): return lax.all_to_all(value, 'y', 0, 0)  3.49 us
  transfers between devices with their start and end apart: 9, of which 4 were waited for; matrix products, arithmetic and copies ran while one was open for 1% of the time, Pallas kernels for 10%

profile of v6, /device:TPU:6, one launch (start us, length us, event | category | flops | bytes accessed | tf_op | source)
XLA Modules:
  0.0 100.7 jit_solution(5947934236060952688)
XLA Ops:
  0.6 0.8 pad_maximum_fusion
  1.5 0.0 copy-start.2
  1.5 0.0 copy-start.3
  1.5 0.0 copy-start.4
  1.5 24.5 %all_to_all.10 = bf16[8,128,256]{2,1,0:T(8,128)(2,1)S(1)} all-to-all(bf16[8,128,256]{2,1,0:T(8,128)(2,1)S(1)} %broadcast_in_dim.2), channel_id=1, replica_groups=mesh['y'=8,'zlo'=2,'core'=2,'x'=4,'zhh'=2,'zhl'=2] {'y'}, dimensions={0} | all-to-all | bytes 1048576 | tf_op jit(solution)/shard_map/all_to_all | solution.py:298
  26.0 0.0 copy-start.5
  26.0 2.0 %collective-permute-start.3 = (bf16[1024,256]{1,0:T(8,128)(2,1)S(1)}, bf16[1024,256]{1,0:T(8,128)(2,1)S(1)}, u32[]{:S(2)}, u32[]{:S(2)}) collective-permute-start(bf16[1024,256]{1,0:T(8,128)(2,1)S(1)} %bitcast.5), channel_id=1, source_target_pairs={{0,16},{16,0},{1,17},{17,1},{2,18},{18,2},{3,19},{19,3},{4,20},{20... | collective-permute-start | bytes 1572872 | tf_op jit(solution)/shard_map/ppermute | solution.py:295
  28.1 0.0 copy-done.2
  28.1 0.0 copy-done.3
  28.1 0.0 copy-done.4
  28.1 0.0 copy-done.5
  28.1 0.0 copy-start
  28.1 0.0 copy-start.1
  28.1 0.2 pack.1.refs_1_
  28.3 0.0 copy-start.6
  28.3 4.4 %collective-permute-start = (bf16[136,1024]{1,0:T(8,128)(2,1)S(1)}, bf16[136,1024]{1,0:T(8,128)(2,1)S(1)}, u32[]{:S(2)}, u32[]{:S(2)}) collective-permute-start(bf16[136,1024]{1,0:T(8,128)(2,1)S(1)} %pack.1.refs_1_), channel_id=1, source_target_pairs={{0,32},{1,33},{32,0},{33,1},{2,34},{3,35},{34,2},{35,3},{4,36},{5,... | collective-permute-start | bytes 835592 | tf_op jit(solution)/shard_map/ppermute | solution.py:292
  32.7 5.5 %collective-permute-start.2 = (bf16[136,1024]{1,0:T(8,128)(2,1)S(1)}, bf16[136,1024]{1,0:T(8,128)(2,1)S(1)}, u32[]{:S(2)}, u32[]{:S(2)}) collective-permute-start(bf16[136,1024]{1,0:T(8,128)(2,1)S(1)} %pack.1.refs_1_), channel_id=1, source_target_pairs={{0,33},{1,32},{32,1},{33,0},{2,35},{3,34},{34,3},{35,2},{4,37},{5,... | collective-permute-start | bytes 835592 | tf_op jit(solution)/shard_map/ppermute | solution.py:292
  38.3 2.5 %collective-permute-start.1 = (bf16[136,1024]{1,0:T(8,128)(2,1)S(1)}, bf16[136,1024]{1,0:T(8,128)(2,1)S(1)}, u32[]{:S(2)}, u32[]{:S(2)}) collective-permute-start(bf16[136,1024]{1,0:T(8,128)(2,1)S(1)} %pack.1.refs_1_), channel_id=1, source_target_pairs={{0,1},{1,0},{32,33},{33,32},{2,3},{3,2},{34,35},{35,34},{4,5},{5,4... | collective-permute-start | bytes 835592 | tf_op jit(solution)/shard_map/ppermute | solution.py:292
  40.8 0.0 copy-done
  40.8 0.0 copy-done.1
  40.8 0.0 copy-done.6
  40.8 1.5 %plan.1 = (s32[48,128]{1,0:T(8,128)S(1)}, s32[16,128]{1,0:T(8,128)S(1)}, s32[8,3,256]{2,1,0:T(4,128)S(1)}) custom-call(s32[3,3]{1,0:T(4,128)S(1)} %copy-done.6, s32[512,1,128]{2,1,0:T(1,128)S(1)} %bitcast.8, s32[512,1,128]{2,1,0:T(1,128)S(1)} %bitcast.9), custom_call_target="tpu_custom_call" | custom-call | tf_op jit(solution)/shard_map/plan/pallas_call | solution.py:272
  42.3 0.0 collective-permute-done.refs_2_
  42.3 4.2 %shard_map.112 = (f32[4,128,256]{2,1,0:T(8,128)S(1)}, f32[1024,256]{1,0:T(8,128)S(1)}) custom-call(s32[48,128]{1,0:T(8,128)S(1)} %get-tuple-element.17.refs_0_, bf16[136,1024]{1,0:T(8,128)(2,1)S(1)} %pack.1.refs_1_, bf16[136,1024]{1,0:T(8,128)(2,1)S(1)} %collective-permute-done.refs_2_, bf16[1024,256]{1,0:T(8,128)(2,1)S(1)} %bitcast.6, ...), custom_call_target="tpu_custom_call" | custom-call | tf_op jit(solution)/shard_map/pallas_call | solution.py:194
  46.5 3.4 %collective-permute-done.2.refs_4_.refs_2_ = bf16[136,1024]{1,0:T(8,128)(2,1)S(1)} collective-permute-done((bf16[136,1024]{1,0:T(8,128)(2,1)S(1)}, bf16[136,1024]{1,0:T(8,128)(2,1)S(1)}, u32[]{:S(2)}, u32[]{:S(2)}) %collective-permute-start.2) | collective-permute-done | bytes 278560 | tf_op jit(solution)/shard_map/ppermute | solution.py:292
  49.9 13.8 %collective-permute-done.1.refs_3_.refs_1_ = bf16[136,1024]{1,0:T(8,128)(2,1)S(1)} collective-permute-done((bf16[136,1024]{1,0:T(8,128)(2,1)S(1)}, bf16[136,1024]{1,0:T(8,128)(2,1)S(1)}, u32[]{:S(2)}, u32[]{:S(2)}) %collective-permute-start.1) | collective-permute-done | bytes 278560 | tf_op jit(solution)/shard_map/ppermute | solution.py:292
  63.8 0.0 collective-permute-done.3.refs_5_
  63.8 7.1 %shard_map.113 = (f32[128,512]{1,0:T(8,128)S(1)}, bf16[128,512]{1,0:T(8,128)(2,1)S(1)}, f32[4,128,256]{2,1,0:T(8,128)S(1)}, bf16[1024,256]{1,0:T(8,128)(2,1)S(1)}) custom-call(s32[48,128]{1,0:T(8,128)S(1)} %get-tuple-element.17.refs_0_, bf16[136,1024]{1,0:T(8,128)(2,1)S(1)} %pack.1.refs_1_, bf16[136,1024]{1,0:T(8,128)(2,1)S(1)} %collective-permute-done.refs_2_, ...), custom_call_target="tpu_custom_call" | custom-call | tf_op jit(solution)/shard_map/pallas_call | solution.py:194
  70.9 1.9 %collective-permute-start.7 = (bf16[1024,256]{1,0:T(8,128)(2,1)S(1)}, bf16[1024,256]{1,0:T(8,128)(2,1)S(1)}, u32[]{:S(2)}, u32[]{:S(2)}) collective-permute-start(bf16[1024,256]{1,0:T(8,128)(2,1)S(1)} %get-tuple-element.28), channel_id=1, source_target_pairs={{0,16},{16,0},{1,17},{17,1},{2,18},{18,2},{3,19},{19,3},{4,20},{20... | collective-permute-start | bytes 1572872 | tf_op jit(solution)/shard_map/ppermute | solution.py:295
  72.8 4.3 %shard_map.114 = (bf16[128,512]{1,0:T(8,128)(2,1)S(1)}, bf16[128,512]{1,0:T(8,128)(2,1)S(1)}, f32[1024,256]{1,0:T(8,128)S(1)}) custom-call(s32[48,128]{1,0:T(8,128)S(1)} %get-tuple-element.17.refs_0_, bf16[136,1024]{1,0:T(8,128)(2,1)S(1)} %collective-permute-done.1.refs_3_.refs_1_, bf16[136,1024]{1,0:T(8,128)(2,1)S(1)} %collective-permute-done.2.refs_4_.refs_2_, ...), custom_call_target="tpu_custom_call" | custom-call | tf_op jit(solution)/shard_map/pallas_call | solution.py:194
  77.1 0.0 collective-permute-done.7
  77.2 0.9 add_convert_fusion
  78.1 3.5 %all-to-all-start.1 = ((bf16[8,128,256]{2,1,0:T(8,128)(2,1)}), bf16[8,128,256]{2,1,0:T(8,128)(2,1)S(1)}, u32[]{:S(2)}, u32[]{:S(2)}) async-start(bf16[8,128,256]{2,1,0:T(8,128)(2,1)} %bitcast.4), calls=%async_computation.1 | async-start | bytes 1048576 | tf_op jit(solution)/shard_map/all_to_all | solution.py:298
  81.6 1.9 %collective-permute-start.4 = (bf16[128,512]{1,0:T(8,128)(2,1)S(1)}, bf16[128,512]{1,0:T(8,128)(2,1)S(1)}, u32[]{:S(2)}, u32[]{:S(2)}) collective-permute-start(bf16[128,512]{1,0:T(8,128)(2,1)S(1)} %get-tuple-element.22), channel_id=1, source_target_pairs={{0,32},{1,33},{32,0},{33,1},{2,34},{3,35},{34,2},{35,3},{4,36},{5,... | collective-permute-start | bytes 393224 | tf_op jit(solution)/shard_map/ppermute | solution.py:292
  83.5 5.1 %collective-permute-start.5 = (bf16[128,512]{1,0:T(8,128)(2,1)S(1)}, bf16[128,512]{1,0:T(8,128)(2,1)S(1)}, u32[]{:S(2)}, u32[]{:S(2)}) collective-permute-start(bf16[128,512]{1,0:T(8,128)(2,1)S(1)} %get-tuple-element.25), channel_id=1, source_target_pairs={{0,1},{1,0},{32,33},{33,32},{2,3},{3,2},{34,35},{35,34},{4,5},{5,4... | collective-permute-start | bytes 393224 | tf_op jit(solution)/shard_map/ppermute | solution.py:292
  88.6 3.1 %collective-permute-start.6 = (bf16[128,512]{1,0:T(8,128)(2,1)S(1)}, bf16[128,512]{1,0:T(8,128)(2,1)S(1)}, u32[]{:S(2)}, u32[]{:S(2)}) collective-permute-start(bf16[128,512]{1,0:T(8,128)(2,1)S(1)} %get-tuple-element.26), channel_id=1, source_target_pairs={{0,33},{1,32},{32,1},{33,0},{2,35},{3,34},{34,3},{35,2},{4,37},{5,... | collective-permute-start | bytes 393224 | tf_op jit(solution)/shard_map/ppermute | solution.py:292
  91.7 0.0 collective-permute-done.4
  91.7 6.8 %collective-permute-done.5 = bf16[128,512]{1,0:T(8,128)(2,1)S(1)} collective-permute-done((bf16[128,512]{1,0:T(8,128)(2,1)S(1)}, bf16[128,512]{1,0:T(8,128)(2,1)S(1)}, u32[]{:S(2)}, u32[]{:S(2)}) %collective-permute-start.5) | collective-permute-done | bytes 131104 | tf_op jit(solution)/shard_map/ppermute | solution.py:292
  98.6 0.0 collective-permute-done.6
  98.6 0.7 multiply_convert_fusion
  99.3 0.7 all-to-all-done.1.parts
  100.0 0.7 finish.1
  (1 shorter events, 0.0 us)
Async XLA Ops:
  1.5 26.6 %copy-start.2 = (bf16[128,512]{1,0:T(8,128)(2,1)S(1)}, bf16[128,512]{1,0:T(8,128)(2,1)}, u32[]{:S(2)}) copy-start(bf16[128,512]{1,0:T(8,128)(2,1)} %q_ref.1) | copy-start | bytes 393220
  1.5 26.6 %copy-start.3 = (bf16[128,512]{1,0:T(8,128)(2,1)S(1)}, bf16[128,512]{1,0:T(8,128)(2,1)}, u32[]{:S(2)}) copy-start(bf16[128,512]{1,0:T(8,128)(2,1)} %d_ref.1) | copy-start | bytes 393220
  1.5 26.6 %copy-start.4 = (bf16[128,512]{1,0:T(8,128)(2,1)S(1)}, bf16[128,512]{1,0:T(8,128)(2,1)}, u32[]{:S(2)}) copy-start(bf16[128,512]{1,0:T(8,128)(2,1)} %o_ref.1) | copy-start | bytes 393220
  26.0 2.1 %copy-start.5 = (f32[128,4]{0,1:T(4,128)S(1)}, f32[128,4]{0,1:T(4,128)}, u32[]{:S(2)}) copy-start(f32[128,4]{0,1:T(4,128)} %param.14) | copy-start | bytes 6148
  26.0 37.8 %collective-permute-start.3 = (bf16[1024,256]{1,0:T(8,128)(2,1)S(1)}, bf16[1024,256]{1,0:T(8,128)(2,1)S(1)}, u32[]{:S(2)}, u32[]{:S(2)}) collective-permute-start(bf16[1024,256]{1,0:T(8,128)(2,1)S(1)} %bitcast.5), channel_id=1, source_target_pairs={{0,16},{16,0},{1,17},{17,1},{2,18},{18,2},{3,19},{19,3},{4,20},{20... | collective-permute-start | bytes 1572872 | tf_op jit(solution)/shard_map/ppermute | solution.py:295
  28.1 12.7 %copy-start = (s32[65536]{0:T(1024)S(1)}, s32[65536]{0:T(1024)}, u32[]{:S(2)}) copy-start(s32[65536]{0:T(1024)} %param.15) | copy-start | bytes 786436
  28.1 12.7 %copy-start.1 = (s32[65536]{0:T(1024)S(1)}, s32[65536]{0:T(1024)}, u32[]{:S(2)}) copy-start(s32[65536]{0:T(1024)} %param.16) | copy-start | bytes 786436
  28.3 12.5 %copy-start.6 = (s32[3,3]{1,0:T(4,128)S(1)}, s32[3,3]{1,0:T(4,128)}, u32[]{:S(2)}) copy-start(s32[3,3]{1,0:T(4,128)} %table.1) | copy-start | bytes 112
  28.3 14.0 %collective-permute-start = (bf16[136,1024]{1,0:T(8,128)(2,1)S(1)}, bf16[136,1024]{1,0:T(8,128)(2,1)S(1)}, u32[]{:S(2)}, u32[]{:S(2)}) collective-permute-start(bf16[136,1024]{1,0:T(8,128)(2,1)S(1)} %pack.1.refs_1_), channel_id=1, source_target_pairs={{0,32},{1,33},{32,0},{33,1},{2,34},{3,35},{34,2},{35,3},{4,36},{5,... | collective-permute-start | bytes 835592 | tf_op jit(solution)/shard_map/ppermute | solution.py:292
  32.7 17.2 %collective-permute-start.2 = (bf16[136,1024]{1,0:T(8,128)(2,1)S(1)}, bf16[136,1024]{1,0:T(8,128)(2,1)S(1)}, u32[]{:S(2)}, u32[]{:S(2)}) collective-permute-start(bf16[136,1024]{1,0:T(8,128)(2,1)S(1)} %pack.1.refs_1_), channel_id=1, source_target_pairs={{0,33},{1,32},{32,1},{33,0},{2,35},{3,34},{34,3},{35,2},{4,37},{5,... | collective-permute-start | bytes 835592 | tf_op jit(solution)/shard_map/ppermute | solution.py:292
  38.3 25.5 %collective-permute-start.1 = (bf16[136,1024]{1,0:T(8,128)(2,1)S(1)}, bf16[136,1024]{1,0:T(8,128)(2,1)S(1)}, u32[]{:S(2)}, u32[]{:S(2)}) collective-permute-start(bf16[136,1024]{1,0:T(8,128)(2,1)S(1)} %pack.1.refs_1_), channel_id=1, source_target_pairs={{0,1},{1,0},{32,33},{33,32},{2,3},{3,2},{34,35},{35,34},{4,5},{5,4... | collective-permute-start | bytes 835592 | tf_op jit(solution)/shard_map/ppermute | solution.py:292
  70.9 6.3 %collective-permute-start.7 = (bf16[1024,256]{1,0:T(8,128)(2,1)S(1)}, bf16[1024,256]{1,0:T(8,128)(2,1)S(1)}, u32[]{:S(2)}, u32[]{:S(2)}) collective-permute-start(bf16[1024,256]{1,0:T(8,128)(2,1)S(1)} %get-tuple-element.28), channel_id=1, source_target_pairs={{0,16},{16,0},{1,17},{17,1},{2,18},{18,2},{3,19},{19,3},{4,20},{20... | collective-permute-start | bytes 1572872 | tf_op jit(solution)/shard_map/ppermute | solution.py:295
  78.1 21.9 %all-to-all-start.1 = ((bf16[8,128,256]{2,1,0:T(8,128)(2,1)}), bf16[8,128,256]{2,1,0:T(8,128)(2,1)S(1)}, u32[]{:S(2)}, u32[]{:S(2)}) async-start(bf16[8,128,256]{2,1,0:T(8,128)(2,1)} %bitcast.4), calls=%async_computation.1 | async-start | bytes 1048576 | tf_op jit(solution)/shard_map/all_to_all | solution.py:298
  81.6 10.1 %collective-permute-start.4 = (bf16[128,512]{1,0:T(8,128)(2,1)S(1)}, bf16[128,512]{1,0:T(8,128)(2,1)S(1)}, u32[]{:S(2)}, u32[]{:S(2)}) collective-permute-start(bf16[128,512]{1,0:T(8,128)(2,1)S(1)} %get-tuple-element.22), channel_id=1, source_target_pairs={{0,32},{1,33},{32,0},{33,1},{2,34},{3,35},{34,2},{35,3},{4,36},{5,... | collective-permute-start | bytes 393224 | tf_op jit(solution)/shard_map/ppermute | solution.py:292
  83.5 15.1 %collective-permute-start.5 = (bf16[128,512]{1,0:T(8,128)(2,1)S(1)}, bf16[128,512]{1,0:T(8,128)(2,1)S(1)}, u32[]{:S(2)}, u32[]{:S(2)}) collective-permute-start(bf16[128,512]{1,0:T(8,128)(2,1)S(1)} %get-tuple-element.25), channel_id=1, source_target_pairs={{0,1},{1,0},{32,33},{33,32},{2,3},{3,2},{34,35},{35,34},{4,5},{5,4... | collective-permute-start | bytes 393224 | tf_op jit(solution)/shard_map/ppermute | solution.py:292
  88.6 10.0 %collective-permute-start.6 = (bf16[128,512]{1,0:T(8,128)(2,1)S(1)}, bf16[128,512]{1,0:T(8,128)(2,1)S(1)}, u32[]{:S(2)}, u32[]{:S(2)}) collective-permute-start(bf16[128,512]{1,0:T(8,128)(2,1)S(1)} %get-tuple-element.26), channel_id=1, source_target_pairs={{0,33},{1,32},{32,1},{33,0},{2,35},{3,34},{34,3},{35,2},{4,37},{5,... | collective-permute-start | bytes 393224 | tf_op jit(solution)/shard_map/ppermute | solution.py:292

commit v7 on v6

--- a/solution.py
+++ b/solution.py
@@ -284,7 +284,11 @@
         ],
         compiler_params=pltpu.CompilerParams(vmem_limit_bytes=8 << 20),
         name="plan",
-    )(table, position.reshape(lines, 1, TOK), modality.reshape(lines, 1, TOK))
+    )(
+        table,
+        pltpu.with_memory_space_constraint(position.reshape(lines, 1, TOK), pltpu.HBM),
+        pltpu.with_memory_space_constraint(modality.reshape(lines, 1, TOK), pltpu.HBM),
+    )
 
 
 def shards(queries, grad_out, attn_out, key_states, value_states, log_norm, position, modality, table):
@@ -302,19 +306,18 @@
     msg = pl.pallas_call(
         pack_kernel, out_shape=pltpu.VMEM((TOK + 8, 2 * WIDE), bf16), compiler_params=pltpu.CompilerParams(vmem_limit_bytes=8 << 20), name="pack"
     )(queries, grad_out, attn_out, log_norm.T)
-    far, last = along_z(msg, MASKS[2]), along_z(msg, MASKS[3])
     kvo = over_y(copies).reshape(NY * TOK, 2 * DIM)
-    near = along_z(msg, MASKS[1])
+    far = along_z(msg, 1)
+    near = along_z(msg, 2)
     tab, kcode, qlim = plan(position, modality, table)
     kvx = other_core(kvo)
-    raw_near, old = tile(tab, 0, (msg, near), kvo, kcode, qlim, 0, raws=(0, 4))
-    own_q, near_q, raw_far, gkvx = tile(
-        tab, 0, (msg, near, far, last), kvx, kcode, qlim, 1,
-        ((0, f32), (1, bf16)), (4, 8), raw_near, None, bf16,
-    )
+    last = along_z(far, 2)
+    raw_near, old_own = tile(tab, 0, (msg, near), kvo, kcode, qlim, 0, raws=(0, 4))
+    own_q, near_q, old_oth = tile(tab, 0, (msg, near), kvx, kcode, qlim, 1, ((0, f32), (1, bf16)), None, raw_near)
+    raw_far, gkvx = tile(tab, 2, (far, last), kvx, kcode, qlim, 1, (), (0, 4), None, old_oth, bf16)
     got = other_core(gkvx)
     far_q, last_q, gkvo = tile(
-        tab, 2, (far, last), kvo, kcode, qlim, 0, ((0, bf16), (1, bf16)), None, raw_far, old, f32
+        tab, 2, (far, last), kvo, kcode, qlim, 0, ((0, bf16), (1, bf16)), None, raw_far, old_own, f32
     )
     paired = (gkvo + got.astype(f32)).astype(bf16).reshape(NY, TOK, 2 * DIM)
     summed = over_y(paired)

time: 101 us -> 86 us (0.85); the launches traced: 101 us -> 84.4 us
  blocking collectives: 24.5 us -> 0 us
  starting transfers between devices: 30 us -> 38.9 us
  waiting for transfers between devices: 24.8 us -> 21.1 us
  Pallas kernels: 18 us -> 20.3 us
    all_to_all x1 -> x0, blocking collectives: 24.5 us -> none  [over_y(): return lax.all_to_all(value, 'y', 0, 0)]
    ppermute x6, waiting for transfers between devices: 24.1 us -> 9.95 us  [along_z(): lax.ppermute(value, ('zlo', 'zhl'), [(i, i ^ mask) for i in range(NZ)])]
    all_to_all x1 -> x2, waiting for transfers between devices: 0.68 us -> 11.2 us  [over_y(): return lax.all_to_all(value, 'y', 0, 0)]
    all_to_all x1 -> x2, starting transfers between devices: 3.49 us -> 10.7 us  [over_y(): return lax.all_to_all(value, 'y', 0, 0)]
    ppermute x6, starting transfers between devices: 22.5 us -> 24.2 us  [along_z(): lax.ppermute(value, ('zlo', 'zhl'), [(i, i ^ mask) for i in range(NZ)])]
    pallas_call x3 -> x4, Pallas kernels: 15.6 us -> 17.1 us  [tile(): pl.pallas_call(body, in_specs=[smem] + [vmem] * len(arrays), out_specs=[v...]
  transfers between devices with their start and end apart: 9 -> 10, of which waited for: 4 -> 4; matrix products, arithmetic and copies ran while one was open for 1% -> 1% of each run, Pallas kernels for 10% -> 18%
where the time goes in v7:
time: 86 us; the launch traced here: 84.4 us
  starting transfers between devices  38.9 us (45%)
  waiting for transfers between devices  21.1 us (25%)
  Pallas kernels  20.3 us (24%)
  other arithmetic  2.44 us (3%)
  local copies, waits for them, and re-layouts  0.86 us (1%)
    ppermute x6, starting transfers between devices, along_z(): lax.ppermute(value, ('zlo', 'zhl'), [(i, i ^ mask) for i in range(NZ)])  24.2 us
    pallas_call x4, Pallas kernels, tile(): pl.pallas_call(body, in_specs=[smem] + [vmem] * len(arrays), out_specs=[v...  17.1 us
    all_to_all x2, waiting for transfers between devices, over_y(): return lax.all_to_all(value, 'y', 0, 0)  11.2 us
    all_to_all x2, starting transfers between devices, over_y(): return lax.all_to_all(value, 'y', 0, 0)  10.7 us
    ppermute x6, waiting for transfers between devices, along_z(): lax.ppermute(value, ('zlo', 'zhl'), [(i, i ^ mask) for i in range(NZ)])  9.95 us
    ppermute x2, starting transfers between devices, other_core(): return lax.ppermute(value, 'core', [(0, 1), (1, 0)])  3.97 us
    pallas_call x1, Pallas kernels, plan(): pl.pallas_call(plan_kernel, in_specs=[pl.BlockSpec(memory_space=pltpu.SME...  2.3 us
  transfers between devices with their start and end apart: 10, of which 4 were waited for; matrix products, arithmetic and copies ran while one was open for 1% of the time, Pallas kernels for 18%

profile of v7, /device:TPU:6, one launch (start us, length us, event | category | flops | bytes accessed | tf_op | source)
XLA Modules:
  0.0 84.4 jit_solution(17654851243358781378)
XLA Ops:
  0.6 0.8 pad_maximum_fusion
  1.4 0.8 broadcast_in_dim.2
  2.3 0.0 copy-start
  2.3 0.0 copy-start.1
  2.3 0.0 copy-start.2
  2.3 0.0 copy-start.3
  2.3 7.2 %all-to-all-start = ((bf16[8,128,256]{2,1,0:T(8,128)(2,1)}), bf16[8,128,256]{2,1,0:T(8,128)(2,1)S(1)}, u32[]{:S(2)}, u32[]{:S(2)}) async-start(bf16[8,128,256]{2,1,0:T(8,128)(2,1)} %broadcast_in_dim.2), calls=%async_computation | async-start | bytes 1048576 | tf_op jit(solution)/shard_map/all_to_all | solution.py:302
  9.5 0.0 copy-done
  9.5 0.0 copy-done.1
  9.5 0.0 copy-done.2
  9.5 0.0 copy-done.3
  9.5 0.2 pack.1.refs_1_
  9.7 6.1 %collective-permute-start.3 = (bf16[136,1024]{1,0:T(8,128)(2,1)S(1)}, bf16[136,1024]{1,0:T(8,128)(2,1)S(1)}, u32[]{:S(2)}, u32[]{:S(2)}) collective-permute-start(bf16[136,1024]{1,0:T(8,128)(2,1)S(1)} %pack.1.refs_1_), channel_id=1, source_target_pairs={{0,1},{1,0},{32,33},{33,32},{2,3},{3,2},{34,35},{35,34},{4,5},{5,4... | collective-permute-start | bytes 835592 | tf_op jit(solution)/shard_map/ppermute | solution.py:296
  15.8 11.2 %all-to-all-done = bf16[8,128,256]{2,1,0:T(8,128)(2,1)S(1)} async-done(((bf16[8,128,256]{2,1,0:T(8,128)(2,1)}), bf16[8,128,256]{2,1,0:T(8,128)(2,1)S(1)}, u32[]{:S(2)}, u32[]{:S(2)}) %all-to-all-start) | async-done | bytes 524320 | tf_op jit(solution)/shard_map/all_to_all | solution.py:302
  27.0 0.0 copy-start.4
  27.0 2.0 %collective-permute-start.1 = (bf16[1024,256]{1,0:T(8,128)(2,1)S(1)}, bf16[1024,256]{1,0:T(8,128)(2,1)S(1)}, u32[]{:S(2)}, u32[]{:S(2)}) collective-permute-start(bf16[1024,256]{1,0:T(8,128)(2,1)S(1)} %bitcast.5), channel_id=1, source_target_pairs={{0,16},{16,0},{1,17},{17,1},{2,18},{18,2},{3,19},{19,3},{4,20},{20... | collective-permute-start | bytes 1572872 | tf_op jit(solution)/shard_map/ppermute | solution.py:299
  29.1 4.3 %collective-permute-start = (bf16[136,1024]{1,0:T(8,128)(2,1)S(1)}, bf16[136,1024]{1,0:T(8,128)(2,1)S(1)}, u32[]{:S(2)}, u32[]{:S(2)}) collective-permute-start(bf16[136,1024]{1,0:T(8,128)(2,1)S(1)} %pack.1.refs_1_), channel_id=1, source_target_pairs={{0,32},{1,33},{32,0},{33,1},{2,34},{3,35},{34,2},{35,3},{4,36},{5,... | collective-permute-start | bytes 835592 | tf_op jit(solution)/shard_map/ppermute | solution.py:296
  33.4 0.0 collective-permute-done.3.refs_1_
  33.4 1.9 %collective-permute-start.4 = (bf16[136,1024]{1,0:T(8,128)(2,1)S(1)}, bf16[136,1024]{1,0:T(8,128)(2,1)S(1)}, u32[]{:S(2)}, u32[]{:S(2)}) collective-permute-start(bf16[136,1024]{1,0:T(8,128)(2,1)S(1)} %collective-permute-done.3.refs_1_), channel_id=1, source_target_pairs={{0,32},{1,33},{32,0},{33,1},{2,34},{3,35},{34,2},{35,3},{4,36},{5,... | collective-permute-start | bytes 835592 | tf_op jit(solution)/shard_map/ppermute | solution.py:296
  35.3 0.0 copy-done.4
  35.3 2.3 %plan.1 = (s32[48,128]{1,0:T(8,128)S(1)}, s32[16,128]{1,0:T(8,128)S(1)}, s32[8,3,256]{2,1,0:T(4,128)S(1)}) custom-call(s32[3,3]{1,0:T(4,128)S(1)} %copy-done.4, s32[512,1,128]{2,1,0:T(1,128)} %bitcast.9, s32[512,1,128]{2,1,0:T(1,128)} %bitcast.10), custom_call_target="tpu_custom_call" | custom-call | tf_op jit(solution)/shard_map/plan/pallas_call | solution.py:272
  37.6 3.2 %collective-permute-done.refs_2_ = bf16[136,1024]{1,0:T(8,128)(2,1)S(1)} collective-permute-done((bf16[136,1024]{1,0:T(8,128)(2,1)S(1)}, bf16[136,1024]{1,0:T(8,128)(2,1)S(1)}, u32[]{:S(2)}, u32[]{:S(2)}) %collective-permute-start) | collective-permute-done | bytes 278560 | tf_op jit(solution)/shard_map/ppermute | solution.py:296
  40.8 4.2 %shard_map.112 = (f32[4,128,256]{2,1,0:T(8,128)S(1)}, f32[1024,256]{1,0:T(8,128)S(1)}) custom-call(s32[48,128]{1,0:T(8,128)S(1)} %get-tuple-element.18.refs_0_, bf16[136,1024]{1,0:T(8,128)(2,1)S(1)} %pack.1.refs_1_, bf16[136,1024]{1,0:T(8,128)(2,1)S(1)} %collective-permute-done.refs_2_, bf16[1024,256]{1,0:T(8,128)(2,1)S(1)} %bitcast.6, ...), custom_call_target="tpu_custom_call" | custom-call | tf_op jit(solution)/shard_map/pallas_call | solution.py:194
  45.0 0.0 collective-permute-done.1.refs_3_
  45.1 4.3 %shard_map.113 = (f32[128,512]{1,0:T(8,128)S(1)}, bf16[128,512]{1,0:T(8,128)(2,1)S(1)}, f32[1024,256]{1,0:T(8,128)S(1)}) custom-call(s32[48,128]{1,0:T(8,128)S(1)} %get-tuple-element.18.refs_0_, bf16[136,1024]{1,0:T(8,128)(2,1)S(1)} %pack.1.refs_1_, bf16[136,1024]{1,0:T(8,128)(2,1)S(1)} %collective-permute-done.refs_2_, ...), custom_call_target="tpu_custom_call" | custom-call | tf_op jit(solution)/shard_map/pallas_call | solution.py:194
  49.4 0.0 collective-permute-done.4.refs_2_
  49.4 4.2 %shard_map.114 = (f32[4,128,256]{2,1,0:T(8,128)S(1)}, bf16[1024,256]{1,0:T(8,128)(2,1)S(1)}) custom-call(s32[48,128]{1,0:T(8,128)S(1)} %get-tuple-element.18.refs_0_, bf16[136,1024]{1,0:T(8,128)(2,1)S(1)} %collective-permute-done.3.refs_1_, bf16[136,1024]{1,0:T(8,128)(2,1)S(1)} %collective-permute-done.4.refs_2_, ...), custom_call_target="tpu_custom_call" | custom-call | tf_op jit(solution)/shard_map/pallas_call | solution.py:194
  53.6 1.9 %collective-permute-start.7 = (bf16[1024,256]{1,0:T(8,128)(2,1)S(1)}, bf16[1024,256]{1,0:T(8,128)(2,1)S(1)}, u32[]{:S(2)}, u32[]{:S(2)}) collective-permute-start(bf16[1024,256]{1,0:T(8,128)(2,1)S(1)} %get-tuple-element.30), channel_id=1, source_target_pairs={{0,16},{16,0},{1,17},{17,1},{2,18},{18,2},{3,19},{19,3},{4,20},{20... | collective-permute-start | bytes 1572872 | tf_op jit(solution)/shard_map/ppermute | solution.py:299
  55.6 4.3 %shard_map.115 = (bf16[128,512]{1,0:T(8,128)(2,1)S(1)}, bf16[128,512]{1,0:T(8,128)(2,1)S(1)}, f32[1024,256]{1,0:T(8,128)S(1)}) custom-call(s32[48,128]{1,0:T(8,128)S(1)} %get-tuple-element.18.refs_0_, bf16[136,1024]{1,0:T(8,128)(2,1)S(1)} %collective-permute-done.3.refs_1_, bf16[136,1024]{1,0:T(8,128)(2,1)S(1)} %collective-permute-done.4.refs_2_, ...), custom_call_target="tpu_custom_call" | custom-call | tf_op jit(solution)/shard_map/pallas_call | solution.py:194
  59.9 0.0 collective-permute-done.7
  59.9 0.9 %add_convert_fusion = bf16[1024,256]{1,0:T(8,128)(2,1)} fusion(f32[1024,256]{1,0:T(8,128)S(1)} %get-tuple-element.29, bf16[1024,256]{1,0:T(8,128)(2,1)S(1)} %collective-permute-done.7), kind=kLoop, calls=%fused_computation | loop fusion | flops 786432 | bytes 2097152 | tf_op jit(solution)/shard_map/convert_element_type | solution.py:322
  60.8 3.5 %all-to-all-start.1 = ((bf16[8,128,256]{2,1,0:T(8,128)(2,1)}), bf16[8,128,256]{2,1,0:T(8,128)(2,1)S(1)}, u32[]{:S(2)}, u32[]{:S(2)}) async-start(bf16[8,128,256]{2,1,0:T(8,128)(2,1)} %bitcast.4), calls=%async_computation.1 | async-start | bytes 1048576 | tf_op jit(solution)/shard_map/all_to_all | solution.py:302
  64.3 6.1 %collective-permute-start.5 = (bf16[128,512]{1,0:T(8,128)(2,1)S(1)}, bf16[128,512]{1,0:T(8,128)(2,1)S(1)}, u32[]{:S(2)}, u32[]{:S(2)}) collective-permute-start(bf16[128,512]{1,0:T(8,128)(2,1)S(1)} %get-tuple-element.27), channel_id=1, source_target_pairs={{0,1},{1,0},{32,33},{33,32},{2,3},{3,2},{34,35},{35,34},{4,5},{5,4... | collective-permute-start | bytes 393224 | tf_op jit(solution)/shard_map/ppermute | solution.py:296
  70.4 3.4 %collective-permute-start.6 = (bf16[128,512]{1,0:T(8,128)(2,1)S(1)}, bf16[128,512]{1,0:T(8,128)(2,1)S(1)}, u32[]{:S(2)}, u32[]{:S(2)}) collective-permute-start(bf16[128,512]{1,0:T(8,128)(2,1)S(1)} %get-tuple-element.28), channel_id=1, source_target_pairs={{0,33},{1,32},{32,1},{33,0},{2,35},{3,34},{34,3},{35,2},{4,37},{5,... | collective-permute-start | bytes 393224 | tf_op jit(solution)/shard_map/ppermute | solution.py:296
  73.8 2.5 %collective-permute-start.2 = (bf16[128,512]{1,0:T(8,128)(2,1)S(1)}, bf16[128,512]{1,0:T(8,128)(2,1)S(1)}, u32[]{:S(2)}, u32[]{:S(2)}) collective-permute-start(bf16[128,512]{1,0:T(8,128)(2,1)S(1)} %get-tuple-element.23), channel_id=1, source_target_pairs={{0,32},{1,33},{32,0},{33,1},{2,34},{3,35},{34,2},{35,3},{4,36},{5,... | collective-permute-start | bytes 393224 | tf_op jit(solution)/shard_map/ppermute | solution.py:296
  76.3 4.1 %collective-permute-done.5 = bf16[128,512]{1,0:T(8,128)(2,1)S(1)} collective-permute-done((bf16[128,512]{1,0:T(8,128)(2,1)S(1)}, bf16[128,512]{1,0:T(8,128)(2,1)S(1)}, u32[]{:S(2)}, u32[]{:S(2)}) %collective-permute-start.5) | collective-permute-done | bytes 131104 | tf_op jit(solution)/shard_map/ppermute | solution.py:296
  80.4 0.0 collective-permute-done.6
  80.4 2.6 %collective-permute-done.2 = bf16[128,512]{1,0:T(8,128)(2,1)S(1)} collective-permute-done((bf16[128,512]{1,0:T(8,128)(2,1)S(1)}, bf16[128,512]{1,0:T(8,128)(2,1)S(1)}, u32[]{:S(2)}, u32[]{:S(2)}) %collective-permute-start.2) | collective-permute-done | bytes 131104 | tf_op jit(solution)/shard_map/ppermute | solution.py:296
  83.0 0.7 multiply_convert_fusion
  83.7 0.0 all-to-all-done.1.parts
  83.7 0.7 finish.1
Async XLA Ops:
  2.3 7.3 %copy-start = (bf16[128,512]{1,0:T(8,128)(2,1)S(1)}, bf16[128,512]{1,0:T(8,128)(2,1)}, u32[]{:S(2)}) copy-start(bf16[128,512]{1,0:T(8,128)(2,1)} %q_ref.1) | copy-start | bytes 393220
  2.3 7.3 %copy-start.1 = (bf16[128,512]{1,0:T(8,128)(2,1)S(1)}, bf16[128,512]{1,0:T(8,128)(2,1)}, u32[]{:S(2)}) copy-start(bf16[128,512]{1,0:T(8,128)(2,1)} %d_ref.1) | copy-start | bytes 393220
  2.3 7.3 %copy-start.2 = (bf16[128,512]{1,0:T(8,128)(2,1)S(1)}, bf16[128,512]{1,0:T(8,128)(2,1)}, u32[]{:S(2)}) copy-start(bf16[128,512]{1,0:T(8,128)(2,1)} %o_ref.1) | copy-start | bytes 393220
  2.3 7.3 %copy-start.3 = (f32[128,4]{0,1:T(4,128)S(1)}, f32[128,4]{0,1:T(4,128)}, u32[]{:S(2)}) copy-start(f32[128,4]{0,1:T(4,128)} %param.14) | copy-start | bytes 6148
  2.3 24.7 %all-to-all-start = ((bf16[8,128,256]{2,1,0:T(8,128)(2,1)}), bf16[8,128,256]{2,1,0:T(8,128)(2,1)S(1)}, u32[]{:S(2)}, u32[]{:S(2)}) async-start(bf16[8,128,256]{2,1,0:T(8,128)(2,1)} %broadcast_in_dim.2), calls=%async_computation | async-start | bytes 1048576 | tf_op jit(solution)/shard_map/all_to_all | solution.py:302
  9.7 23.6 %collective-permute-start.3 = (bf16[136,1024]{1,0:T(8,128)(2,1)S(1)}, bf16[136,1024]{1,0:T(8,128)(2,1)S(1)}, u32[]{:S(2)}, u32[]{:S(2)}) collective-permute-start(bf16[136,1024]{1,0:T(8,128)(2,1)S(1)} %pack.1.refs_1_), channel_id=1, source_target_pairs={{0,1},{1,0},{32,33},{33,32},{2,3},{3,2},{34,35},{35,34},{4,5},{5,4... | collective-permute-start | bytes 835592 | tf_op jit(solution)/shard_map/ppermute | solution.py:296
  27.0 8.3 %copy-start.4 = (s32[3,3]{1,0:T(4,128)S(1)}, s32[3,3]{1,0:T(4,128)}, u32[]{:S(2)}) copy-start(s32[3,3]{1,0:T(4,128)} %table.1) | copy-start | bytes 112
  27.0 18.0 %collective-permute-start.1 = (bf16[1024,256]{1,0:T(8,128)(2,1)S(1)}, bf16[1024,256]{1,0:T(8,128)(2,1)S(1)}, u32[]{:S(2)}, u32[]{:S(2)}) collective-permute-start(bf16[1024,256]{1,0:T(8,128)(2,1)S(1)} %bitcast.5), channel_id=1, source_target_pairs={{0,16},{16,0},{1,17},{17,1},{2,18},{18,2},{3,19},{19,3},{4,20},{20... | collective-permute-start | bytes 1572872 | tf_op jit(solution)/shard_map/ppermute | solution.py:299
  29.1 11.8 %collective-permute-start = (bf16[136,1024]{1,0:T(8,128)(2,1)S(1)}, bf16[136,1024]{1,0:T(8,128)(2,1)S(1)}, u32[]{:S(2)}, u32[]{:S(2)}) collective-permute-start(bf16[136,1024]{1,0:T(8,128)(2,1)S(1)} %pack.1.refs_1_), channel_id=1, source_target_pairs={{0,32},{1,33},{32,0},{33,1},{2,34},{3,35},{34,2},{35,3},{4,36},{5,... | collective-permute-start | bytes 835592 | tf_op jit(solution)/shard_map/ppermute | solution.py:296
  33.4 16.0 %collective-permute-start.4 = (bf16[136,1024]{1,0:T(8,128)(2,1)S(1)}, bf16[136,1024]{1,0:T(8,128)(2,1)S(1)}, u32[]{:S(2)}, u32[]{:S(2)}) collective-permute-start(bf16[136,1024]{1,0:T(8,128)(2,1)S(1)} %collective-permute-done.3.refs_1_), channel_id=1, source_target_pairs={{0,32},{1,33},{32,0},{33,1},{2,34},{3,35},{34,2},{35,3},{4,36},{5,... | collective-permute-start | bytes 835592 | tf_op jit(solution)/shard_map/ppermute | solution.py:296
  53.6 6.3 %collective-permute-start.7 = (bf16[1024,256]{1,0:T(8,128)(2,1)S(1)}, bf16[1024,256]{1,0:T(8,128)(2,1)S(1)}, u32[]{:S(2)}, u32[]{:S(2)}) collective-permute-start(bf16[1024,256]{1,0:T(8,128)(2,1)S(1)} %get-tuple-element.30), channel_id=1, source_target_pairs={{0,16},{16,0},{1,17},{17,1},{2,18},{18,2},{3,19},{19,3},{4,20},{20... | collective-permute-start | bytes 1572872 | tf_op jit(solution)/shard_map/ppermute | solution.py:299
  60.8 22.9 %all-to-all-start.1 = ((bf16[8,128,256]{2,1,0:T(8,128)(2,1)}), bf16[8,128,256]{2,1,0:T(8,128)(2,1)S(1)}, u32[]{:S(2)}, u32[]{:S(2)}) async-start(bf16[8,128,256]{2,1,0:T(8,128)(2,1)} %bitcast.4), calls=%async_computation.1 | async-start | bytes 1048576 | tf_op jit(solution)/shard_map/all_to_all | solution.py:302
  64.3 16.1 %collective-permute-start.5 = (bf16[128,512]{1,0:T(8,128)(2,1)S(1)}, bf16[128,512]{1,0:T(8,128)(2,1)S(1)}, u32[]{:S(2)}, u32[]{:S(2)}) collective-permute-start(bf16[128,512]{1,0:T(8,128)(2,1)S(1)} %get-tuple-element.27), channel_id=1, source_target_pairs={{0,1},{1,0},{32,33},{33,32},{2,3},{3,2},{34,35},{35,34},{4,5},{5,4... | collective-permute-start | bytes 393224 | tf_op jit(solution)/shard_map/ppermute | solution.py:296
  70.4 10.0 %collective-permute-start.6 = (bf16[128,512]{1,0:T(8,128)(2,1)S(1)}, bf16[128,512]{1,0:T(8,128)(2,1)S(1)}, u32[]{:S(2)}, u32[]{:S(2)}) collective-permute-start(bf16[128,512]{1,0:T(8,128)(2,1)S(1)} %get-tuple-element.28), channel_id=1, source_target_pairs={{0,33},{1,32},{32,1},{33,0},{2,35},{3,34},{34,3},{35,2},{4,37},{5,... | collective-permute-start | bytes 393224 | tf_op jit(solution)/shard_map/ppermute | solution.py:296
  73.8 9.2 %collective-permute-start.2 = (bf16[128,512]{1,0:T(8,128)(2,1)S(1)}, bf16[128,512]{1,0:T(8,128)(2,1)S(1)}, u32[]{:S(2)}, u32[]{:S(2)}) collective-permute-start(bf16[128,512]{1,0:T(8,128)(2,1)S(1)} %get-tuple-element.23), channel_id=1, source_target_pairs={{0,32},{1,33},{32,0},{33,1},{2,34},{3,35},{34,2},{35,3},{4,36},{5,... | collective-permute-start | bytes 393224 | tf_op jit(solution)/shard_map/ppermute | solution.py:296

commit v8 on v7

--- a/solution.py
+++ b/solution.py
@@ -15,7 +15,7 @@
 QUNITS = 2 * NZ
 KUNITS = NY * TOK // UNIT
 GROUP = 8
-PAR = 2
+PAR = 3
 MASKS = (0, 2, 1, 3)
 ROWS = HEADS * UNIT
 AXES = ("y", "zlo", "core", "x", "zhh", "zhl")
@@ -58,26 +58,44 @@
     def take(n):
         return [next(it) for _ in range(n)]
 
-    start, count, s, finals, raws, old_units, has_acc, spread_out = cfg
+    start, count, sets, given, finals, raws, old_units, export_q = cfg
+    q_given, k_given = given
+    spread_out = k_given
     tab = next(it)
-    msgs = take(count)
-    kv, kcode, qlim = take(3)
+    msgs = [] if q_given else take(count)
+    kvs = [] if k_given else take(len(sets))
+    kcode = None if k_given else next(it)
+    qlim = next(it)
+    q_parts = take(4) if q_given else None
+    k_parts = take(3) if k_given else None
     oldq = next(it) if old_units else None
-    old = next(it) if has_acc else None
+    old = next(it) if k_given else None
     gqs = take(len(finals))
     rawq = next(it) if raws else None
     out = next(it)
-    qs, ds, lse, delta, ks, kt, kc, gq, work = take(9)
+    if q_parts is None and export_q:
+        q_parts = take(4)
+    if k_parts is None:
+        k_parts = take(3)
+    if q_parts is None:
+        q_parts = take(4)
+    gq, work = take(2)
     acc = next(it) if spread_out else out
+    qs, ds, lse, delta = q_parts
+    ks, kt, kc = k_parts
     base = 2 * start
     units = 2 * count
     chunks = KUNITS // GROUP
+    keys = KUNITS * UNIT
+    span = GROUP * UNIT
+    chunk0 = sets[0] * chunks
     filled = jnp.int32(0)
-    for u in range(units):
-        for c in range(chunks):
-            work[filled] = c * units + u
-            active = c * GROUP < tab[2 * KUNITS + s * QUNITS + base + u, 0]
-            filled = filled + active.astype(jnp.int32)
+    for which, s in enumerate(sets):
+        for u in range(units):
+            for c in range(chunks):
+                work[filled] = (which * chunks + c) * units + u
+                active = c * GROUP < tab[2 + s, base + u]
+                filled = filled + active.astype(jnp.int32)
     rounds = (filled + PAR - 1) // PAR
     for a, m in enumerate(msgs):
         meta = m[TOK : TOK + 8, :].astype(f32)
@@ -92,24 +110,28 @@
             for ref, first in ((lse, 0), (delta, WIDE)):
                 cuts = [first + h * TOK + half * UNIT for h in range(HEADS)]
                 ref[u] = jnp.concatenate([meta[:, c : c + UNIT] for c in cuts], axis=1)
-    gq[...] = jnp.zeros_like(gq)
-    if oldq is not None:
-        gq[:old_units] = oldq[...]
-    acc[...] = jnp.zeros_like(acc) if old is None else old[...]
+    gq[...] = jnp.zeros_like(gq) if oldq is None else oldq[...]
+    if old is None:
+        acc[...] = jnp.zeros_like(acc)
+    else:
+        acc[...] = old[sets[0] * keys : (sets[0] + 1) * keys, :]
     spots = []
-    for b in range(NY):
-        row = kcode[s * NY + b : s * NY + b + 1, :]
-        wide = jnp.broadcast_to(row, (TOK, TOK)).T
-        for half in range(2):
-            i = half * NY + b
-            spot = pl.multiple_of(tab[s * KUNITS + i, 0] * UNIT, UNIT)
-            nat = slice(b * TOK + half * UNIT, b * TOK + (half + 1) * UNIT)
-            spots.append((nat, spot))
-            ks[pl.ds(spot, UNIT), :] = kv[nat, :]
-            kc[pl.ds(spot, UNIT), :] = wide[half * UNIT : (half + 1) * UNIT]
-    span = GROUP * UNIT
-    for c in range(chunks):
-        kt[c] = ks[c * span : (c + 1) * span, :DIM].astype(f32).T.astype(bf16)
+    for which, s in enumerate(sets):
+        for b in range(NY):
+            if not k_given:
+                row = kcode[s * NY + b : s * NY + b + 1, :]
+                wide = jnp.broadcast_to(row, (TOK, TOK)).T
+            for half in range(2):
+                at = tab[s, half * NY + b] + which * KUNITS
+                spot = pl.multiple_of(at * UNIT, UNIT)
+                nat = slice(b * TOK + half * UNIT, b * TOK + (half + 1) * UNIT)
+                spots.append((nat, spot))
+                if not k_given:
+                    ks[pl.ds(spot, UNIT), :] = kvs[which][nat, :]
+                    kc[pl.ds(spot, UNIT), :] = wide[half * UNIT : (half + 1) * UNIT]
+    if not k_given:
+        for c in range(chunks * len(sets)):
+            kt[c] = ks[c * span : (c + 1) * span, :DIM].astype(f32).T.astype(bf16)
     score_scale = DIM ** (-0.5)
 
     def item(index):
@@ -117,11 +139,12 @@
         u = code % units
         c = code // units
         spot = pl.ds(pl.multiple_of(c * span, span), span)
-        keys, vals = ks[spot, :DIM], ks[spot, DIM:]
+        where_ = pl.ds(pl.multiple_of((chunk0 + c) * span, span), span)
+        keys, vals = ks[where_, :DIM], ks[where_, DIM:]
         at = pl.ds(pl.multiple_of(u * ROWS, ROWS), ROWS)
         q, d = qs[at, :], ds[at, :]
         probs = jnp.exp(nt(keys, q) * score_scale - lse[u])
-        kcodes = kc[spot, :]
+        kcodes = kc[where_, :]
         mod, pos = kcodes & 3, kcodes >> 2
         lim = jnp.where(index < filled, qlim[base + u], -1)
         bands = []
@@ -134,7 +157,7 @@
         glow = grads.astype(bf16)
         acc[spot, DIM:] += nn(plow, d)
         acc[spot, :DIM] += nn(glow, q)
-        gq[u] += nn(kt[c], glow)
+        gq[u] += nn(kt[chunk0 + c], glow)
 
     def body(r, _):
         for j in range(PAR):
@@ -160,33 +183,44 @@
     return pltpu.with_memory_space_constraint(value, pltpu.VMEM)
 
 
-def tile(tab, start, msgs, kv, kcode, qlim, s, finals=(), raws=None, oldq=None, old=None, out_type=None):
-    count = len(msgs)
+def tile(tab, start, sets, qlim, msgs=(), kvs=(), kcode=None, q_parts=None, k_parts=None, finals=(),
+         raws=None, oldq=None, old=None, out_type=f32, export_q=False):
+    count = q_parts[2].shape[0] // 2 if q_parts is not None else len(msgs)
     units = 2 * count
-    keys = KUNITS * UNIT
+    keys = len(sets) * KUNITS * UNIT
     smem = pl.BlockSpec(memory_space=pltpu.SMEM)
     vmem = pl.BlockSpec(memory_space=pltpu.VMEM)
-    arrays = [*msgs, kv, kcode, qlim] + [v for v in (oldq, old) if v is not None]
-    outs = [pltpu.VMEM((TOK, WIDE), t) for _, t in finals]
-    if raws:
-        outs.append(pltpu.VMEM((raws[1] - raws[0], DIM, ROWS), f32))
-    outs.append(pltpu.VMEM((keys, 2 * DIM), out_type or f32))
-    scratch = [
+    arrays = [*msgs, *kvs] + ([] if kcode is None else [kcode]) + [qlim]
+    arrays += [*(q_parts or ()), *(k_parts or ())] + [v for v in (oldq, old) if v is not None]
+    q_shapes = [
         pltpu.VMEM((units * ROWS, DIM), bf16),
         pltpu.VMEM((units * ROWS, DIM), bf16),
         pltpu.VMEM((units, 1, ROWS), f32),
         pltpu.VMEM((units, 1, ROWS), f32),
+    ]
+    k_shapes = [
         pltpu.VMEM((keys, 2 * DIM), bf16),
-        pltpu.VMEM((KUNITS // GROUP, DIM, GROUP * UNIT), bf16),
+        pltpu.VMEM((keys // (GROUP * UNIT), DIM, GROUP * UNIT), bf16),
         pltpu.VMEM((keys, DIM), jnp.int32),
+    ]
+    outs = [pltpu.VMEM((TOK, WIDE), t) for _, t in finals]
+    if raws:
+        outs.append(pltpu.VMEM((raws[1] - raws[0], DIM, ROWS), f32))
+    outs.append(pltpu.VMEM((keys, 2 * DIM), out_type))
+    if q_parts is None and export_q:
+        outs += q_shapes
+    if k_parts is None:
+        outs += k_shapes
+    scratch = [
         pltpu.VMEM((units, DIM, ROWS), f32),
-        pltpu.SMEM((units * (KUNITS // GROUP) + 1,), jnp.int32),
+        pltpu.SMEM((units * len(sets) * (KUNITS // GROUP) + 1,), jnp.int32),
     ]
-    if out_type:
+    if q_parts is None and not export_q:
+        scratch = q_shapes + scratch
+    if k_parts is not None:
         scratch.append(pltpu.VMEM((keys, 2 * DIM), f32))
-    cfg = (
-        start, count, s, finals, raws, 0 if oldq is None else oldq.shape[0], old is not None, out_type is not None
-    )
+    given = (q_parts is not None, k_parts is not None)
+    cfg = (start, count, sets, given, finals, raws, 0 if oldq is None else units, export_q)
 
     def body(*refs):
         tile_kernel(cfg, *refs)
@@ -239,7 +273,8 @@
     qlast = jnp.concatenate(
         [high[half][a : a + 1] for a in range(NZ) for half in range(2)], axis=0
     )
-    qlast = jnp.broadcast_to(qlast, (QUNITS, TOK)) >> 6
+    qlast = jnp.concatenate([qlast, jnp.zeros((TOK - QUNITS, 1), jnp.int32)], axis=0)
+    qlast = jnp.broadcast_to(qlast, (TOK, TOK)).T[:KUNITS] >> 6
     lane = lax.broadcasted_iota(jnp.int32, (KUNITS, TOK), 1)
     index = lax.broadcasted_iota(jnp.int32, (KUNITS, TOK), 0)
     for s in range(2):
@@ -247,13 +282,10 @@
         column = jnp.broadcast_to(jnp.concatenate([low[0][part], low[1][part]], axis=0), (KUNITS, TOK))
         square = jnp.concatenate([column, jnp.zeros((TOK - KUNITS, TOK), jnp.int32)], axis=0).T
         across = square[:KUNITS]
-        before = ((across < column) | ((across == column) & (lane < index))) & (lane < KUNITS)
-        rank = jnp.sum(before.astype(jnp.int32), axis=1, keepdims=True)
-        tab[s * KUNITS : (s + 1) * KUNITS, :] = jnp.broadcast_to(rank, (KUNITS, TOK))
-        seen = ((across[:QUNITS] >> 6) <= qlast) & (lane[:QUNITS] < KUNITS)
-        need = jnp.sum(seen.astype(jnp.int32), axis=1, keepdims=True)
-        at = 2 * KUNITS + s * QUNITS
-        tab[at : at + QUNITS, :] = jnp.broadcast_to(need, (QUNITS, TOK))
+        before = (column < across) | ((column == across) & (index < lane))
+        tab[s : s + 1, :] = jnp.sum(before.astype(jnp.int32), axis=0, keepdims=True)
+        seen = (column >> 6) <= qlast
+        tab[2 + s : 3 + s, :] = jnp.sum(seen.astype(jnp.int32), axis=0, keepdims=True)
     qpos, qmod = pos[keys:], mod[keys:]
     for m in range(3):
         bid = jnp.where(qmod == 0, table[0, m], jnp.where(qmod == 1, table[1, m], table[2, m]))
@@ -274,7 +306,7 @@
         in_specs=[pl.BlockSpec(memory_space=pltpu.SMEM), hbm, hbm],
         out_specs=[vmem] * 3,
         out_shape=[
-            jax.ShapeDtypeStruct((2 * KUNITS + 2 * QUNITS, TOK), jnp.int32),
+            jax.ShapeDtypeStruct((4, TOK), jnp.int32),
             pltpu.VMEM((2 * NY, TOK), jnp.int32),
             pltpu.VMEM((QUNITS, 3, ROWS), jnp.int32),
         ],
@@ -312,12 +344,17 @@
     tab, kcode, qlim = plan(position, modality, table)
     kvx = other_core(kvo)
     last = along_z(far, 2)
-    raw_near, old_own = tile(tab, 0, (msg, near), kvo, kcode, qlim, 0, raws=(0, 4))
-    own_q, near_q, old_oth = tile(tab, 0, (msg, near), kvx, kcode, qlim, 1, ((0, f32), (1, bf16)), None, raw_near)
-    raw_far, gkvx = tile(tab, 2, (far, last), kvx, kcode, qlim, 1, (), (0, 4), None, old_oth, bf16)
+    own_q, near_q, old, *k_parts = tile(
+        tab, 0, (0, 1), qlim, (msg, near), (kvo, kvx), kcode, finals=((0, f32), (1, bf16))
+    )
+    raw_far, gkvx, *q_parts = tile(
+        tab, 2, (1,), qlim, (far, last), k_parts=k_parts, raws=(0, 4), old=old, out_type=bf16,
+        export_q=True,
+    )
     got = other_core(gkvx)
     far_q, last_q, gkvo = tile(
-        tab, 2, (far, last), kvo, kcode, qlim, 0, ((0, bf16), (1, bf16)), None, raw_far, old_own, f32
+        tab, 2, (0,), qlim, q_parts=q_parts, k_parts=k_parts, finals=((0, bf16), (1, bf16)),
+        oldq=raw_far, old=old,
     )
     paired = (gkvo + got.astype(f32)).astype(bf16).reshape(NY, TOK, 2 * DIM)
     summed = over_y(paired)

time: 86 us -> 84.2 us (0.979)
  local copies, waits for them, and re-layouts: 0.86 us -> 4.23 us
  Pallas kernels: 20.3 us -> 17.6 us
  waiting for transfers between devices: 21.1 us -> 19.1 us
    unnamed x10, local copies, waits for them, and re-layouts: 0.02 us -> 3.39 us
    all_to_all x2, waiting for transfers between devices: 11.2 us -> 7.82 us  [over_y(): return lax.all_to_all(value, 'y', 0, 0)]
    pallas_call x4 -> x3, Pallas kernels: 17.1 us -> 14.5 us  [tile(): pl.pallas_call(body, in_specs=[smem] + [vmem] * len(arrays), out_specs=[v...]
    ppermute x6, waiting for transfers between devices: 9.95 us -> 11.3 us  [along_z(): lax.ppermute(value, ('zlo', 'zhl'), [(i, i ^ mask) for i in range(NZ)])]
  transfers between devices with their start and end apart: 10 -> 10, of which waited for: 4 -> 3; matrix products, arithmetic and copies ran while one was open for 1% -> 1% of each run, Pallas kernels for 18% -> 16%
where the time goes in v8:
time: 84.2 us; the launch traced here: 82.9 us
  starting transfers between devices  38.7 us (46%)
  waiting for transfers between devices  19.1 us (23%)
  Pallas kernels  17.6 us (21%)
  local copies, waits for them, and re-layouts  4.23 us (5%)
  other arithmetic  2.47 us (3%)
    ppermute x6, starting transfers between devices, along_z(): lax.ppermute(value, ('zlo', 'zhl'), [(i, i ^ mask) for i in range(NZ)])  23.9 us
    pallas_call x3, Pallas kernels, tile(): pl.pallas_call(body, in_specs=[smem] + [vmem] * len(arrays), out_specs=[v...  14.5 us
    ppermute x6, waiting for transfers between devices, along_z(): lax.ppermute(value, ('zlo', 'zhl'), [(i, i ^ mask) for i in range(NZ)])  11.3 us
    all_to_all x2, starting transfers between devices, over_y(): return lax.all_to_all(value, 'y', 0, 0)  10.9 us
    all_to_all x2, waiting for transfers between devices, over_y(): return lax.all_to_all(value, 'y', 0, 0)  7.82 us
    ppermute x2, starting transfers between devices, other_core(): return lax.ppermute(value, 'core', [(0, 1), (1, 0)])  3.83 us
    unnamed x10, local copies, waits for them, and re-layouts  3.39 us
    pallas_call x1, Pallas kernels, plan(): pl.pallas_call(plan_kernel, in_specs=[pl.BlockSpec(memory_space=pltpu.SME...  2.19 us
  transfers between devices with their start and end apart: 10, of which 3 were waited for; matrix products, arithmetic and copies ran while one was open for 1% of the time, Pallas kernels for 16%

profile of v8, /device:TPU:6, one launch (start us, length us, event | category | flops | bytes accessed | tf_op | source)
XLA Modules:
  0.0 82.9 jit_solution(8894998636374448776)
XLA Ops:
  0.6 0.0 copy-start.4
  0.6 0.8 pad_maximum_fusion
  1.4 0.8 %broadcast_in_dim.2 = bf16[8,128,256]{2,1,0:T(8,128)(2,1)} broadcast(bf16[128,256]{1,0:T(8,128)(2,1)S(1)} %pad_maximum_fusion), dimensions={1,2} | broadcast | bytes 589824 | tf_op jit(solution)/shard_map/broadcast_in_dim | solution.py:337
  2.3 7.1 %all-to-all-start = ((bf16[8,128,256]{2,1,0:T(8,128)(2,1)}), bf16[8,128,256]{2,1,0:T(8,128)(2,1)S(1)}, u32[]{:S(2)}, u32[]{:S(2)}) async-start(bf16[8,128,256]{2,1,0:T(8,128)(2,1)} %broadcast_in_dim.2), calls=%async_computation | async-start | bytes 1048576 | tf_op jit(solution)/shard_map/all_to_all | solution.py:334
  9.4 0.0 copy-start
  9.4 0.9 %copy-done = bf16[128,512]{1,0:T(8,128)(2,1)S(1)} copy-done((bf16[128,512]{1,0:T(8,128)(2,1)S(1)}, bf16[128,512]{1,0:T(8,128)(2,1)}, u32[]{:S(2)}) %copy-start) | copy-done | bytes 131096
  10.3 0.0 copy-start.1
  10.3 0.9 %copy-done.1 = bf16[128,512]{1,0:T(8,128)(2,1)S(1)} copy-done((bf16[128,512]{1,0:T(8,128)(2,1)S(1)}, bf16[128,512]{1,0:T(8,128)(2,1)}, u32[]{:S(2)}) %copy-start.1) | copy-done | bytes 131096
  11.2 0.0 copy-start.2
  11.2 0.9 %copy-done.2 = bf16[128,512]{1,0:T(8,128)(2,1)S(1)} copy-done((bf16[128,512]{1,0:T(8,128)(2,1)S(1)}, bf16[128,512]{1,0:T(8,128)(2,1)}, u32[]{:S(2)}) %copy-start.2) | copy-done | bytes 131096
  12.1 0.0 copy-start.3
  12.1 0.7 copy-done.3
  12.8 0.2 pack.1.refs_1_
  13.0 6.1 %collective-permute-start.3 = (bf16[136,1024]{1,0:T(8,128)(2,1)S(1)}, bf16[136,1024]{1,0:T(8,128)(2,1)S(1)}, u32[]{:S(2)}, u32[]{:S(2)}) collective-permute-start(bf16[136,1024]{1,0:T(8,128)(2,1)S(1)} %pack.1.refs_1_), channel_id=1, source_target_pairs={{0,1},{1,0},{32,33},{33,32},{2,3},{3,2},{34,35},{35,34},{4,5},{5,4... | collective-permute-start | bytes 835592 | tf_op jit(solution)/shard_map/ppermute | solution.py:328
  19.0 7.8 %all-to-all-done = bf16[8,128,256]{2,1,0:T(8,128)(2,1)S(1)} async-done(((bf16[8,128,256]{2,1,0:T(8,128)(2,1)}), bf16[8,128,256]{2,1,0:T(8,128)(2,1)S(1)}, u32[]{:S(2)}, u32[]{:S(2)}) %all-to-all-start) | async-done | bytes 524320 | tf_op jit(solution)/shard_map/all_to_all | solution.py:334
  26.9 1.9 %collective-permute-start.1 = (bf16[1024,256]{1,0:T(8,128)(2,1)S(1)}, bf16[1024,256]{1,0:T(8,128)(2,1)S(1)}, u32[]{:S(2)}, u32[]{:S(2)}) collective-permute-start(bf16[1024,256]{1,0:T(8,128)(2,1)S(1)} %bitcast.5), channel_id=1, source_target_pairs={{0,16},{16,0},{1,17},{17,1},{2,18},{18,2},{3,19},{19,3},{4,20},{20... | collective-permute-start | bytes 1572872 | tf_op jit(solution)/shard_map/ppermute | solution.py:331
  28.8 4.3 %collective-permute-start = (bf16[136,1024]{1,0:T(8,128)(2,1)S(1)}, bf16[136,1024]{1,0:T(8,128)(2,1)S(1)}, u32[]{:S(2)}, u32[]{:S(2)}) collective-permute-start(bf16[136,1024]{1,0:T(8,128)(2,1)S(1)} %pack.1.refs_1_), channel_id=1, source_target_pairs={{0,32},{1,33},{32,0},{33,1},{2,34},{3,35},{34,2},{35,3},{4,36},{5,... | collective-permute-start | bytes 835592 | tf_op jit(solution)/shard_map/ppermute | solution.py:328
  33.1 0.0 collective-permute-done.3.refs_1_
  33.1 1.9 %collective-permute-start.4 = (bf16[136,1024]{1,0:T(8,128)(2,1)S(1)}, bf16[136,1024]{1,0:T(8,128)(2,1)S(1)}, u32[]{:S(2)}, u32[]{:S(2)}) collective-permute-start(bf16[136,1024]{1,0:T(8,128)(2,1)S(1)} %collective-permute-done.3.refs_1_), channel_id=1, source_target_pairs={{0,32},{1,33},{32,0},{33,1},{2,34},{3,35},{34,2},{35,3},{4,36},{5,... | collective-permute-start | bytes 835592 | tf_op jit(solution)/shard_map/ppermute | solution.py:328
  35.0 0.0 copy-done.4
  35.0 2.2 %plan.1 = (s32[4,128]{1,0:T(4,128)S(1)}, s32[16,128]{1,0:T(8,128)S(1)}, s32[8,3,256]{2,1,0:T(4,128)S(1)}) custom-call(s32[3,3]{1,0:T(4,128)S(1)} %copy-done.4, s32[512,1,128]{2,1,0:T(1,128)} %bitcast.8, s32[512,1,128]{2,1,0:T(1,128)} %bitcast.9), custom_call_target="tpu_custom_call" | custom-call | tf_op jit(solution)/shard_map/plan/pallas_call | solution.py:304
  37.2 3.3 %collective-permute-done.refs_2_ = bf16[136,1024]{1,0:T(8,128)(2,1)S(1)} collective-permute-done((bf16[136,1024]{1,0:T(8,128)(2,1)S(1)}, bf16[136,1024]{1,0:T(8,128)(2,1)S(1)}, u32[]{:S(2)}, u32[]{:S(2)}) %collective-permute-start) | collective-permute-done | bytes 278560 | tf_op jit(solution)/shard_map/ppermute | solution.py:328
  40.6 0.0 collective-permute-done.1.refs_4_
  40.6 7.2 %shard_map.112 = (f32[128,512]{1,0:T(8,128)S(1)}, bf16[128,512]{1,0:T(8,128)(2,1)S(1)}, f32[2048,256]{1,0:T(8,128)S(1)}, bf16[2048,256]{1,0:T(8,128)(2,1)S(1)}, ...) custom-call(s32[4,128]{1,0:T(4,128)S(1)} %get-tuple-element.23.refs_0_, bf16[136,1024]{1,0:T(8,128)(2,1)S(1)} %pack.1.refs_1_, ...), custom_call_target="tpu_custom_call" | custom-call | tf_op jit(solution)/shard_map/pallas_call | solution.py:228
  47.8 0.0 collective-permute-done.4.refs_2_
  47.8 3.7 %shard_map.113 = (f32[4,128,256]{2,1,0:T(8,128)S(1)}, bf16[1024,256]{1,0:T(8,128)(2,1)S(1)}, bf16[1024,128]{1,0:T(8,128)(2,1)S(1)}, bf16[1024,128]{1,0:T(8,128)(...) custom-call(s32[4,128]{1,0:T(4,128)S(1)} %get-tuple-element.23.refs_0_, ...), custom_call_target="tpu_custom_call" | custom-call | tf_op jit(solution)/shard_map/pallas_call | solution.py:228
  51.5 1.9 %collective-permute-start.7 = (bf16[1024,256]{1,0:T(8,128)(2,1)S(1)}, bf16[1024,256]{1,0:T(8,128)(2,1)S(1)}, u32[]{:S(2)}, u32[]{:S(2)}) collective-permute-start(bf16[1024,256]{1,0:T(8,128)(2,1)S(1)} %get-tuple-element.40), channel_id=1, source_target_pairs={{0,16},{16,0},{1,17},{17,1},{2,18},{18,2},{3,19},{19,3},{4,20},{20... | collective-permute-start | bytes 1572872 | tf_op jit(solution)/shard_map/ppermute | solution.py:331
  53.4 3.7 %shard_map.114 = (bf16[128,512]{1,0:T(8,128)(2,1)S(1)}, bf16[128,512]{1,0:T(8,128)(2,1)S(1)}, f32[1024,256]{1,0:T(8,128)S(1)}) custom-call(s32[4,128]{1,0:T(4,128)S(1)} %get-tuple-element.23.refs_0_, s32[8,3,256]{2,1,0:T(4,128)S(1)} %get-tuple-element.25.refs_6_.refs_3_.refs_1_, bf16[1024,128]{1,0:T(8,128)(2,1)S(1)} %get-tuple-element.32.refs_2_, ...), custom_call_target="tpu_custom_call" | custom-call | tf_op jit(solution)/shard_map/pallas_call | solution.py:228
  57.1 0.0 collective-permute-done.7
  57.1 0.9 %add_convert_fusion = bf16[1024,256]{1,0:T(8,128)(2,1)} fusion(f32[1024,256]{1,0:T(8,128)S(1)} %get-tuple-element.39, bf16[1024,256]{1,0:T(8,128)(2,1)S(1)} %collective-permute-done.7), kind=kLoop, calls=%fused_computation | loop fusion | flops 786432 | bytes 2097152 | tf_op jit(solution)/shard_map/convert_element_type | solution.py:359
  58.0 3.8 %all-to-all-start.1 = ((bf16[8,128,256]{2,1,0:T(8,128)(2,1)}), bf16[8,128,256]{2,1,0:T(8,128)(2,1)S(1)}, u32[]{:S(2)}, u32[]{:S(2)}) async-start(bf16[8,128,256]{2,1,0:T(8,128)(2,1)} %bitcast.4), calls=%async_computation.1 | async-start | bytes 1048576 | tf_op jit(solution)/shard_map/all_to_all | solution.py:334
  61.8 3.6 %collective-permute-start.2 = (bf16[128,512]{1,0:T(8,128)(2,1)S(1)}, bf16[128,512]{1,0:T(8,128)(2,1)S(1)}, u32[]{:S(2)}, u32[]{:S(2)}) collective-permute-start(bf16[128,512]{1,0:T(8,128)(2,1)S(1)} %get-tuple-element.27), channel_id=1, source_target_pairs={{0,32},{1,33},{32,0},{33,1},{2,34},{3,35},{34,2},{35,3},{4,36},{5,... | collective-permute-start | bytes 393224 | tf_op jit(solution)/shard_map/ppermute | solution.py:328
  65.5 6.1 %collective-permute-start.5 = (bf16[128,512]{1,0:T(8,128)(2,1)S(1)}, bf16[128,512]{1,0:T(8,128)(2,1)S(1)}, u32[]{:S(2)}, u32[]{:S(2)}) collective-permute-start(bf16[128,512]{1,0:T(8,128)(2,1)S(1)} %get-tuple-element.37), channel_id=1, source_target_pairs={{0,1},{1,0},{32,33},{33,32},{2,3},{3,2},{34,35},{35,34},{4,5},{5,4... | collective-permute-start | bytes 393224 | tf_op jit(solution)/shard_map/ppermute | solution.py:328
  71.6 1.9 %collective-permute-start.6 = (bf16[128,512]{1,0:T(8,128)(2,1)S(1)}, bf16[128,512]{1,0:T(8,128)(2,1)S(1)}, u32[]{:S(2)}, u32[]{:S(2)}) collective-permute-start(bf16[128,512]{1,0:T(8,128)(2,1)S(1)} %get-tuple-element.38), channel_id=1, source_target_pairs={{0,33},{1,32},{32,1},{33,0},{2,35},{3,34},{34,3},{35,2},{4,37},{5,... | collective-permute-start | bytes 393224 | tf_op jit(solution)/shard_map/ppermute | solution.py:328
  73.5 0.0 collective-permute-done.2
  73.5 8.0 %collective-permute-done.5 = bf16[128,512]{1,0:T(8,128)(2,1)S(1)} collective-permute-done((bf16[128,512]{1,0:T(8,128)(2,1)S(1)}, bf16[128,512]{1,0:T(8,128)(2,1)S(1)}, u32[]{:S(2)}, u32[]{:S(2)}) %collective-permute-start.5) | collective-permute-done | bytes 131104 | tf_op jit(solution)/shard_map/ppermute | solution.py:328
  81.5 0.0 collective-permute-done.6
  81.5 0.7 multiply_convert_fusion
  82.2 0.0 all-to-all-done.1.parts
  82.2 0.7 finish.1
Async XLA Ops:
  0.6 34.4 %copy-start.4 = (s32[3,3]{1,0:T(4,128)S(1)}, s32[3,3]{1,0:T(4,128)}, u32[]{:S(2)}) copy-start(s32[3,3]{1,0:T(4,128)} %table.1) | copy-start | bytes 112
  2.3 24.6 %all-to-all-start = ((bf16[8,128,256]{2,1,0:T(8,128)(2,1)}), bf16[8,128,256]{2,1,0:T(8,128)(2,1)S(1)}, u32[]{:S(2)}, u32[]{:S(2)}) async-start(bf16[8,128,256]{2,1,0:T(8,128)(2,1)} %broadcast_in_dim.2), calls=%async_computation | async-start | bytes 1048576 | tf_op jit(solution)/shard_map/all_to_all | solution.py:334
  9.4 0.9 %copy-start = (bf16[128,512]{1,0:T(8,128)(2,1)S(1)}, bf16[128,512]{1,0:T(8,128)(2,1)}, u32[]{:S(2)}) copy-start(bf16[128,512]{1,0:T(8,128)(2,1)} %q_ref.1) | copy-start | bytes 393220
  10.3 0.9 %copy-start.1 = (bf16[128,512]{1,0:T(8,128)(2,1)S(1)}, bf16[128,512]{1,0:T(8,128)(2,1)}, u32[]{:S(2)}) copy-start(bf16[128,512]{1,0:T(8,128)(2,1)} %d_ref.1) | copy-start | bytes 393220
  11.2 0.9 %copy-start.2 = (bf16[128,512]{1,0:T(8,128)(2,1)S(1)}, bf16[128,512]{1,0:T(8,128)(2,1)}, u32[]{:S(2)}) copy-start(bf16[128,512]{1,0:T(8,128)(2,1)} %o_ref.1) | copy-start | bytes 393220
  12.1 0.7 copy-start.3
  13.0 20.1 %collective-permute-start.3 = (bf16[136,1024]{1,0:T(8,128)(2,1)S(1)}, bf16[136,1024]{1,0:T(8,128)(2,1)S(1)}, u32[]{:S(2)}, u32[]{:S(2)}) collective-permute-start(bf16[136,1024]{1,0:T(8,128)(2,1)S(1)} %pack.1.refs_1_), channel_id=1, source_target_pairs={{0,1},{1,0},{32,33},{33,32},{2,3},{3,2},{34,35},{35,34},{4,5},{5,4... | collective-permute-start | bytes 835592 | tf_op jit(solution)/shard_map/ppermute | solution.py:328
  26.9 13.7 %collective-permute-start.1 = (bf16[1024,256]{1,0:T(8,128)(2,1)S(1)}, bf16[1024,256]{1,0:T(8,128)(2,1)S(1)}, u32[]{:S(2)}, u32[]{:S(2)}) collective-permute-start(bf16[1024,256]{1,0:T(8,128)(2,1)S(1)} %bitcast.5), channel_id=1, source_target_pairs={{0,16},{16,0},{1,17},{17,1},{2,18},{18,2},{3,19},{19,3},{4,20},{20... | collective-permute-start | bytes 1572872 | tf_op jit(solution)/shard_map/ppermute | solution.py:331
  28.8 11.8 %collective-permute-start = (bf16[136,1024]{1,0:T(8,128)(2,1)S(1)}, bf16[136,1024]{1,0:T(8,128)(2,1)S(1)}, u32[]{:S(2)}, u32[]{:S(2)}) collective-permute-start(bf16[136,1024]{1,0:T(8,128)(2,1)S(1)} %pack.1.refs_1_), channel_id=1, source_target_pairs={{0,32},{1,33},{32,0},{33,1},{2,34},{3,35},{34,2},{35,3},{4,36},{5,... | collective-permute-start | bytes 835592 | tf_op jit(solution)/shard_map/ppermute | solution.py:328
  33.1 14.7 %collective-permute-start.4 = (bf16[136,1024]{1,0:T(8,128)(2,1)S(1)}, bf16[136,1024]{1,0:T(8,128)(2,1)S(1)}, u32[]{:S(2)}, u32[]{:S(2)}) collective-permute-start(bf16[136,1024]{1,0:T(8,128)(2,1)S(1)} %collective-permute-done.3.refs_1_), channel_id=1, source_target_pairs={{0,32},{1,33},{32,0},{33,1},{2,34},{3,35},{34,2},{35,3},{4,36},{5,... | collective-permute-start | bytes 835592 | tf_op jit(solution)/shard_map/ppermute | solution.py:328
  51.5 5.6 %collective-permute-start.7 = (bf16[1024,256]{1,0:T(8,128)(2,1)S(1)}, bf16[1024,256]{1,0:T(8,128)(2,1)S(1)}, u32[]{:S(2)}, u32[]{:S(2)}) collective-permute-start(bf16[1024,256]{1,0:T(8,128)(2,1)S(1)} %get-tuple-element.40), channel_id=1, source_target_pairs={{0,16},{16,0},{1,17},{17,1},{2,18},{18,2},{3,19},{19,3},{4,20},{20... | collective-permute-start | bytes 1572872 | tf_op jit(solution)/shard_map/ppermute | solution.py:331
  58.0 24.2 %all-to-all-start.1 = ((bf16[8,128,256]{2,1,0:T(8,128)(2,1)}), bf16[8,128,256]{2,1,0:T(8,128)(2,1)S(1)}, u32[]{:S(2)}, u32[]{:S(2)}) async-start(bf16[8,128,256]{2,1,0:T(8,128)(2,1)} %bitcast.4), calls=%async_computation.1 | async-start | bytes 1048576 | tf_op jit(solution)/shard_map/all_to_all | solution.py:334
  61.8 11.7 %collective-permute-start.2 = (bf16[128,512]{1,0:T(8,128)(2,1)S(1)}, bf16[128,512]{1,0:T(8,128)(2,1)S(1)}, u32[]{:S(2)}, u32[]{:S(2)}) collective-permute-start(bf16[128,512]{1,0:T(8,128)(2,1)S(1)} %get-tuple-element.27), channel_id=1, source_target_pairs={{0,32},{1,33},{32,0},{33,1},{2,34},{3,35},{34,2},{35,3},{4,36},{5,... | collective-permute-start | bytes 393224 | tf_op jit(solution)/shard_map/ppermute | solution.py:328
  65.5 16.0 %collective-permute-start.5 = (bf16[128,512]{1,0:T(8,128)(2,1)S(1)}, bf16[128,512]{1,0:T(8,128)(2,1)S(1)}, u32[]{:S(2)}, u32[]{:S(2)}) collective-permute-start(bf16[128,512]{1,0:T(8,128)(2,1)S(1)} %get-tuple-element.37), channel_id=1, source_target_pairs={{0,1},{1,0},{32,33},{33,32},{2,3},{3,2},{34,35},{35,34},{4,5},{5,4... | collective-permute-start | bytes 393224 | tf_op jit(solution)/shard_map/ppermute | solution.py:328
  71.6 9.9 %collective-permute-start.6 = (bf16[128,512]{1,0:T(8,128)(2,1)S(1)}, bf16[128,512]{1,0:T(8,128)(2,1)S(1)}, u32[]{:S(2)}, u32[]{:S(2)}) collective-permute-start(bf16[128,512]{1,0:T(8,128)(2,1)S(1)} %get-tuple-element.38), channel_id=1, source_target_pairs={{0,33},{1,32},{32,1},{33,0},{2,35},{3,34},{34,3},{35,2},{4,37},{5,... | collective-permute-start | bytes 393224 | tf_op jit(solution)/shard_map/ppermute | solution.py:328

commit v9 on v8

--- a/solution.py
+++ b/solution.py
@@ -344,17 +344,18 @@
     tab, kcode, qlim = plan(position, modality, table)
     kvx = other_core(kvo)
     last = along_z(far, 2)
-    own_q, near_q, old, *k_parts = tile(
-        tab, 0, (0, 1), qlim, (msg, near), (kvo, kvx), kcode, finals=((0, f32), (1, bf16))
-    )
-    raw_far, gkvx, *q_parts = tile(
-        tab, 2, (1,), qlim, (far, last), k_parts=k_parts, raws=(0, 4), old=old, out_type=bf16,
+    own_q, near_q, far_q, old, *k_parts = tile(
+        tab, 0, (0, 1), qlim, (msg, near, far), (kvo, kvx), kcode,
+        finals=((0, f32), (1, bf16), (2, bf16)),
+    )
+    raw_last, gkvx, *q_parts = tile(
+        tab, 3, (1,), qlim, (last,), k_parts=k_parts, raws=(0, 2), old=old, out_type=bf16,
         export_q=True,
     )
     got = other_core(gkvx)
-    far_q, last_q, gkvo = tile(
-        tab, 2, (0,), qlim, q_parts=q_parts, k_parts=k_parts, finals=((0, bf16), (1, bf16)),
-        oldq=raw_far, old=old,
+    last_q, gkvo = tile(
+        tab, 3, (0,), qlim, q_parts=q_parts, k_parts=k_parts, finals=((0, bf16),),
+        oldq=raw_last, old=old,
     )
     paired = (gkvo + got.astype(f32)).astype(bf16).reshape(NY, TOK, 2 * DIM)
     summed = over_y(paired)

time: 84.2 us -> 84 us (level)
  transfers between devices with their start and end apart: 10 -> 10, of which waited for: 3 -> 3; matrix products, arithmetic and copies ran while one was open for 1% -> 1% of each run, Pallas kernels for 16% -> 18%
where the time goes in v9:
time: 84 us; the launch traced here: 82.8 us
  starting transfers between devices  38.7 us (46%)
  waiting for transfers between devices  19.2 us (23%)
  Pallas kernels  17.5 us (21%)
  local copies, waits for them, and re-layouts  4.23 us (5%)
  other arithmetic  2.46 us (3%)
    ppermute x6, starting transfers between devices, along_z(): lax.ppermute(value, ('zlo', 'zhl'), [(i, i ^ mask) for i in range(NZ)])  23.9 us
    pallas_call x3, Pallas kernels, tile(): pl.pallas_call(body, in_specs=[smem] + [vmem] * len(arrays), out_specs=[v...  14.4 us
    ppermute x6, waiting for transfers between devices, along_z(): lax.ppermute(value, ('zlo', 'zhl'), [(i, i ^ mask) for i in range(NZ)])  11.3 us
    all_to_all x2, starting transfers between devices, over_y(): return lax.all_to_all(value, 'y', 0, 0)  10.9 us
    all_to_all x2, waiting for transfers between devices, over_y(): return lax.all_to_all(value, 'y', 0, 0)  7.82 us
    ppermute x2, starting transfers between devices, other_core(): return lax.ppermute(value, 'core', [(0, 1), (1, 0)])  3.83 us
    unnamed x10, local copies, waits for them, and re-layouts  3.39 us
    pallas_call x1, Pallas kernels, plan(): pl.pallas_call(plan_kernel, in_specs=[pl.BlockSpec(memory_space=pltpu.SME...  2.19 us
  transfers between devices with their start and end apart: 10, of which 3 were waited for; matrix products, arithmetic and copies ran while one was open for 1% of the time, Pallas kernels for 18%

profile of v9, /device:TPU:6, one launch (start us, length us, event | category | flops | bytes accessed | tf_op | source)
XLA Modules:
  0.0 82.8 jit_solution(10690921708993858389)
XLA Ops:
  0.6 0.0 copy-start.4
  0.6 0.8 pad_maximum_fusion
  1.4 0.8 %broadcast_in_dim.2 = bf16[8,128,256]{2,1,0:T(8,128)(2,1)} broadcast(bf16[128,256]{1,0:T(8,128)(2,1)S(1)} %pad_maximum_fusion), dimensions={1,2} | broadcast | bytes 589824 | tf_op jit(solution)/shard_map/broadcast_in_dim | solution.py:337
  2.3 7.1 %all-to-all-start = ((bf16[8,128,256]{2,1,0:T(8,128)(2,1)}), bf16[8,128,256]{2,1,0:T(8,128)(2,1)S(1)}, u32[]{:S(2)}, u32[]{:S(2)}) async-start(bf16[8,128,256]{2,1,0:T(8,128)(2,1)} %broadcast_in_dim.2), calls=%async_computation | async-start | bytes 1048576 | tf_op jit(solution)/shard_map/all_to_all | solution.py:334
  9.4 0.0 copy-start
  9.4 0.9 %copy-done = bf16[128,512]{1,0:T(8,128)(2,1)S(1)} copy-done((bf16[128,512]{1,0:T(8,128)(2,1)S(1)}, bf16[128,512]{1,0:T(8,128)(2,1)}, u32[]{:S(2)}) %copy-start) | copy-done | bytes 131096
  10.3 0.0 copy-start.1
  10.3 0.9 %copy-done.1 = bf16[128,512]{1,0:T(8,128)(2,1)S(1)} copy-done((bf16[128,512]{1,0:T(8,128)(2,1)S(1)}, bf16[128,512]{1,0:T(8,128)(2,1)}, u32[]{:S(2)}) %copy-start.1) | copy-done | bytes 131096
  11.2 0.0 copy-start.2
  11.2 0.9 %copy-done.2 = bf16[128,512]{1,0:T(8,128)(2,1)S(1)} copy-done((bf16[128,512]{1,0:T(8,128)(2,1)S(1)}, bf16[128,512]{1,0:T(8,128)(2,1)}, u32[]{:S(2)}) %copy-start.2) | copy-done | bytes 131096
  12.1 0.0 copy-start.3
  12.1 0.7 copy-done.3
  12.8 0.2 pack.1.refs_1_
  13.0 6.1 %collective-permute-start.1 = (bf16[136,1024]{1,0:T(8,128)(2,1)S(1)}, bf16[136,1024]{1,0:T(8,128)(2,1)S(1)}, u32[]{:S(2)}, u32[]{:S(2)}) collective-permute-start(bf16[136,1024]{1,0:T(8,128)(2,1)S(1)} %pack.1.refs_1_), channel_id=1, source_target_pairs={{0,1},{1,0},{32,33},{33,32},{2,3},{3,2},{34,35},{35,34},{4,5},{5,4... | collective-permute-start | bytes 835592 | tf_op jit(solution)/shard_map/ppermute | solution.py:328
  19.0 7.8 %all-to-all-done = bf16[8,128,256]{2,1,0:T(8,128)(2,1)S(1)} async-done(((bf16[8,128,256]{2,1,0:T(8,128)(2,1)}), bf16[8,128,256]{2,1,0:T(8,128)(2,1)S(1)}, u32[]{:S(2)}, u32[]{:S(2)}) %all-to-all-start) | async-done | bytes 524320 | tf_op jit(solution)/shard_map/all_to_all | solution.py:334
  26.9 1.9 %collective-permute-start.2 = (bf16[1024,256]{1,0:T(8,128)(2,1)S(1)}, bf16[1024,256]{1,0:T(8,128)(2,1)S(1)}, u32[]{:S(2)}, u32[]{:S(2)}) collective-permute-start(bf16[1024,256]{1,0:T(8,128)(2,1)S(1)} %bitcast.5), channel_id=1, source_target_pairs={{0,16},{16,0},{1,17},{17,1},{2,18},{18,2},{3,19},{19,3},{4,20},{20... | collective-permute-start | bytes 1572872 | tf_op jit(solution)/shard_map/ppermute | solution.py:331
  28.8 4.3 %collective-permute-start = (bf16[136,1024]{1,0:T(8,128)(2,1)S(1)}, bf16[136,1024]{1,0:T(8,128)(2,1)S(1)}, u32[]{:S(2)}, u32[]{:S(2)}) collective-permute-start(bf16[136,1024]{1,0:T(8,128)(2,1)S(1)} %pack.1.refs_1_), channel_id=1, source_target_pairs={{0,32},{1,33},{32,0},{33,1},{2,34},{3,35},{34,2},{35,3},{4,36},{5,... | collective-permute-start | bytes 835592 | tf_op jit(solution)/shard_map/ppermute | solution.py:328
  33.1 0.0 collective-permute-done.1.refs_3_
  33.1 1.9 %collective-permute-start.5 = (bf16[136,1024]{1,0:T(8,128)(2,1)S(1)}, bf16[136,1024]{1,0:T(8,128)(2,1)S(1)}, u32[]{:S(2)}, u32[]{:S(2)}) collective-permute-start(bf16[136,1024]{1,0:T(8,128)(2,1)S(1)} %collective-permute-done.1.refs_3_), channel_id=1, source_target_pairs={{0,32},{1,33},{32,0},{33,1},{2,34},{3,35},{34,2},{35,3},{4,36},{5,... | collective-permute-start | bytes 835592 | tf_op jit(solution)/shard_map/ppermute | solution.py:328
  35.0 0.0 copy-done.4
  35.0 2.2 %plan.1 = (s32[4,128]{1,0:T(4,128)S(1)}, s32[16,128]{1,0:T(8,128)S(1)}, s32[8,3,256]{2,1,0:T(4,128)S(1)}) custom-call(s32[3,3]{1,0:T(4,128)S(1)} %copy-done.4, s32[512,1,128]{2,1,0:T(1,128)} %bitcast.8, s32[512,1,128]{2,1,0:T(1,128)} %bitcast.9), custom_call_target="tpu_custom_call" | custom-call | tf_op jit(solution)/shard_map/plan/pallas_call | solution.py:304
  37.2 3.3 %collective-permute-done.refs_2_ = bf16[136,1024]{1,0:T(8,128)(2,1)S(1)} collective-permute-done((bf16[136,1024]{1,0:T(8,128)(2,1)S(1)}, bf16[136,1024]{1,0:T(8,128)(2,1)S(1)}, u32[]{:S(2)}, u32[]{:S(2)}) %collective-permute-start) | collective-permute-done | bytes 278560 | tf_op jit(solution)/shard_map/ppermute | solution.py:328
  40.6 0.0 collective-permute-done.2.refs_5_
  40.6 10.1 %shard_map.112 = (f32[128,512]{1,0:T(8,128)S(1)}, bf16[128,512]{1,0:T(8,128)(2,1)S(1)}, bf16[128,512]{1,0:T(8,128)(2,1)S(1)}, f32[2048,256]{1,0:T(8,128)S(1)}, b...) custom-call(s32[4,128]{1,0:T(4,128)S(1)} %get-tuple-element.23.refs_0_, ...), custom_call_target="tpu_custom_call" | custom-call | tf_op jit(solution)/shard_map/pallas_call | solution.py:228
  50.6 0.0 collective-permute-done.5.refs_1_
  50.6 2.2 %shard_map.113 = (f32[2,128,256]{2,1,0:T(8,128)S(1)}, bf16[1024,256]{1,0:T(8,128)(2,1)S(1)}, bf16[512,128]{1,0:T(8,128)(2,1)S(1)}, bf16[512,128]{1,0:T(8,128)(2,...) custom-call(s32[4,128]{1,0:T(4,128)S(1)} %get-tuple-element.23.refs_0_, ...), custom_call_target="tpu_custom_call" | custom-call | tf_op jit(solution)/shard_map/pallas_call | solution.py:228
  52.8 1.9 %collective-permute-start.7 = (bf16[1024,256]{1,0:T(8,128)(2,1)S(1)}, bf16[1024,256]{1,0:T(8,128)(2,1)S(1)}, u32[]{:S(2)}, u32[]{:S(2)}) collective-permute-start(bf16[1024,256]{1,0:T(8,128)(2,1)S(1)} %get-tuple-element.40), channel_id=1, source_target_pairs={{0,16},{16,0},{1,17},{17,1},{2,18},{18,2},{3,19},{19,3},{4,20},{20... | collective-permute-start | bytes 1572872 | tf_op jit(solution)/shard_map/ppermute | solution.py:331
  54.7 2.2 %shard_map.114 = (bf16[128,512]{1,0:T(8,128)(2,1)S(1)}, f32[1024,256]{1,0:T(8,128)S(1)}) custom-call(s32[4,128]{1,0:T(4,128)S(1)} %get-tuple-element.23.refs_0_, s32[8,3,256]{2,1,0:T(4,128)S(1)} %get-tuple-element.25.refs_7_.refs_2_.refs_1_, bf16[512,128]{1,0:T(8,128)(2,1)S(1)} %get-tuple-element.33.refs_2_, bf16[512,128]{1,0:T(8,128)(2,1)S(1)} %get-tuple-element.34.refs_3_, ...), custom_call_target="tpu_custom_call" | custom-call | tf_op jit(solution)/shard_map/pallas_call | solution.py:228
  56.9 0.0 collective-permute-done.7
  56.9 0.9 %add_convert_fusion = bf16[1024,256]{1,0:T(8,128)(2,1)} fusion(f32[1024,256]{1,0:T(8,128)S(1)} %get-tuple-element.39, bf16[1024,256]{1,0:T(8,128)(2,1)S(1)} %collective-permute-done.7), kind=kLoop, calls=%fused_computation | loop fusion | flops 786432 | bytes 2097152 | tf_op jit(solution)/shard_map/convert_element_type | solution.py:360
  57.9 3.8 %all-to-all-start.1 = ((bf16[8,128,256]{2,1,0:T(8,128)(2,1)}), bf16[8,128,256]{2,1,0:T(8,128)(2,1)S(1)}, u32[]{:S(2)}, u32[]{:S(2)}) async-start(bf16[8,128,256]{2,1,0:T(8,128)(2,1)} %bitcast.4), calls=%async_computation.1 | async-start | bytes 1048576 | tf_op jit(solution)/shard_map/all_to_all | solution.py:334
  61.7 3.6 %collective-permute-start.3 = (bf16[128,512]{1,0:T(8,128)(2,1)S(1)}, bf16[128,512]{1,0:T(8,128)(2,1)S(1)}, u32[]{:S(2)}, u32[]{:S(2)}) collective-permute-start(bf16[128,512]{1,0:T(8,128)(2,1)S(1)} %get-tuple-element.27), channel_id=1, source_target_pairs={{0,32},{1,33},{32,0},{33,1},{2,34},{3,35},{34,2},{35,3},{4,36},{5,... | collective-permute-start | bytes 393224 | tf_op jit(solution)/shard_map/ppermute | solution.py:328
  65.3 6.1 %collective-permute-start.4 = (bf16[128,512]{1,0:T(8,128)(2,1)S(1)}, bf16[128,512]{1,0:T(8,128)(2,1)S(1)}, u32[]{:S(2)}, u32[]{:S(2)}) collective-permute-start(bf16[128,512]{1,0:T(8,128)(2,1)S(1)} %get-tuple-element.28), channel_id=1, source_target_pairs={{0,1},{1,0},{32,33},{33,32},{2,3},{3,2},{34,35},{35,34},{4,5},{5,4... | collective-permute-start | bytes 393224 | tf_op jit(solution)/shard_map/ppermute | solution.py:328
  71.4 1.9 %collective-permute-start.6 = (bf16[128,512]{1,0:T(8,128)(2,1)S(1)}, bf16[128,512]{1,0:T(8,128)(2,1)S(1)}, u32[]{:S(2)}, u32[]{:S(2)}) collective-permute-start(bf16[128,512]{1,0:T(8,128)(2,1)S(1)} %get-tuple-element.38), channel_id=1, source_target_pairs={{0,33},{1,32},{32,1},{33,0},{2,35},{3,34},{34,3},{35,2},{4,37},{5,... | collective-permute-start | bytes 393224 | tf_op jit(solution)/shard_map/ppermute | solution.py:328
  73.4 0.0 collective-permute-done.3
  73.4 8.0 %collective-permute-done.4 = bf16[128,512]{1,0:T(8,128)(2,1)S(1)} collective-permute-done((bf16[128,512]{1,0:T(8,128)(2,1)S(1)}, bf16[128,512]{1,0:T(8,128)(2,1)S(1)}, u32[]{:S(2)}, u32[]{:S(2)}) %collective-permute-start.4) | collective-permute-done | bytes 131104 | tf_op jit(solution)/shard_map/ppermute | solution.py:328
  81.3 0.0 collective-permute-done.6
  81.4 0.7 multiply_convert_fusion
  82.1 0.0 all-to-all-done.1.parts
  82.1 0.7 finish.1
Async XLA Ops:
  0.6 34.4 %copy-start.4 = (s32[3,3]{1,0:T(4,128)S(1)}, s32[3,3]{1,0:T(4,128)}, u32[]{:S(2)}) copy-start(s32[3,3]{1,0:T(4,128)} %table.1) | copy-start | bytes 112
  2.3 24.6 %all-to-all-start = ((bf16[8,128,256]{2,1,0:T(8,128)(2,1)}), bf16[8,128,256]{2,1,0:T(8,128)(2,1)S(1)}, u32[]{:S(2)}, u32[]{:S(2)}) async-start(bf16[8,128,256]{2,1,0:T(8,128)(2,1)} %broadcast_in_dim.2), calls=%async_computation | async-start | bytes 1048576 | tf_op jit(solution)/shard_map/all_to_all | solution.py:334
  9.4 0.9 %copy-start = (bf16[128,512]{1,0:T(8,128)(2,1)S(1)}, bf16[128,512]{1,0:T(8,128)(2,1)}, u32[]{:S(2)}) copy-start(bf16[128,512]{1,0:T(8,128)(2,1)} %q_ref.1) | copy-start | bytes 393220
  10.3 0.9 %copy-start.1 = (bf16[128,512]{1,0:T(8,128)(2,1)S(1)}, bf16[128,512]{1,0:T(8,128)(2,1)}, u32[]{:S(2)}) copy-start(bf16[128,512]{1,0:T(8,128)(2,1)} %d_ref.1) | copy-start | bytes 393220
  11.2 0.9 %copy-start.2 = (bf16[128,512]{1,0:T(8,128)(2,1)S(1)}, bf16[128,512]{1,0:T(8,128)(2,1)}, u32[]{:S(2)}) copy-start(bf16[128,512]{1,0:T(8,128)(2,1)} %o_ref.1) | copy-start | bytes 393220
  12.1 0.7 copy-start.3
  13.0 20.1 %collective-permute-start.1 = (bf16[136,1024]{1,0:T(8,128)(2,1)S(1)}, bf16[136,1024]{1,0:T(8,128)(2,1)S(1)}, u32[]{:S(2)}, u32[]{:S(2)}) collective-permute-start(bf16[136,1024]{1,0:T(8,128)(2,1)S(1)} %pack.1.refs_1_), channel_id=1, source_target_pairs={{0,1},{1,0},{32,33},{33,32},{2,3},{3,2},{34,35},{35,34},{4,5},{5,4... | collective-permute-start | bytes 835592 | tf_op jit(solution)/shard_map/ppermute | solution.py:328
  26.9 13.7 %collective-permute-start.2 = (bf16[1024,256]{1,0:T(8,128)(2,1)S(1)}, bf16[1024,256]{1,0:T(8,128)(2,1)S(1)}, u32[]{:S(2)}, u32[]{:S(2)}) collective-permute-start(bf16[1024,256]{1,0:T(8,128)(2,1)S(1)} %bitcast.5), channel_id=1, source_target_pairs={{0,16},{16,0},{1,17},{17,1},{2,18},{18,2},{3,19},{19,3},{4,20},{20... | collective-permute-start | bytes 1572872 | tf_op jit(solution)/shard_map/ppermute | solution.py:331
  28.8 11.8 %collective-permute-start = (bf16[136,1024]{1,0:T(8,128)(2,1)S(1)}, bf16[136,1024]{1,0:T(8,128)(2,1)S(1)}, u32[]{:S(2)}, u32[]{:S(2)}) collective-permute-start(bf16[136,1024]{1,0:T(8,128)(2,1)S(1)} %pack.1.refs_1_), channel_id=1, source_target_pairs={{0,32},{1,33},{32,0},{33,1},{2,34},{3,35},{34,2},{35,3},{4,36},{5,... | collective-permute-start | bytes 835592 | tf_op jit(solution)/shard_map/ppermute | solution.py:328
  33.1 17.5 %collective-permute-start.5 = (bf16[136,1024]{1,0:T(8,128)(2,1)S(1)}, bf16[136,1024]{1,0:T(8,128)(2,1)S(1)}, u32[]{:S(2)}, u32[]{:S(2)}) collective-permute-start(bf16[136,1024]{1,0:T(8,128)(2,1)S(1)} %collective-permute-done.1.refs_3_), channel_id=1, source_target_pairs={{0,32},{1,33},{32,0},{33,1},{2,34},{3,35},{34,2},{35,3},{4,36},{5,... | collective-permute-start | bytes 835592 | tf_op jit(solution)/shard_map/ppermute | solution.py:328
  52.8 4.1 %collective-permute-start.7 = (bf16[1024,256]{1,0:T(8,128)(2,1)S(1)}, bf16[1024,256]{1,0:T(8,128)(2,1)S(1)}, u32[]{:S(2)}, u32[]{:S(2)}) collective-permute-start(bf16[1024,256]{1,0:T(8,128)(2,1)S(1)} %get-tuple-element.40), channel_id=1, source_target_pairs={{0,16},{16,0},{1,17},{17,1},{2,18},{18,2},{3,19},{19,3},{4,20},{20... | collective-permute-start | bytes 1572872 | tf_op jit(solution)/shard_map/ppermute | solution.py:331
  57.9 24.2 %all-to-all-start.1 = ((bf16[8,128,256]{2,1,0:T(8,128)(2,1)}), bf16[8,128,256]{2,1,0:T(8,128)(2,1)S(1)}, u32[]{:S(2)}, u32[]{:S(2)}) async-start(bf16[8,128,256]{2,1,0:T(8,128)(2,1)} %bitcast.4), calls=%async_computation.1 | async-start | bytes 1048576 | tf_op jit(solution)/shard_map/all_to_all | solution.py:334
  61.7 11.7 %collective-permute-start.3 = (bf16[128,512]{1,0:T(8,128)(2,1)S(1)}, bf16[128,512]{1,0:T(8,128)(2,1)S(1)}, u32[]{:S(2)}, u32[]{:S(2)}) collective-permute-start(bf16[128,512]{1,0:T(8,128)(2,1)S(1)} %get-tuple-element.27), channel_id=1, source_target_pairs={{0,32},{1,33},{32,0},{33,1},{2,34},{3,35},{34,2},{35,3},{4,36},{5,... | collective-permute-start | bytes 393224 | tf_op jit(solution)/shard_map/ppermute | solution.py:328
  65.3 16.0 %collective-permute-start.4 = (bf16[128,512]{1,0:T(8,128)(2,1)S(1)}, bf16[128,512]{1,0:T(8,128)(2,1)S(1)}, u32[]{:S(2)}, u32[]{:S(2)}) collective-permute-start(bf16[128,512]{1,0:T(8,128)(2,1)S(1)} %get-tuple-element.28), channel_id=1, source_target_pairs={{0,1},{1,0},{32,33},{33,32},{2,3},{3,2},{34,35},{35,34},{4,5},{5,4... | collective-permute-start | bytes 393224 | tf_op jit(solution)/shard_map/ppermute | solution.py:328
  71.4 9.9 %collective-permute-start.6 = (bf16[128,512]{1,0:T(8,128)(2,1)S(1)}, bf16[128,512]{1,0:T(8,128)(2,1)S(1)}, u32[]{:S(2)}, u32[]{:S(2)}) collective-permute-start(bf16[128,512]{1,0:T(8,128)(2,1)S(1)} %get-tuple-element.38), channel_id=1, source_target_pairs={{0,33},{1,32},{32,1},{33,0},{2,35},{3,34},{34,3},{35,2},{4,37},{5,... | collective-permute-start | bytes 393224 | tf_op jit(solution)/shard_map/ppermute | solution.py:328

commit v10 on v9

--- a/solution.py
+++ b/solution.py
@@ -235,6 +235,18 @@
     )(tab, *[in_vmem(v) for v in arrays])
 
 
+def copies_kernel(key_ref, value_ref, out, sems):
+    moves = []
+    for i in range(NY):
+        for j, ref in enumerate((key_ref, value_ref)):
+            half = out.at[i, :, j * DIM : (j + 1) * DIM]
+            moves.append(pltpu.make_async_copy(ref, half, sems.at[2 * i + j]))
+    for move in moves:
+        move.start()
+    for move in moves:
+        move.wait()
+
+
 def finish_kernel(parts, key_ref, value_ref):
     total = jnp.sum(parts[...].astype(f32), axis=0)
     key_ref[...] = (total[:, :DIM] * DIM ** (-0.5)).astype(bf16)
@@ -333,8 +345,19 @@
     def over_y(value):
         return lax.all_to_all(value, "y", 0, 0)
 
-    pair = jnp.concatenate([key_states, value_states], axis=1)
-    copies = jnp.broadcast_to(pair[None], (NY, TOK, 2 * DIM))
+    hbm = pl.BlockSpec(memory_space=pltpu.HBM)
+    copies = pl.pallas_call(
+        copies_kernel,
+        out_shape=jax.ShapeDtypeStruct((NY, TOK, 2 * DIM), bf16),
+        in_specs=[hbm] * 2,
+        out_specs=hbm,
+        scratch_shapes=[pltpu.SemaphoreType.DMA((2 * NY,))],
+        compiler_params=pltpu.CompilerParams(vmem_limit_bytes=8 << 20),
+        name="copies",
+    )(
+        pltpu.with_memory_space_constraint(key_states, pltpu.HBM),
+        pltpu.with_memory_space_constraint(value_states, pltpu.HBM),
+    )
     msg = pl.pallas_call(
         pack_kernel, out_shape=pltpu.VMEM((TOK + 8, 2 * WIDE), bf16), compiler_params=pltpu.CompilerParams(vmem_limit_bytes=8 << 20), name="pack"
     )(queries, grad_out, attn_out, log_norm.T)
@@ -363,8 +386,10 @@
     grad_key, grad_value = pl.pallas_call(
         finish_kernel, out_shape=[narrow] * 2, compiler_params=pltpu.CompilerParams(vmem_limit_bytes=8 << 20), name="finish"
     )(in_vmem(summed))
-    back = [along_z(g, mask) for g, mask in zip((near_q, far_q, last_q), MASKS[1:])]
-    grad_q = (own_q + back[0].astype(f32) + back[1].astype(f32) + back[2].astype(f32)) * DIM ** (-0.5)
+    back = []
+    for part, mask in ((last_q, 3), (far_q, 1), (near_q, 2)):
+        back.append(along_z(part, mask).astype(f32))
+    grad_q = (own_q + back[2] + back[1] + back[0]) * DIM ** (-0.5)
     return grad_q.astype(bf16), grad_key, grad_value
 
 

time: 84 us -> 99.5 us (1.18)
  Pallas kernels: 17.5 us -> 34.6 us
    pallas_call x0 -> x1, Pallas kernels: none -> 17.1 us  [shards(): pl.pallas_call(copies_kernel, out_shape=jax.ShapeDtypeStruct((NY, TOK, 2...]
  transfers between devices with their start and end apart: 10 -> 10, of which waited for: 3 -> 3; matrix products, arithmetic and copies ran while one was open for 1% -> 1% of each run, Pallas kernels for 18% -> 15%
where the time goes in v10:
time: 99.5 us; the launch traced here: 98.3 us
  starting transfers between devices  38.7 us (39%)
  Pallas kernels  34.6 us (35%)
  waiting for transfers between devices  19.2 us (19%)
  local copies, waits for them, and re-layouts  3.39 us (3%)
  other arithmetic  1.67 us (2%)
    ppermute x6, starting transfers between devices, along_z(): lax.ppermute(value, ('zlo', 'zhl'), [(i, i ^ mask) for i in range(NZ)])  23.9 us
    pallas_call x1, Pallas kernels, shards(): pl.pallas_call(copies_kernel, out_shape=jax.ShapeDtypeStruct((NY, TOK, 2...  17.1 us
    pallas_call x3, Pallas kernels, tile(): pl.pallas_call(body, in_specs=[smem] + [vmem] * len(arrays), out_specs=[v...  14.4 us
    ppermute x6, waiting for transfers between devices, along_z(): lax.ppermute(value, ('zlo', 'zhl'), [(i, i ^ mask) for i in range(NZ)])  11.3 us
    all_to_all x2, starting transfers between devices, over_y(): return lax.all_to_all(value, 'y', 0, 0)  10.9 us
    all_to_all x2, waiting for transfers between devices, over_y(): return lax.all_to_all(value, 'y', 0, 0)  7.82 us
    ppermute x2, starting transfers between devices, other_core(): return lax.ppermute(value, 'core', [(0, 1), (1, 0)])  3.83 us
    unnamed x10, local copies, waits for them, and re-layouts  3.39 us
  transfers between devices with their start and end apart: 10, of which 3 were waited for; matrix products, arithmetic and copies ran while one was open for 1% of the time, Pallas kernels for 15%

profile of v10, /device:TPU:6, one launch (start us, length us, event | category | flops | bytes accessed | tf_op | source)
XLA Modules:
  0.0 98.3 jit_solution(9881074505297645406)
XLA Ops:
  0.6 0.0 copy-start.4
  0.6 17.1 %copies.1 = bf16[8,128,256]{2,1,0:T(8,128)(2,1)} custom-call(bf16[128,128]{1,0:T(8,128)(2,1)} %key_ref.1, bf16[128,128]{1,0:T(8,128)(2,1)} %value_ref.1), custom_call_target="tpu_custom_call" | custom-call | tf_op jit(solution)/shard_map/copies/pallas_call | solution.py:349
  17.8 7.1 %all-to-all-start = ((bf16[8,128,256]{2,1,0:T(8,128)(2,1)}), bf16[8,128,256]{2,1,0:T(8,128)(2,1)S(1)}, u32[]{:S(2)}, u32[]{:S(2)}) async-start(bf16[8,128,256]{2,1,0:T(8,128)(2,1)} %copies.1), calls=%async_computation | async-start | bytes 1048576 | tf_op jit(solution)/shard_map/all_to_all | solution.py:346
  24.9 0.0 copy-start
  24.9 0.9 copy-done
  25.8 0.0 copy-start.1
  25.8 0.9 copy-done.1
  26.7 0.0 copy-start.2
  26.7 0.9 copy-done.2
  27.6 0.0 copy-start.3
  27.6 0.7 copy-done.3
  28.3 0.2 pack.1.refs_1_
  28.5 6.1 %collective-permute-start.1 = (bf16[136,1024]{1,0:T(8,128)(2,1)S(1)}, bf16[136,1024]{1,0:T(8,128)(2,1)S(1)}, u32[]{:S(2)}, u32[]{:S(2)}) collective-permute-start(bf16[136,1024]{1,0:T(8,128)(2,1)S(1)} %pack.1.refs_1_), channel_id=1, source_target_pairs={{0,1},{1,0},{32,33},{33,32},{2,3},{3,2},{34,35},{35,34},{4,5},{5,4... | collective-permute-start | bytes 835592 | tf_op jit(solution)/shard_map/ppermute | solution.py:340
  34.6 7.8 %all-to-all-done = bf16[8,128,256]{2,1,0:T(8,128)(2,1)S(1)} async-done(((bf16[8,128,256]{2,1,0:T(8,128)(2,1)}), bf16[8,128,256]{2,1,0:T(8,128)(2,1)S(1)}, u32[]{:S(2)}, u32[]{:S(2)}) %all-to-all-start) | async-done | bytes 524320 | tf_op jit(solution)/shard_map/all_to_all | solution.py:346
  42.4 1.9 %collective-permute-start.2 = (bf16[1024,256]{1,0:T(8,128)(2,1)S(1)}, bf16[1024,256]{1,0:T(8,128)(2,1)S(1)}, u32[]{:S(2)}, u32[]{:S(2)}) collective-permute-start(bf16[1024,256]{1,0:T(8,128)(2,1)S(1)} %bitcast.5), channel_id=1, source_target_pairs={{0,16},{16,0},{1,17},{17,1},{2,18},{18,2},{3,19},{19,3},{4,20},{20... | collective-permute-start | bytes 1572872 | tf_op jit(solution)/shard_map/ppermute | solution.py:343
  44.3 4.3 %collective-permute-start = (bf16[136,1024]{1,0:T(8,128)(2,1)S(1)}, bf16[136,1024]{1,0:T(8,128)(2,1)S(1)}, u32[]{:S(2)}, u32[]{:S(2)}) collective-permute-start(bf16[136,1024]{1,0:T(8,128)(2,1)S(1)} %pack.1.refs_1_), channel_id=1, source_target_pairs={{0,32},{1,33},{32,0},{33,1},{2,34},{3,35},{34,2},{35,3},{4,36},{5,... | collective-permute-start | bytes 835592 | tf_op jit(solution)/shard_map/ppermute | solution.py:340
  48.6 0.0 collective-permute-done.1.refs_3_
  48.6 1.9 %collective-permute-start.5 = (bf16[136,1024]{1,0:T(8,128)(2,1)S(1)}, bf16[136,1024]{1,0:T(8,128)(2,1)S(1)}, u32[]{:S(2)}, u32[]{:S(2)}) collective-permute-start(bf16[136,1024]{1,0:T(8,128)(2,1)S(1)} %collective-permute-done.1.refs_3_), channel_id=1, source_target_pairs={{0,32},{1,33},{32,0},{33,1},{2,34},{3,35},{34,2},{35,3},{4,36},{5,... | collective-permute-start | bytes 835592 | tf_op jit(solution)/shard_map/ppermute | solution.py:340
  50.5 0.0 copy-done.4
  50.5 2.2 %plan.1 = (s32[4,128]{1,0:T(4,128)S(1)}, s32[16,128]{1,0:T(8,128)S(1)}, s32[8,3,256]{2,1,0:T(4,128)S(1)}) custom-call(s32[3,3]{1,0:T(4,128)S(1)} %copy-done.4, s32[512,1,128]{2,1,0:T(1,128)} %bitcast.8, s32[512,1,128]{2,1,0:T(1,128)} %bitcast.9), custom_call_target="tpu_custom_call" | custom-call | tf_op jit(solution)/shard_map/plan/pallas_call | solution.py:316
  52.7 3.3 %collective-permute-done.refs_2_ = bf16[136,1024]{1,0:T(8,128)(2,1)S(1)} collective-permute-done((bf16[136,1024]{1,0:T(8,128)(2,1)S(1)}, bf16[136,1024]{1,0:T(8,128)(2,1)S(1)}, u32[]{:S(2)}, u32[]{:S(2)}) %collective-permute-start) | collective-permute-done | bytes 278560 | tf_op jit(solution)/shard_map/ppermute | solution.py:340
  56.1 0.0 collective-permute-done.2.refs_5_
  56.1 10.1 %shard_map.112 = (f32[128,512]{1,0:T(8,128)S(1)}, bf16[128,512]{1,0:T(8,128)(2,1)S(1)}, bf16[128,512]{1,0:T(8,128)(2,1)S(1)}, f32[2048,256]{1,0:T(8,128)S(1)}, b...) custom-call(s32[4,128]{1,0:T(4,128)S(1)} %get-tuple-element.23.refs_0_, ...), custom_call_target="tpu_custom_call" | custom-call | tf_op jit(solution)/shard_map/pallas_call | solution.py:228
  66.1 0.0 collective-permute-done.5.refs_1_
  66.2 2.2 %shard_map.113 = (f32[2,128,256]{2,1,0:T(8,128)S(1)}, bf16[1024,256]{1,0:T(8,128)(2,1)S(1)}, bf16[512,128]{1,0:T(8,128)(2,1)S(1)}, bf16[512,128]{1,0:T(8,128)(2,...) custom-call(s32[4,128]{1,0:T(4,128)S(1)} %get-tuple-element.23.refs_0_, ...), custom_call_target="tpu_custom_call" | custom-call | tf_op jit(solution)/shard_map/pallas_call | solution.py:228
  68.3 1.9 %collective-permute-start.7 = (bf16[1024,256]{1,0:T(8,128)(2,1)S(1)}, bf16[1024,256]{1,0:T(8,128)(2,1)S(1)}, u32[]{:S(2)}, u32[]{:S(2)}) collective-permute-start(bf16[1024,256]{1,0:T(8,128)(2,1)S(1)} %get-tuple-element.40), channel_id=1, source_target_pairs={{0,16},{16,0},{1,17},{17,1},{2,18},{18,2},{3,19},{19,3},{4,20},{20... | collective-permute-start | bytes 1572872 | tf_op jit(solution)/shard_map/ppermute | solution.py:343
  70.3 2.2 %shard_map.114 = (bf16[128,512]{1,0:T(8,128)(2,1)S(1)}, f32[1024,256]{1,0:T(8,128)S(1)}) custom-call(s32[4,128]{1,0:T(4,128)S(1)} %get-tuple-element.23.refs_0_, s32[8,3,256]{2,1,0:T(4,128)S(1)} %get-tuple-element.25.refs_7_.refs_2_.refs_1_, bf16[512,128]{1,0:T(8,128)(2,1)S(1)} %get-tuple-element.33.refs_2_, bf16[512,128]{1,0:T(8,128)(2,1)S(1)} %get-tuple-element.34.refs_3_, ...), custom_call_target="tpu_custom_call" | custom-call | tf_op jit(solution)/shard_map/pallas_call | solution.py:228
  72.4 0.0 collective-permute-done.7
  72.5 0.9 add_convert_fusion
  73.4 3.8 %all-to-all-start.1 = ((bf16[8,128,256]{2,1,0:T(8,128)(2,1)}), bf16[8,128,256]{2,1,0:T(8,128)(2,1)S(1)}, u32[]{:S(2)}, u32[]{:S(2)}) async-start(bf16[8,128,256]{2,1,0:T(8,128)(2,1)} %bitcast.4), calls=%async_computation.1 | async-start | bytes 1048576 | tf_op jit(solution)/shard_map/all_to_all | solution.py:346
  77.2 3.6 %collective-permute-start.3 = (bf16[128,512]{1,0:T(8,128)(2,1)S(1)}, bf16[128,512]{1,0:T(8,128)(2,1)S(1)}, u32[]{:S(2)}, u32[]{:S(2)}) collective-permute-start(bf16[128,512]{1,0:T(8,128)(2,1)S(1)} %get-tuple-element.27), channel_id=1, source_target_pairs={{0,32},{1,33},{32,0},{33,1},{2,34},{3,35},{34,2},{35,3},{4,36},{5,... | collective-permute-start | bytes 393224 | tf_op jit(solution)/shard_map/ppermute | solution.py:340
  80.8 6.1 %collective-permute-start.4 = (bf16[128,512]{1,0:T(8,128)(2,1)S(1)}, bf16[128,512]{1,0:T(8,128)(2,1)S(1)}, u32[]{:S(2)}, u32[]{:S(2)}) collective-permute-start(bf16[128,512]{1,0:T(8,128)(2,1)S(1)} %get-tuple-element.28), channel_id=1, source_target_pairs={{0,1},{1,0},{32,33},{33,32},{2,3},{3,2},{34,35},{35,34},{4,5},{5,4... | collective-permute-start | bytes 393224 | tf_op jit(solution)/shard_map/ppermute | solution.py:340
  87.0 1.9 %collective-permute-start.6 = (bf16[128,512]{1,0:T(8,128)(2,1)S(1)}, bf16[128,512]{1,0:T(8,128)(2,1)S(1)}, u32[]{:S(2)}, u32[]{:S(2)}) collective-permute-start(bf16[128,512]{1,0:T(8,128)(2,1)S(1)} %get-tuple-element.38), channel_id=1, source_target_pairs={{0,33},{1,32},{32,1},{33,0},{2,35},{3,34},{34,3},{35,2},{4,37},{5,... | collective-permute-start | bytes 393224 | tf_op jit(solution)/shard_map/ppermute | solution.py:340
  88.9 0.0 collective-permute-done.3
  88.9 8.0 %collective-permute-done.4 = bf16[128,512]{1,0:T(8,128)(2,1)S(1)} collective-permute-done((bf16[128,512]{1,0:T(8,128)(2,1)S(1)}, bf16[128,512]{1,0:T(8,128)(2,1)S(1)}, u32[]{:S(2)}, u32[]{:S(2)}) %collective-permute-start.4) | collective-permute-done | bytes 131104 | tf_op jit(solution)/shard_map/ppermute | solution.py:340
  96.9 0.0 collective-permute-done.6
  96.9 0.7 multiply_convert_fusion
  97.6 0.0 all-to-all-done.1.parts
  97.6 0.7 finish.1
Async XLA Ops:
  0.6 49.9 %copy-start.4 = (s32[3,3]{1,0:T(4,128)S(1)}, s32[3,3]{1,0:T(4,128)}, u32[]{:S(2)}) copy-start(s32[3,3]{1,0:T(4,128)} %table.1) | copy-start | bytes 112
  17.8 24.6 %all-to-all-start = ((bf16[8,128,256]{2,1,0:T(8,128)(2,1)}), bf16[8,128,256]{2,1,0:T(8,128)(2,1)S(1)}, u32[]{:S(2)}, u32[]{:S(2)}) async-start(bf16[8,128,256]{2,1,0:T(8,128)(2,1)} %copies.1), calls=%async_computation | async-start | bytes 1048576 | tf_op jit(solution)/shard_map/all_to_all | solution.py:346
  24.9 0.9 copy-start
  25.8 0.9 copy-start.1
  26.7 0.9 copy-start.2
  27.6 0.7 copy-start.3
  28.5 20.1 %collective-permute-start.1 = (bf16[136,1024]{1,0:T(8,128)(2,1)S(1)}, bf16[136,1024]{1,0:T(8,128)(2,1)S(1)}, u32[]{:S(2)}, u32[]{:S(2)}) collective-permute-start(bf16[136,1024]{1,0:T(8,128)(2,1)S(1)} %pack.1.refs_1_), channel_id=1, source_target_pairs={{0,1},{1,0},{32,33},{33,32},{2,3},{3,2},{34,35},{35,34},{4,5},{5,4... | collective-permute-start | bytes 835592 | tf_op jit(solution)/shard_map/ppermute | solution.py:340
  42.4 13.7 %collective-permute-start.2 = (bf16[1024,256]{1,0:T(8,128)(2,1)S(1)}, bf16[1024,256]{1,0:T(8,128)(2,1)S(1)}, u32[]{:S(2)}, u32[]{:S(2)}) collective-permute-start(bf16[1024,256]{1,0:T(8,128)(2,1)S(1)} %bitcast.5), channel_id=1, source_target_pairs={{0,16},{16,0},{1,17},{17,1},{2,18},{18,2},{3,19},{19,3},{4,20},{20... | collective-permute-start | bytes 1572872 | tf_op jit(solution)/shard_map/ppermute | solution.py:343
  44.3 11.8 %collective-permute-start = (bf16[136,1024]{1,0:T(8,128)(2,1)S(1)}, bf16[136,1024]{1,0:T(8,128)(2,1)S(1)}, u32[]{:S(2)}, u32[]{:S(2)}) collective-permute-start(bf16[136,1024]{1,0:T(8,128)(2,1)S(1)} %pack.1.refs_1_), channel_id=1, source_target_pairs={{0,32},{1,33},{32,0},{33,1},{2,34},{3,35},{34,2},{35,3},{4,36},{5,... | collective-permute-start | bytes 835592 | tf_op jit(solution)/shard_map/ppermute | solution.py:340
  48.6 17.5 %collective-permute-start.5 = (bf16[136,1024]{1,0:T(8,128)(2,1)S(1)}, bf16[136,1024]{1,0:T(8,128)(2,1)S(1)}, u32[]{:S(2)}, u32[]{:S(2)}) collective-permute-start(bf16[136,1024]{1,0:T(8,128)(2,1)S(1)} %collective-permute-done.1.refs_3_), channel_id=1, source_target_pairs={{0,32},{1,33},{32,0},{33,1},{2,34},{3,35},{34,2},{35,3},{4,36},{5,... | collective-permute-start | bytes 835592 | tf_op jit(solution)/shard_map/ppermute | solution.py:340
  68.3 4.1 %collective-permute-start.7 = (bf16[1024,256]{1,0:T(8,128)(2,1)S(1)}, bf16[1024,256]{1,0:T(8,128)(2,1)S(1)}, u32[]{:S(2)}, u32[]{:S(2)}) collective-permute-start(bf16[1024,256]{1,0:T(8,128)(2,1)S(1)} %get-tuple-element.40), channel_id=1, source_target_pairs={{0,16},{16,0},{1,17},{17,1},{2,18},{18,2},{3,19},{19,3},{4,20},{20... | collective-permute-start | bytes 1572872 | tf_op jit(solution)/shard_map/ppermute | solution.py:343
  73.4 24.2 %all-to-all-start.1 = ((bf16[8,128,256]{2,1,0:T(8,128)(2,1)}), bf16[8,128,256]{2,1,0:T(8,128)(2,1)S(1)}, u32[]{:S(2)}, u32[]{:S(2)}) async-start(bf16[8,128,256]{2,1,0:T(8,128)(2,1)} %bitcast.4), calls=%async_computation.1 | async-start | bytes 1048576 | tf_op jit(solution)/shard_map/all_to_all | solution.py:346
  77.2 11.7 %collective-permute-start.3 = (bf16[128,512]{1,0:T(8,128)(2,1)S(1)}, bf16[128,512]{1,0:T(8,128)(2,1)S(1)}, u32[]{:S(2)}, u32[]{:S(2)}) collective-permute-start(bf16[128,512]{1,0:T(8,128)(2,1)S(1)} %get-tuple-element.27), channel_id=1, source_target_pairs={{0,32},{1,33},{32,0},{33,1},{2,34},{3,35},{34,2},{35,3},{4,36},{5,... | collective-permute-start | bytes 393224 | tf_op jit(solution)/shard_map/ppermute | solution.py:340
  80.8 16.0 %collective-permute-start.4 = (bf16[128,512]{1,0:T(8,128)(2,1)S(1)}, bf16[128,512]{1,0:T(8,128)(2,1)S(1)}, u32[]{:S(2)}, u32[]{:S(2)}) collective-permute-start(bf16[128,512]{1,0:T(8,128)(2,1)S(1)} %get-tuple-element.28), channel_id=1, source_target_pairs={{0,1},{1,0},{32,33},{33,32},{2,3},{3,2},{34,35},{35,34},{4,5},{5,4... | collective-permute-start | bytes 393224 | tf_op jit(solution)/shard_map/ppermute | solution.py:340
  87.0 9.9 %collective-permute-start.6 = (bf16[128,512]{1,0:T(8,128)(2,1)S(1)}, bf16[128,512]{1,0:T(8,128)(2,1)S(1)}, u32[]{:S(2)}, u32[]{:S(2)}) collective-permute-start(bf16[128,512]{1,0:T(8,128)(2,1)S(1)} %get-tuple-element.38), channel_id=1, source_target_pairs={{0,33},{1,32},{32,1},{33,0},{2,35},{3,34},{34,3},{35,2},{4,37},{5,... | collective-permute-start | bytes 393224 | tf_op jit(solution)/shard_map/ppermute | solution.py:340

commit v11 on v9

--- a/solution.py
+++ b/solution.py
@@ -363,8 +363,10 @@
     grad_key, grad_value = pl.pallas_call(
         finish_kernel, out_shape=[narrow] * 2, compiler_params=pltpu.CompilerParams(vmem_limit_bytes=8 << 20), name="finish"
     )(in_vmem(summed))
-    back = [along_z(g, mask) for g, mask in zip((near_q, far_q, last_q), MASKS[1:])]
-    grad_q = (own_q + back[0].astype(f32) + back[1].astype(f32) + back[2].astype(f32)) * DIM ** (-0.5)
+    back = []
+    for part, mask in ((far_q, 1), (last_q, 3), (near_q, 2)):
+        back.append(along_z(part, mask).astype(f32))
+    grad_q = (own_q + back[2] + back[1] + back[0]) * DIM ** (-0.5)
     return grad_q.astype(bf16), grad_key, grad_value
 
 

time: 84 us -> 84 us (level)
  no operation moved by 1% of the time
where the time goes in v11:
time: 84 us; the launch traced here: 82.8 us
  starting transfers between devices  38.7 us (46%)
  waiting for transfers between devices  19.2 us (23%)
  Pallas kernels  17.5 us (21%)
  local copies, waits for them, and re-layouts  4.23 us (5%)
  other arithmetic  2.46 us (3%)
    ppermute x6, starting transfers between devices, along_z(): lax.ppermute(value, ('zlo', 'zhl'), [(i, i ^ mask) for i in range(NZ)])  23.9 us
    pallas_call x3, Pallas kernels, tile(): pl.pallas_call(body, in_specs=[smem] + [vmem] * len(arrays), out_specs=[v...  14.4 us
    ppermute x6, waiting for transfers between devices, along_z(): lax.ppermute(value, ('zlo', 'zhl'), [(i, i ^ mask) for i in range(NZ)])  11.3 us
    all_to_all x2, starting transfers between devices, over_y(): return lax.all_to_all(value, 'y', 0, 0)  10.9 us
    all_to_all x2, waiting for transfers between devices, over_y(): return lax.all_to_all(value, 'y', 0, 0)  7.82 us
    ppermute x2, starting transfers between devices, other_core(): return lax.ppermute(value, 'core', [(0, 1), (1, 0)])  3.83 us
    unnamed x10, local copies, waits for them, and re-layouts  3.39 us
    pallas_call x1, Pallas kernels, plan(): pl.pallas_call(plan_kernel, in_specs=[pl.BlockSpec(memory_space=pltpu.SME...  2.19 us
  transfers between devices with their start and end apart: 10, of which 3 were waited for; matrix products, arithmetic and copies ran while one was open for 1% of the time, Pallas kernels for 18%

profile of v11, /device:TPU:6, one launch (start us, length us, event | category | flops | bytes accessed | tf_op | source)
XLA Modules:
  0.0 82.8 jit_solution(14848984818423683166)
XLA Ops:
  0.6 0.0 copy-start.4
  0.6 0.8 pad_maximum_fusion
  1.4 0.8 %broadcast_in_dim.2 = bf16[8,128,256]{2,1,0:T(8,128)(2,1)} broadcast(bf16[128,256]{1,0:T(8,128)(2,1)S(1)} %pad_maximum_fusion), dimensions={1,2} | broadcast | bytes 589824 | tf_op jit(solution)/shard_map/broadcast_in_dim | solution.py:337
  2.3 7.1 %all-to-all-start = ((bf16[8,128,256]{2,1,0:T(8,128)(2,1)}), bf16[8,128,256]{2,1,0:T(8,128)(2,1)S(1)}, u32[]{:S(2)}, u32[]{:S(2)}) async-start(bf16[8,128,256]{2,1,0:T(8,128)(2,1)} %broadcast_in_dim.2), calls=%async_computation | async-start | bytes 1048576 | tf_op jit(solution)/shard_map/all_to_all | solution.py:334
  9.4 0.0 copy-start
  9.4 0.9 %copy-done = bf16[128,512]{1,0:T(8,128)(2,1)S(1)} copy-done((bf16[128,512]{1,0:T(8,128)(2,1)S(1)}, bf16[128,512]{1,0:T(8,128)(2,1)}, u32[]{:S(2)}) %copy-start) | copy-done | bytes 131096
  10.3 0.0 copy-start.1
  10.3 0.9 %copy-done.1 = bf16[128,512]{1,0:T(8,128)(2,1)S(1)} copy-done((bf16[128,512]{1,0:T(8,128)(2,1)S(1)}, bf16[128,512]{1,0:T(8,128)(2,1)}, u32[]{:S(2)}) %copy-start.1) | copy-done | bytes 131096
  11.2 0.0 copy-start.2
  11.2 0.9 %copy-done.2 = bf16[128,512]{1,0:T(8,128)(2,1)S(1)} copy-done((bf16[128,512]{1,0:T(8,128)(2,1)S(1)}, bf16[128,512]{1,0:T(8,128)(2,1)}, u32[]{:S(2)}) %copy-start.2) | copy-done | bytes 131096
  12.1 0.0 copy-start.3
  12.1 0.7 copy-done.3
  12.8 0.2 pack.1.refs_1_
  13.0 6.1 %collective-permute-start.1 = (bf16[136,1024]{1,0:T(8,128)(2,1)S(1)}, bf16[136,1024]{1,0:T(8,128)(2,1)S(1)}, u32[]{:S(2)}, u32[]{:S(2)}) collective-permute-start(bf16[136,1024]{1,0:T(8,128)(2,1)S(1)} %pack.1.refs_1_), channel_id=1, source_target_pairs={{0,1},{1,0},{32,33},{33,32},{2,3},{3,2},{34,35},{35,34},{4,5},{5,4... | collective-permute-start | bytes 835592 | tf_op jit(solution)/shard_map/ppermute | solution.py:328
  19.0 7.8 %all-to-all-done = bf16[8,128,256]{2,1,0:T(8,128)(2,1)S(1)} async-done(((bf16[8,128,256]{2,1,0:T(8,128)(2,1)}), bf16[8,128,256]{2,1,0:T(8,128)(2,1)S(1)}, u32[]{:S(2)}, u32[]{:S(2)}) %all-to-all-start) | async-done | bytes 524320 | tf_op jit(solution)/shard_map/all_to_all | solution.py:334
  26.9 1.9 %collective-permute-start.2 = (bf16[1024,256]{1,0:T(8,128)(2,1)S(1)}, bf16[1024,256]{1,0:T(8,128)(2,1)S(1)}, u32[]{:S(2)}, u32[]{:S(2)}) collective-permute-start(bf16[1024,256]{1,0:T(8,128)(2,1)S(1)} %bitcast.5), channel_id=1, source_target_pairs={{0,16},{16,0},{1,17},{17,1},{2,18},{18,2},{3,19},{19,3},{4,20},{20... | collective-permute-start | bytes 1572872 | tf_op jit(solution)/shard_map/ppermute | solution.py:331
  28.8 4.3 %collective-permute-start = (bf16[136,1024]{1,0:T(8,128)(2,1)S(1)}, bf16[136,1024]{1,0:T(8,128)(2,1)S(1)}, u32[]{:S(2)}, u32[]{:S(2)}) collective-permute-start(bf16[136,1024]{1,0:T(8,128)(2,1)S(1)} %pack.1.refs_1_), channel_id=1, source_target_pairs={{0,32},{1,33},{32,0},{33,1},{2,34},{3,35},{34,2},{35,3},{4,36},{5,... | collective-permute-start | bytes 835592 | tf_op jit(solution)/shard_map/ppermute | solution.py:328
  33.1 0.0 collective-permute-done.1.refs_3_
  33.1 1.9 %collective-permute-start.4 = (bf16[136,1024]{1,0:T(8,128)(2,1)S(1)}, bf16[136,1024]{1,0:T(8,128)(2,1)S(1)}, u32[]{:S(2)}, u32[]{:S(2)}) collective-permute-start(bf16[136,1024]{1,0:T(8,128)(2,1)S(1)} %collective-permute-done.1.refs_3_), channel_id=1, source_target_pairs={{0,32},{1,33},{32,0},{33,1},{2,34},{3,35},{34,2},{35,3},{4,36},{5,... | collective-permute-start | bytes 835592 | tf_op jit(solution)/shard_map/ppermute | solution.py:328
  35.0 0.0 copy-done.4
  35.0 2.2 %plan.1 = (s32[4,128]{1,0:T(4,128)S(1)}, s32[16,128]{1,0:T(8,128)S(1)}, s32[8,3,256]{2,1,0:T(4,128)S(1)}) custom-call(s32[3,3]{1,0:T(4,128)S(1)} %copy-done.4, s32[512,1,128]{2,1,0:T(1,128)} %bitcast.8, s32[512,1,128]{2,1,0:T(1,128)} %bitcast.9), custom_call_target="tpu_custom_call" | custom-call | tf_op jit(solution)/shard_map/plan/pallas_call | solution.py:304
  37.2 3.3 %collective-permute-done.refs_2_ = bf16[136,1024]{1,0:T(8,128)(2,1)S(1)} collective-permute-done((bf16[136,1024]{1,0:T(8,128)(2,1)S(1)}, bf16[136,1024]{1,0:T(8,128)(2,1)S(1)}, u32[]{:S(2)}, u32[]{:S(2)}) %collective-permute-start) | collective-permute-done | bytes 278560 | tf_op jit(solution)/shard_map/ppermute | solution.py:328
  40.6 0.0 collective-permute-done.2.refs_5_
  40.6 10.1 %shard_map.112 = (f32[128,512]{1,0:T(8,128)S(1)}, bf16[128,512]{1,0:T(8,128)(2,1)S(1)}, bf16[128,512]{1,0:T(8,128)(2,1)S(1)}, f32[2048,256]{1,0:T(8,128)S(1)}, b...) custom-call(s32[4,128]{1,0:T(4,128)S(1)} %get-tuple-element.23.refs_0_, ...), custom_call_target="tpu_custom_call" | custom-call | tf_op jit(solution)/shard_map/pallas_call | solution.py:228
  50.6 0.0 collective-permute-done.4.refs_1_
  50.6 2.2 %shard_map.113 = (f32[2,128,256]{2,1,0:T(8,128)S(1)}, bf16[1024,256]{1,0:T(8,128)(2,1)S(1)}, bf16[512,128]{1,0:T(8,128)(2,1)S(1)}, bf16[512,128]{1,0:T(8,128)(2,...) custom-call(s32[4,128]{1,0:T(4,128)S(1)} %get-tuple-element.23.refs_0_, ...), custom_call_target="tpu_custom_call" | custom-call | tf_op jit(solution)/shard_map/pallas_call | solution.py:228
  52.8 1.9 %collective-permute-start.7 = (bf16[1024,256]{1,0:T(8,128)(2,1)S(1)}, bf16[1024,256]{1,0:T(8,128)(2,1)S(1)}, u32[]{:S(2)}, u32[]{:S(2)}) collective-permute-start(bf16[1024,256]{1,0:T(8,128)(2,1)S(1)} %get-tuple-element.40), channel_id=1, source_target_pairs={{0,16},{16,0},{1,17},{17,1},{2,18},{18,2},{3,19},{19,3},{4,20},{20... | collective-permute-start | bytes 1572872 | tf_op jit(solution)/shard_map/ppermute | solution.py:331
  54.7 2.2 %shard_map.114 = (bf16[128,512]{1,0:T(8,128)(2,1)S(1)}, f32[1024,256]{1,0:T(8,128)S(1)}) custom-call(s32[4,128]{1,0:T(4,128)S(1)} %get-tuple-element.23.refs_0_, s32[8,3,256]{2,1,0:T(4,128)S(1)} %get-tuple-element.25.refs_7_.refs_2_.refs_1_, bf16[512,128]{1,0:T(8,128)(2,1)S(1)} %get-tuple-element.32.refs_2_, bf16[512,128]{1,0:T(8,128)(2,1)S(1)} %get-tuple-element.33.refs_3_, ...), custom_call_target="tpu_custom_call" | custom-call | tf_op jit(solution)/shard_map/pallas_call | solution.py:228
  56.9 0.0 collective-permute-done.7
  56.9 0.9 %add_convert_fusion = bf16[1024,256]{1,0:T(8,128)(2,1)} fusion(f32[1024,256]{1,0:T(8,128)S(1)} %get-tuple-element.39, bf16[1024,256]{1,0:T(8,128)(2,1)S(1)} %collective-permute-done.7), kind=kLoop, calls=%fused_computation | loop fusion | flops 786432 | bytes 2097152 | tf_op jit(solution)/shard_map/convert_element_type | solution.py:360
  57.9 3.8 %all-to-all-start.1 = ((bf16[8,128,256]{2,1,0:T(8,128)(2,1)}), bf16[8,128,256]{2,1,0:T(8,128)(2,1)S(1)}, u32[]{:S(2)}, u32[]{:S(2)}) async-start(bf16[8,128,256]{2,1,0:T(8,128)(2,1)} %bitcast.4), calls=%async_computation.1 | async-start | bytes 1048576 | tf_op jit(solution)/shard_map/all_to_all | solution.py:334
  61.7 3.6 %collective-permute-start.3 = (bf16[128,512]{1,0:T(8,128)(2,1)S(1)}, bf16[128,512]{1,0:T(8,128)(2,1)S(1)}, u32[]{:S(2)}, u32[]{:S(2)}) collective-permute-start(bf16[128,512]{1,0:T(8,128)(2,1)S(1)} %get-tuple-element.27), channel_id=1, source_target_pairs={{0,32},{1,33},{32,0},{33,1},{2,34},{3,35},{34,2},{35,3},{4,36},{5,... | collective-permute-start | bytes 393224 | tf_op jit(solution)/shard_map/ppermute | solution.py:328
  65.3 6.1 %collective-permute-start.6 = (bf16[128,512]{1,0:T(8,128)(2,1)S(1)}, bf16[128,512]{1,0:T(8,128)(2,1)S(1)}, u32[]{:S(2)}, u32[]{:S(2)}) collective-permute-start(bf16[128,512]{1,0:T(8,128)(2,1)S(1)} %get-tuple-element.38), channel_id=1, source_target_pairs={{0,1},{1,0},{32,33},{33,32},{2,3},{3,2},{34,35},{35,34},{4,5},{5,4... | collective-permute-start | bytes 393224 | tf_op jit(solution)/shard_map/ppermute | solution.py:328
  71.4 1.9 %collective-permute-start.5 = (bf16[128,512]{1,0:T(8,128)(2,1)S(1)}, bf16[128,512]{1,0:T(8,128)(2,1)S(1)}, u32[]{:S(2)}, u32[]{:S(2)}) collective-permute-start(bf16[128,512]{1,0:T(8,128)(2,1)S(1)} %get-tuple-element.37), channel_id=1, source_target_pairs={{0,33},{1,32},{32,1},{33,0},{2,35},{3,34},{34,3},{35,2},{4,37},{5,... | collective-permute-start | bytes 393224 | tf_op jit(solution)/shard_map/ppermute | solution.py:328
  73.4 0.0 collective-permute-done.3
  73.4 8.0 %collective-permute-done.6 = bf16[128,512]{1,0:T(8,128)(2,1)S(1)} collective-permute-done((bf16[128,512]{1,0:T(8,128)(2,1)S(1)}, bf16[128,512]{1,0:T(8,128)(2,1)S(1)}, u32[]{:S(2)}, u32[]{:S(2)}) %collective-permute-start.6) | collective-permute-done | bytes 131104 | tf_op jit(solution)/shard_map/ppermute | solution.py:328
  81.3 0.0 collective-permute-done.5
  81.4 0.7 multiply_convert_fusion
  82.1 0.0 all-to-all-done.1.parts
  82.1 0.7 finish.1
Async XLA Ops:
  0.6 34.4 %copy-start.4 = (s32[3,3]{1,0:T(4,128)S(1)}, s32[3,3]{1,0:T(4,128)}, u32[]{:S(2)}) copy-start(s32[3,3]{1,0:T(4,128)} %table.1) | copy-start | bytes 112
  2.3 24.6 %all-to-all-start = ((bf16[8,128,256]{2,1,0:T(8,128)(2,1)}), bf16[8,128,256]{2,1,0:T(8,128)(2,1)S(1)}, u32[]{:S(2)}, u32[]{:S(2)}) async-start(bf16[8,128,256]{2,1,0:T(8,128)(2,1)} %broadcast_in_dim.2), calls=%async_computation | async-start | bytes 1048576 | tf_op jit(solution)/shard_map/all_to_all | solution.py:334
  9.4 0.9 %copy-start = (bf16[128,512]{1,0:T(8,128)(2,1)S(1)}, bf16[128,512]{1,0:T(8,128)(2,1)}, u32[]{:S(2)}) copy-start(bf16[128,512]{1,0:T(8,128)(2,1)} %q_ref.1) | copy-start | bytes 393220
  10.3 0.9 %copy-start.1 = (bf16[128,512]{1,0:T(8,128)(2,1)S(1)}, bf16[128,512]{1,0:T(8,128)(2,1)}, u32[]{:S(2)}) copy-start(bf16[128,512]{1,0:T(8,128)(2,1)} %d_ref.1) | copy-start | bytes 393220
  11.2 0.9 %copy-start.2 = (bf16[128,512]{1,0:T(8,128)(2,1)S(1)}, bf16[128,512]{1,0:T(8,128)(2,1)}, u32[]{:S(2)}) copy-start(bf16[128,512]{1,0:T(8,128)(2,1)} %o_ref.1) | copy-start | bytes 393220
  12.1 0.7 copy-start.3
  13.0 20.1 %collective-permute-start.1 = (bf16[136,1024]{1,0:T(8,128)(2,1)S(1)}, bf16[136,1024]{1,0:T(8,128)(2,1)S(1)}, u32[]{:S(2)}, u32[]{:S(2)}) collective-permute-start(bf16[136,1024]{1,0:T(8,128)(2,1)S(1)} %pack.1.refs_1_), channel_id=1, source_target_pairs={{0,1},{1,0},{32,33},{33,32},{2,3},{3,2},{34,35},{35,34},{4,5},{5,4... | collective-permute-start | bytes 835592 | tf_op jit(solution)/shard_map/ppermute | solution.py:328
  26.9 13.7 %collective-permute-start.2 = (bf16[1024,256]{1,0:T(8,128)(2,1)S(1)}, bf16[1024,256]{1,0:T(8,128)(2,1)S(1)}, u32[]{:S(2)}, u32[]{:S(2)}) collective-permute-start(bf16[1024,256]{1,0:T(8,128)(2,1)S(1)} %bitcast.5), channel_id=1, source_target_pairs={{0,16},{16,0},{1,17},{17,1},{2,18},{18,2},{3,19},{19,3},{4,20},{20... | collective-permute-start | bytes 1572872 | tf_op jit(solution)/shard_map/ppermute | solution.py:331
  28.8 11.8 %collective-permute-start = (bf16[136,1024]{1,0:T(8,128)(2,1)S(1)}, bf16[136,1024]{1,0:T(8,128)(2,1)S(1)}, u32[]{:S(2)}, u32[]{:S(2)}) collective-permute-start(bf16[136,1024]{1,0:T(8,128)(2,1)S(1)} %pack.1.refs_1_), channel_id=1, source_target_pairs={{0,32},{1,33},{32,0},{33,1},{2,34},{3,35},{34,2},{35,3},{4,36},{5,... | collective-permute-start | bytes 835592 | tf_op jit(solution)/shard_map/ppermute | solution.py:328
  33.1 17.5 %collective-permute-start.4 = (bf16[136,1024]{1,0:T(8,128)(2,1)S(1)}, bf16[136,1024]{1,0:T(8,128)(2,1)S(1)}, u32[]{:S(2)}, u32[]{:S(2)}) collective-permute-start(bf16[136,1024]{1,0:T(8,128)(2,1)S(1)} %collective-permute-done.1.refs_3_), channel_id=1, source_target_pairs={{0,32},{1,33},{32,0},{33,1},{2,34},{3,35},{34,2},{35,3},{4,36},{5,... | collective-permute-start | bytes 835592 | tf_op jit(solution)/shard_map/ppermute | solution.py:328
  52.8 4.1 %collective-permute-start.7 = (bf16[1024,256]{1,0:T(8,128)(2,1)S(1)}, bf16[1024,256]{1,0:T(8,128)(2,1)S(1)}, u32[]{:S(2)}, u32[]{:S(2)}) collective-permute-start(bf16[1024,256]{1,0:T(8,128)(2,1)S(1)} %get-tuple-element.40), channel_id=1, source_target_pairs={{0,16},{16,0},{1,17},{17,1},{2,18},{18,2},{3,19},{19,3},{4,20},{20... | collective-permute-start | bytes 1572872 | tf_op jit(solution)/shard_map/ppermute | solution.py:331
  57.9 24.2 %all-to-all-start.1 = ((bf16[8,128,256]{2,1,0:T(8,128)(2,1)}), bf16[8,128,256]{2,1,0:T(8,128)(2,1)S(1)}, u32[]{:S(2)}, u32[]{:S(2)}) async-start(bf16[8,128,256]{2,1,0:T(8,128)(2,1)} %bitcast.4), calls=%async_computation.1 | async-start | bytes 1048576 | tf_op jit(solution)/shard_map/all_to_all | solution.py:334
  61.7 11.7 %collective-permute-start.3 = (bf16[128,512]{1,0:T(8,128)(2,1)S(1)}, bf16[128,512]{1,0:T(8,128)(2,1)S(1)}, u32[]{:S(2)}, u32[]{:S(2)}) collective-permute-start(bf16[128,512]{1,0:T(8,128)(2,1)S(1)} %get-tuple-element.27), channel_id=1, source_target_pairs={{0,32},{1,33},{32,0},{33,1},{2,34},{3,35},{34,2},{35,3},{4,36},{5,... | collective-permute-start | bytes 393224 | tf_op jit(solution)/shard_map/ppermute | solution.py:328
  65.3 16.0 %collective-permute-start.6 = (bf16[128,512]{1,0:T(8,128)(2,1)S(1)}, bf16[128,512]{1,0:T(8,128)(2,1)S(1)}, u32[]{:S(2)}, u32[]{:S(2)}) collective-permute-start(bf16[128,512]{1,0:T(8,128)(2,1)S(1)} %get-tuple-element.38), channel_id=1, source_target_pairs={{0,1},{1,0},{32,33},{33,32},{2,3},{3,2},{34,35},{35,34},{4,5},{5,4... | collective-permute-start | bytes 393224 | tf_op jit(solution)/shard_map/ppermute | solution.py:328
  71.4 9.9 %collective-permute-start.5 = (bf16[128,512]{1,0:T(8,128)(2,1)S(1)}, bf16[128,512]{1,0:T(8,128)(2,1)S(1)}, u32[]{:S(2)}, u32[]{:S(2)}) collective-permute-start(bf16[128,512]{1,0:T(8,128)(2,1)S(1)} %get-tuple-element.37), channel_id=1, source_target_pairs={{0,33},{1,32},{32,1},{33,0},{2,35},{3,34},{34,3},{35,2},{4,37},{5,... | collective-permute-start | bytes 393224 | tf_op jit(solution)/shard_map/ppermute | solution.py:328
